TPU v7x, 32 devices: a whole 2x2x4 slice. The times are simulated.
32 devices in a mesh: group: 2 (over x), dp: 8 (over z, y), section: 2 (over core).
Axes of the slice: x: 2, y: 2, z: 4, core: 2. Of those that a mesh axis runs over, the one named last changes fastest.
Arguments:
- queries: bfloat16 [6144, 2048], P(('group', 'dp'), 'section'), parts along dimension 0, may hold values from -3 to 3
- grad_out: bfloat16 [6144, 2048], P(('group', 'dp'), 'section'), parts along dimension 0, may hold values from -16 to 16
- log_sums: float32 [16, 6144], P('section', ('group', 'dp')), parts along dimension 1, may hold values from 5 to 7
- neighbours: bfloat16 [96, 256, 896], P(('group', 'dp')), parts along dimension 0, may hold values from -3 to 3
- key_weight: bfloat16 [896, 2048], P(None, 'section'), may hold values from -0.1875 to 0.1875
- value_weight: bfloat16 [896, 2048], P(None, 'section'), may hold values from -0.1875 to 0.1875
- neighbour_ids: int32 [96, 2], P(('group', 'dp')), parts along dimension 0, may hold values from 0 to 31, as said below
- block_slot: int32 [64], P('group'), parts along dimension 0, may hold values from 0 to 31, as said below
- enc_input: bfloat16 [8192, 896], P(('group', 'dp')), parts along dimension 0, may hold values from -4 to 4
Outputs:
- query_grad: bfloat16 [6144, 2048], P(('group', 'dp'), 'section'), parts along dimension 0
- weight_grad: float32 [1792, 896], P(('group', 'dp', 'section')), parts along dimension 0
There are 2 independent parts, one for each index of `group`. A program takes and returns all parts, laid end to end along the dimension named above; an argument that names none is the same for every part. Nothing has to cross between parts.
Inputs may be any that keep to these rules, and one draw needn't show every extreme that they name: `neighbour_ids`: the two entries of a span differ. With owner(n) = block_slot[n] // 4, among the 12 entries of the spans on one index of dp at most 3 have the same owner, and in every draw one owner gets exactly 3 from the spans of every index of dp. A permutation: block n is stored at block position block_slot[n] of enc_input.
All inputs are finite; a program needn't handle non-finite values.
Results may differ from a plain program's by a relative error of at most 0.006.
The roundings to bfloat16 on the way count: a program that leaves them out, or rounds other values in their place, can miss the bound.
Values may be sent and summed in bfloat16 or wider, within the bound.
No kernel may reach another device: no remote copies, remote signals or barrier semaphores. Data moves between devices by JAX's collectives and lax.ppermute only.
A program may use at most 128 MiB of HBM per device.

v0:
```python
import jax
import jax.numpy as jnp
from jax import lax
from jax.sharding import PartitionSpec as P

HD = 128
DE = 896
CL = 64
R = 128


def per_device(
    queries,
    grad_out,
    log_sums,
    neighbours,
    key_weight,
    value_weight,
    neighbour_ids,
    block_slot,
    enc_input,
):
    spans = neighbour_ids.shape[0]
    columns = queries.shape[1]
    head_count = columns // HD
    inv_root = HD ** (-0.5)
    query_heads = queries.reshape(spans, CL, head_count, HD)
    grad_heads = grad_out.reshape(spans, CL, head_count, HD)
    flat_rows = neighbours.reshape(spans * 2 * R, DE)
    key_rows = jnp.dot(flat_rows, key_weight, preferred_element_type=jnp.float32).astype(
        jnp.bfloat16
    )
    value_rows = jnp.dot(flat_rows, value_weight, preferred_element_type=jnp.float32).astype(
        jnp.bfloat16
    )
    key_heads = key_rows.reshape(spans, 2 * R, head_count, HD)
    value_heads = value_rows.reshape(spans, 2 * R, head_count, HD)
    scores = (
        jnp.einsum("cqhe,ckhe->chqk", query_heads, key_heads, preferred_element_type=jnp.float32)
        * inv_root
    )
    log_table = log_sums.reshape(head_count, spans, CL).transpose(1, 0, 2)[..., None]
    prob_rows = jnp.exp(scores - log_table)
    prob_grad = jnp.einsum(
        "cqhe,ckhe->chqk", grad_heads, value_heads, preferred_element_type=jnp.float32
    )
    row_delta = jnp.sum(prob_rows * prob_grad, axis=3, keepdims=True)
    score_grad = prob_rows * (prob_grad - row_delta)
    prob_bf = prob_rows.astype(jnp.bfloat16)
    score_bf = score_grad.astype(jnp.bfloat16)
    query_grad = (
        jnp.einsum("chqk,ckhe->cqhe", score_bf, key_heads, preferred_element_type=jnp.float32)
        * inv_root
    ).astype(jnp.bfloat16)
    query_grad = query_grad.reshape(spans * CL, columns)
    key_grad = (
        jnp.einsum("chqk,cqhe->ckhe", score_bf, query_heads, preferred_element_type=jnp.float32)
        * inv_root
    ).astype(jnp.bfloat16)
    value_grad = jnp.einsum(
        "chqk,cqhe->ckhe", prob_bf, grad_heads, preferred_element_type=jnp.float32
    ).astype(jnp.bfloat16)
    key_grad = key_grad.reshape(spans * 2 * R, columns)
    value_grad = value_grad.reshape(spans * 2 * R, columns)
    contract = (((1,), (1,)), ((), ()))
    partial_grad = lax.dot_general(
        key_grad, key_weight, contract, preferred_element_type=jnp.float32
    )
    partial_grad = partial_grad + lax.dot_general(
        value_grad, value_weight, contract, preferred_element_type=jnp.float32
    )
    partial_grad = partial_grad.astype(jnp.bfloat16)
    ref_count = spans * 2
    block_total = block_slot.shape[0]
    owned_blocks = enc_input.shape[0] // R
    peer_count = lax.axis_size("dp")
    capacity = max(1, 4 * spans // peer_count)
    slot_total = peer_count * capacity
    flat_ids = neighbour_ids.reshape(ref_count)
    match_table = flat_ids[:, None] == jnp.arange(block_total, dtype=jnp.int32)[None, :]
    storage = jnp.sum(jnp.where(match_table, block_slot[None, :], 0), axis=1)
    owners = storage // owned_blocks
    local_idx = storage % owned_blocks
    owner_hits = (owners[:, None] == jnp.arange(peer_count, dtype=jnp.int32)[None, :]).astype(
        jnp.int32
    )
    slot_rank = jnp.sum(jnp.cumsum(owner_hits, axis=0) * owner_hits, axis=1) - 1
    slot_index = owners * capacity + slot_rank
    selector = slot_index[None, :] == jnp.arange(slot_total, dtype=jnp.int32)[:, None]
    outgoing = jnp.dot(
        selector.astype(jnp.bfloat16),
        partial_grad.reshape(ref_count, R * DE),
        preferred_element_type=jnp.float32,
    )
    outgoing = outgoing.astype(jnp.bfloat16).reshape(peer_count, capacity, 2, R // 2, DE)
    slot_ids = jnp.sum(jnp.where(selector, local_idx[None, :] + 1, 0), axis=1) - 1
    slot_ids = slot_ids.reshape(peer_count, capacity)
    incoming, got_ids = (
        lax.all_to_all(outgoing, "dp", split_axis=0, concat_axis=0, tiled=True),
        lax.all_to_all(slot_ids, "dp", split_axis=0, concat_axis=0, tiled=True),
    )
    halves = lax.all_to_all(incoming, "section", split_axis=2, concat_axis=2, tiled=True)
    summed = (halves[:, :, 0].astype(jnp.float32) + halves[:, :, 1].astype(jnp.float32)).astype(
        jnp.bfloat16
    )
    member = (
        got_ids.reshape(slot_total)[None, :] == jnp.arange(owned_blocks, dtype=jnp.int32)[:, None]
    ).astype(jnp.bfloat16)
    enc_grad = jnp.dot(
        member, summed.reshape(slot_total, R // 2 * DE), preferred_element_type=jnp.float32
    )
    enc_grad = enc_grad.astype(jnp.bfloat16).reshape(owned_blocks * (R // 2), DE)
    section_idx = lax.axis_index("section")
    input_half = lax.dynamic_index_in_dim(
        enc_input.reshape(owned_blocks, 2, R // 2, DE), section_idx, 1, keepdims=False
    )
    input_half = input_half.reshape(owned_blocks * (R // 2), DE)
    weight_grad = lax.psum_scatter(
        lax.dot_general(
            input_half, enc_grad, (((0,), (0,)), ((), ())), preferred_element_type=jnp.float32
        ),
        ("dp", "section"),
        scatter_dimension=0,
        tiled=True,
    )
    weight_grad = weight_grad * (block_total * R) ** (-0.5)
    return (query_grad, weight_grad)


def solution(mesh):
    return jax.shard_map(
        per_device,
        mesh=mesh,
        in_specs=(
            P(("group", "dp"), "section"),
            P(("group", "dp"), "section"),
            P("section", ("group", "dp")),
            P(("group", "dp"), None, None),
            P(None, "section"),
            P(None, "section"),
            P(("group", "dp"), None),
            P("group"),
            P(("group", "dp"), None),
        ),
        out_specs=(P(("group", "dp"), "section"), P(("group", "dp", "section"), None)),
        check_vma=False,
    )
```

profile of v0, /device:TPU:0, one launch (start us, length us, event | category | flops | bytes accessed | tf_op | source)
XLA Modules:
  0.0 290.1 jit_solution(5300900303963711736)
XLA Ops:
  7.2 0.0 copy-start
  7.2 0.9 copy.68
  8.1 0.1 eq.58
  8.2 0.8 select_reduce_fusion.1
  9.0 0.2 reduce_window_sum.11
  9.2 0.5 copy-done.7
  9.7 0.1 select_reduce_fusion
  9.8 0.7 sub.36
  10.5 7.3 %all-to-all-start = ((s32[8,1,3]{2,1,0:T(1,128)}), s32[8,1,3]{2,1,0:T(1,128)S(1)}, u32[]{:S(2)}, u32[]{:S(2)}) async-start(s32[8,1,3]{2,1,0:T(1,128)} %bitcast.7), calls=%async_computation | async-start | bytes 8192 | tf_op jit(solution)/shard_map/all_to_all | solution.py:100
  17.8 0.0 copy-done
  17.8 5.1 %fusion.15 = bf16[192,8,8,128]{3,1,2,0:T(8,128)(2,1)S(1)} fusion(bf16[1536,896]{1,0:T(8,128)(2,1)S(1)} %bitcast.74, bf16[896,1024]{1,0:T(8,128)(2,1)} %param.13), kind=kOutput, calls=%fused_computation.27 | convolution fusion | flops 2820145152 | bytes 7733248 | tf_op jit(solution)/shard_map/dot_general | solution.py:30
  22.9 0.0 copy-start.4
  22.9 0.0 copy-start.6
  23.0 2.6 copy.76
  25.5 0.0 copy-done.4
  25.5 0.2 copy.77
  25.7 0.0 copy-done.6
  25.7 0.7 reshape.133
  26.4 0.8 copy.63
  27.2 1.3 copy.79
  28.5 5.1 %fusion.16 = bf16[192,8,8,128]{3,1,2,0:T(8,128)(2,1)S(1)} fusion(bf16[1536,896]{1,0:T(8,128)(2,1)S(1)} %bitcast.75, bf16[896,1024]{1,0:T(8,128)(2,1)} %param.14), kind=kOutput, calls=%fused_computation.28 | convolution fusion | flops 2820145152 | bytes 7733248 | tf_op jit(solution)/shard_map/dot_general | solution.py:33
  33.6 0.0 copy-start.2
  33.6 0.8 copy.78
  34.5 1.0 copy-done.2
  35.5 1.2 fusion.11
  36.7 2.1 convert_bitcast_fusion
  38.8 1.9 fusion.6
  40.8 1.2 fusion.8
  42.0 0.0 copy-start.3
  42.0 1.1 copy-done.3
  43.1 1.2 fusion
  44.3 0.0 copy-start.9
  44.3 2.0 copy.71
  46.4 3.5 %fusion.3 = f32[1536,896]{1,0:T(8,128)S(1)} fusion(bf16[896,1024]{1,0:T(8,128)(2,1)S(1)} %copy-done.9, bf16[192,8,8,128]{3,2,1,0:T(8,128)(2,1)S(1)} %bitcast.88), kind=kOutput, calls=%fused_computation.10 | convolution fusion | flops 2818572288 | bytes 10485760 | tf_op jit(solution)/shard_map/dot_general | solution.py:66
  49.9 0.0 copy-start.10
  49.9 2.0 copy.73
  52.0 4.0 %add_convert_fusion.1 = bf16[1536,896]{1,0:T(8,128)(2,1)S(1)} fusion(f32[1536,896]{1,0:T(8,128)S(1)} %fusion.3, bf16[896,1024]{1,0:T(8,128)(2,1)S(1)} %copy-done.10, bf16[192,8,8,128]{3,2,1,0:T(8,128)(2,1)S(1)} %bitcast.87), kind=kOutput, calls=%fused_computation.4 | convolution fusion | flops 2821324800 | bytes 13238272 | tf_op jit(solution)/shard_map/dot_general | solution.py:69
  56.0 0.0 copy-start.8
  56.0 3.6 %reshape.141 = bf16[12,114688]{1,0:T(8,128)(2,1)} reshape(bf16[1536,896]{1,0:T(8,128)(2,1)S(1)} %add_convert_fusion.1) | data formatting | bytes 5505024 | tf_op jit(solution)/shard_map/reshape | solution.py:92
  59.6 0.0 copy-done.8
  59.6 3.7 %convolution_convert_fusion = bf16[24,114688]{1,0:T(8,128)(2,1)S(1)} fusion(bf16[12,114688]{1,0:T(8,128)(2,1)} %reshape.141, s32[12]{0:T(128)S(1)} %copy-done.8), kind=kOutput, calls=%fused_computation | convolution fusion | flops 68813088 | bytes 8257584 | tf_op jit(solution)/shard_map/dot_general | solution.py:90
  63.4 1.0 copy.83
  64.4 3.1 %copy.74 = bf16[8,3,2,64,896]{4,3,1,2,0:T(8,128)(2,1)} copy(bf16[8,3,2,64,896]{4,3,2,1,0:T(8,128)(2,1)S(1)} %bitcast.77) | data formatting | bytes 11010048 | tf_op jit(solution)/shard_map/reshape | solution.py:95
  67.4 0.0 all-to-all-done
  67.4 6.1 %all-to-all-start.1 = ((bf16[8,3,2,64,896]{4,3,1,2,0:T(8,128)(2,1)}), bf16[8,3,2,64,896]{4,3,1,2,0:T(8,128)(2,1)}, u32[]{:S(2)}, u32[]{:S(2)}) async-start(bf16[8,3,2,64,896]{4,3,1,2,0:T(8,128)(2,1)} %copy.74), calls=%async_computation.1 | async-start | bytes 11010048 | tf_op jit(solution)/shard_map/all_to_all | solution.py:99
  73.6 0.0 reduce-scatter.4.cloned.1.call-start
  73.7 0.5 broadcast.153
  74.2 0.7 reduce.3
  74.8 0.1 eq.68
  74.9 119.4 %all-to-all-done.1 = bf16[8,3,2,64,896]{4,3,1,2,0:T(8,128)(2,1)} async-done(((bf16[8,3,2,64,896]{4,3,1,2,0:T(8,128)(2,1)}), bf16[8,3,2,64,896]{4,3,1,2,0:T(8,128)(2,1)}, u32[]{:S(2)}, u32[]{:S(2)}) %all-to-all-start.1) | async-done | bytes 5505056 | tf_op jit(solution)/shard_map/all_to_all | solution.py:99
  194.4 3.1 %copy.75 = bf16[8,3,2,64,896]{4,3,1,0,2:T(8,128)(2,1)S(1)} copy(bf16[8,3,2,64,896]{4,3,1,2,0:T(8,128)(2,1)} %all-to-all-done.1) | data formatting | bytes 11010048 | tf_op jit(solution)/shard_map/all_to_all | solution.py:99
  197.5 8.2 %all_to_all.16 = bf16[8,3,2,64,896]{4,3,1,0,2:T(8,128)(2,1)S(1)} all-to-all(bf16[8,3,2,64,896]{4,3,1,0,2:T(8,128)(2,1)S(1)} %copy.75), channel_id=1, replica_groups=mesh['group'=2,'dp'=8,'section'=2] {'section'}, dimensions={2} | all-to-all | bytes 11010048 | tf_op jit(solution)/shard_map/all_to_all | solution.py:102
  205.7 1.0 add_convert_fusion
  206.6 1.6 copy.84
  208.2 1.5 convolution_convert_fusion.1
  209.6 1.3 reshape.143
  210.9 2.3 fusion.33
  213.3 0.0 reduce-scatter.4.cloned.1.call-update
  213.3 0.0 copy-start.1
  213.3 3.1 %fusion.21 = bf16[6,64,8,128]{3,1,2,0:T(8,128)(2,1)S(1)} fusion(bf16[6,8,64,256]{3,2,1,0:T(8,128)(2,1)} %copy-done.3, bf16[6,256,8,128]{3,2,1,0:T(8,128)(2,1)} %bitcast.78), kind=kOutput, calls=%fused_computation.32 | convolution fusion | flops 202113024 | bytes 5505024 | tf_op jit(solution)/shard_map/chqk,ckhe->cqhe/dot_general | solution.py:52
  216.5 0.5 copy.67
  217.0 1.1 copy.116
  218.1 63.6 %reduce-scatter.4.cloned.1.call-done = f32[56,896]{1,0:T(8,128)} async-done(((f32[896,896]{1,0:T(8,128)}), f32[56,896]{1,0:T(8,128)}) %reduce-scatter.4.cloned.1.call-update) | async-done | bytes 200720
  281.7 1.6 broadcast_multiply_fusion
  (12 shorter events, 0.1 us)
Async XLA Ops:
  7.2 10.6 %copy-start = (bf16[6,256,896]{2,1,0:T(8,128)(2,1)S(1)}, bf16[6,256,896]{2,1,0:T(8,128)(2,1)}, u32[]{:S(2)}) copy-start(bf16[6,256,896]{2,1,0:T(8,128)(2,1)} %param.12) | copy-start | bytes 8257540
  9.2 0.5 copy-start.7
  10.5 56.9 %all-to-all-start = ((s32[8,1,3]{2,1,0:T(1,128)}), s32[8,1,3]{2,1,0:T(1,128)S(1)}, u32[]{:S(2)}, u32[]{:S(2)}) async-start(s32[8,1,3]{2,1,0:T(1,128)} %bitcast.7), calls=%async_computation | async-start | bytes 8192 | tf_op jit(solution)/shard_map/all_to_all | solution.py:100
  22.9 2.6 copy-start.4
  22.9 2.8 copy-start.6
  33.6 1.9 copy-start.2
  42.0 1.1 copy-start.3
  44.3 2.1 copy-start.9
  49.9 2.1 copy-start.10
  56.0 3.7 %copy-start.8 = (s32[12]{0:T(128)S(1)}, s32[12]{0:T(128)}, u32[]{:S(2)}) copy-start(s32[12]{0:T(128)} %copy-done.7) | copy-start | bytes 148
  67.4 6.2 %copy-start.5 = (bf16[512,896]{1,0:T(8,128)(2,1)S(1)}, bf16[512,896]{1,0:T(8,128)(2,1)}, u32[]{:S(2)}) copy-start(bf16[512,896]{1,0:T(8,128)(2,1)} %param.17) | copy-start | bytes 2752516
  67.4 126.9 %all-to-all-start.1 = ((bf16[8,3,2,64,896]{4,3,1,2,0:T(8,128)(2,1)}), bf16[8,3,2,64,896]{4,3,1,2,0:T(8,128)(2,1)}, u32[]{:S(2)}, u32[]{:S(2)}) async-start(bf16[8,3,2,64,896]{4,3,1,2,0:T(8,128)(2,1)} %copy.74), calls=%async_computation.1 | async-start | bytes 11010048 | tf_op jit(solution)/shard_map/all_to_all | solution.py:99
  73.6 208.1 %reduce-scatter.4.cloned.1.call-start = ((), (), s32[]{:S(2)}) async-start(), calls=%async_computation.4 | async-start | bytes 3411968
  213.3 70.0 %copy-start.1 = (bf16[6,256,896]{2,1,0:T(8,128)(2,1)S(1)}, bf16[6,256,896]{2,1,0:T(8,128)(2,1)}, u32[]{:S(2)}) copy-start(bf16[6,256,896]{2,1,0:T(8,128)(2,1)} %param.12) | copy-start | bytes 8257540
Sparse Core Ops, SparseCore 0:
  213.4 68.1 reduce-scatter.3
where the time goes:
time: 291 us; the launch traced here: 290 us
  waiting for transfers between devices  183 us (63%)
  matrix products  34.8 us (12%)
  local copies, waits for them, and re-layouts  30.7 us (11%)
  between operations  14.3 us (5%)
  starting transfers between devices  13.4 us (5%)
  blocking collectives  8.16 us (3%)
  other arithmetic  5.59 us (2%)
    all_to_all x1, waiting for transfers between devices, per_device(): lax.all_to_all(outgoing, 'dp', split_axis=0, concat_axis=0, tiled=True)  119 us
    unnamed x2, waiting for transfers between devices  63.6 us
    unnamed x30, local copies, waits for them, and re-layouts  12.2 us
    all_to_all x1, blocking collectives, per_device(): lax.all_to_all(incoming, 'section', split_axis=2, concat_axis=2, tiled=True)  8.16 us
    all_to_all x1, starting transfers between devices, per_device(): lax.all_to_all(slot_ids, 'dp', split_axis=0, concat_axis=0, tiled=True)  7.28 us
    all_to_all x1, starting transfers between devices, per_device(): lax.all_to_all(outgoing, 'dp', split_axis=0, concat_axis=0, tiled=True)  6.11 us
  transfers between devices with their start and end apart: 3, of which 2 were waited for; matrix products, arithmetic and copies ran while one was open for 18% of the time, Pallas kernels for 0%

commit v1 on v0

v1 whole, which is shorter than its diff:
```python
import functools

import jax
import jax.numpy as jnp
from jax import lax
from jax.experimental import pallas as pl
from jax.experimental.pallas import tpu as pltpu
from jax.sharding import PartitionSpec as P

HD = 128
DE = 896
CL = 64
R = 128
HR = R // 2
STEP = 2
CHUNKS = (1, 2)
F32 = jnp.float32
BF16 = jnp.bfloat16
NT = (((1,), (1,)), ((), ()))
TN = (((0,), (0,)), ((), ()))


def _dot(a, b, dims=(((1,), (0,)), ((), ()))):
    return lax.dot_general(a, b, dims, preferred_element_type=F32)


def _span_kernel(sec_ref, q_ref, g_ref, l_ref, n_ref, wk_ref, wv_ref, *rest):
    dq_ref, mine_ref, send_ref = rest[-3:]
    sec = sec_ref[0]
    near = pl.multiple_of(sec * HR, HR)
    far = pl.multiple_of((1 - sec) * HR, HR)
    inv_root = HD ** (-0.5)
    pieces = []
    for a in range(STEP):
        for base in (near, far):
            for k in range(2):
                pieces.append(n_ref[a, pl.ds(base + k * R, HR), :])
    rows = jnp.concatenate(pieces, axis=0)
    keys = _dot(rows, wk_ref[...]).astype(BF16)
    values = _dot(rows, wv_ref[...]).astype(BF16)
    pairs = q_ref.shape[1] // (2 * HD)
    left = lax.broadcasted_iota(jnp.int32, (CL, 2 * HD), 1) < HD
    low = lax.broadcasted_iota(jnp.int32, (1, 2 * CL), 1) < CL
    key_parts, value_parts = [], []
    for a in range(STEP):
        key_cols, value_cols = [], []
        for p in range(pairs):
            cols = slice(2 * HD * p, 2 * HD * (p + 1))
            ks = keys[2 * R * a : 2 * R * (a + 1), cols]
            vs = values[2 * R * a : 2 * R * (a + 1), cols]
            q = q_ref[CL * a : CL * (a + 1), cols]
            g = g_ref[CL * a : CL * (a + 1), cols]
            zero = jnp.zeros_like(q)
            qd = jnp.concatenate([jnp.where(left, q, zero), jnp.where(left, zero, q)], axis=0)
            gd = jnp.concatenate([jnp.where(left, g, zero), jnp.where(left, zero, g)], axis=0)
            first = l_ref[2 * p : 2 * p + 1, :]
            second = l_ref[2 * p + 1 : 2 * p + 2, :]
            if a == 0:
                logs = jnp.where(low, first, pltpu.roll(second, CL, 1))
            else:
                logs = jnp.where(low, pltpu.roll(first, CL, 1), second)
            scores = _dot(ks, qd, NT) * inv_root
            prob = jnp.exp(scores - logs)
            prob_grad = _dot(vs, gd, NT)
            delta = jnp.sum(prob * prob_grad, axis=0, keepdims=True)
            score_bf = (prob * (prob_grad - delta)).astype(BF16)
            prob_bf = prob.astype(BF16)
            key_cols.append((_dot(score_bf, qd) * inv_root).astype(BF16))
            value_cols.append(_dot(prob_bf, gd).astype(BF16))
            dq = (_dot(score_bf, ks, TN) * inv_root).astype(BF16)
            dq_ref[CL * a : CL * (a + 1), 2 * HD * p : 2 * HD * p + HD] = dq[:CL, :HD]
            dq_ref[CL * a : CL * (a + 1), 2 * HD * p + HD : 2 * HD * (p + 1)] = dq[CL:, HD:]
        key_parts.append(jnp.concatenate(key_cols, axis=1))
        value_parts.append(jnp.concatenate(value_cols, axis=1))
    key_grad = jnp.concatenate(key_parts, axis=0)
    value_grad = jnp.concatenate(value_parts, axis=0)
    half = (_dot(wk_ref[...], key_grad, NT) + _dot(wv_ref[...], value_grad, NT)).astype(BF16)
    for a in range(STEP):
        mine_ref[:, R * a : R * (a + 1)] = half[:, 2 * R * a : 2 * R * a + R]
        send_ref[:, R * a : R * (a + 1)] = half[:, 2 * R * a + R : 2 * R * (a + 1)]


def _span_call(first, steps, section, queries, grad_out, log_sums, neighbours, kw, vw, held):
    tokens, columns = queries.shape
    heads = log_sums.shape[0]
    whole = lambda i, s: (0, 0)
    rows = lambda i, s: (first + i, 0)
    in_specs = [
        pl.BlockSpec((STEP * CL, columns), rows),
        pl.BlockSpec((STEP * CL, columns), rows),
        pl.BlockSpec((heads, STEP * CL), lambda i, s: (0, first + i)),
        pl.BlockSpec((STEP, 2 * R, DE), lambda i, s: (first + i, 0, 0)),
        pl.BlockSpec((DE, columns), whole),
        pl.BlockSpec((DE, columns), whole),
    ]
    args = [queries, grad_out, log_sums, neighbours, kw, vw]
    aliases = {}
    if held is not None:
        in_specs.append(pl.BlockSpec(memory_space=pl.ANY))
        args.append(held)
        aliases = {len(args): 0}
    half_spec = pl.BlockSpec((DE, STEP * R), lambda i, s: (0, i))
    half_shape = jax.ShapeDtypeStruct((DE, steps * STEP * R), BF16)
    spans = steps * STEP
    return pl.pallas_call(
        _span_kernel,
        grid_spec=pltpu.PrefetchScalarGridSpec(
            num_scalar_prefetch=1,
            grid=(steps,),
            in_specs=in_specs,
            out_specs=[pl.BlockSpec((STEP * CL, columns), rows), half_spec, half_spec],
        ),
        out_shape=[jax.ShapeDtypeStruct((tokens, columns), BF16), half_shape, half_shape],
        input_output_aliases=aliases,
        compiler_params=pltpu.CompilerParams(vmem_limit_bytes=48 << 20),
        cost_estimate=pl.CostEstimate(
            flops=spans * 2 * R * columns * (8 * DE + 10 * CL),
            transcendentals=spans * 2 * R * CL * heads,
            bytes_accessed=4 * DE * columns + spans * 1000000,
        ),
    )(section, *args)


def _weight_kernel(order, spans, chunk_spans, ids_ref, *refs):
    got_refs = refs[: len(chunk_spans)]
    x_ref, out_ref, acc_ref, enc_ref = refs[len(chunk_spans) :]
    peers = got_refs[0].shape[0]
    blocks = acc_ref.shape[0]
    cols = acc_ref.shape[1]
    owned = blocks // peers
    low = lax.broadcasted_iota(jnp.int32, (cols, R), 1) < HR
    acc_ref[...] = jnp.zeros_like(acc_ref)

    def add_peer(src, carry):
        at = 0
        for got_ref, count in zip(got_refs, chunk_spans):
            for c in range(count):
                tile = got_ref[src, :, R * c : R * (c + 1)].astype(F32)
                base = src * (2 * spans) + 2 * (at + c)
                first = ids_ref[base]
                second = ids_ref[base + 1]
                acc_ref[first] += jnp.where(low, tile, 0.0)
                acc_ref[second] += jnp.where(low, 0.0, tile)
            at += count
        return carry

    lax.fori_loop(0, peers, add_peer, 0)
    for b in range(0, blocks, 2):
        even = acc_ref[b]
        odd = acc_ref[b + 1]
        even = even + pltpu.roll(even, HR, 1)
        odd = odd + pltpu.roll(odd, HR, 1)
        enc_ref[:, HR * b : HR * (b + 2)] = jnp.where(low, even, odd).astype(BF16)
    total = None
    for pos, owner in enumerate(order):
        lo = owner * owned * HR
        part = _dot(enc_ref[:, lo : lo + owned * HR], x_ref[pos, : owned * HR, :])
        total = part if total is None else total + part
    scale = (blocks * R) ** (-0.5)
    out_ref[...] = (total * scale).T


def _weight_call(order, spans, chunk_spans, ids, gots, x_all, blocks):
    cols = gots[0].shape[1]
    vmem = pl.BlockSpec(memory_space=pltpu.VMEM)
    return pl.pallas_call(
        functools.partial(_weight_kernel, order, spans, chunk_spans),
        in_specs=[pl.BlockSpec(memory_space=pltpu.SMEM)] + [vmem] * (len(gots) + 1),
        out_specs=vmem,
        out_shape=jax.ShapeDtypeStruct((DE, cols), F32),
        scratch_shapes=[
            pltpu.VMEM((blocks, cols, R), F32),
            pltpu.VMEM((cols, blocks * HR), BF16),
        ],
        compiler_params=pltpu.CompilerParams(vmem_limit_bytes=56 << 20),
        cost_estimate=pl.CostEstimate(
            flops=2 * cols * blocks * HR * DE, transcendentals=0, bytes_accessed=6000000
        ),
    )(ids, *gots, x_all)


def per_device(
    queries,
    grad_out,
    log_sums,
    neighbours,
    key_weight,
    value_weight,
    neighbour_ids,
    block_slot,
    enc_input,
):
    spans = neighbour_ids.shape[0]
    blocks = block_slot.shape[0]
    owned = enc_input.shape[0] // R
    peers = lax.axis_size("dp")
    section = lax.axis_index("section").astype(jnp.int32)
    order = (0, 2, 4, 6, 7, 5, 3, 1) if peers == 8 else tuple(range(peers))

    flat_ids = neighbour_ids.reshape(2 * spans)
    hit = flat_ids[:, None] == jnp.arange(blocks, dtype=jnp.int32)[None, :]
    storage = jnp.sum(jnp.where(hit, block_slot[None, :], 0), axis=1)
    id_rows = jnp.pad(storage.astype(BF16)[None, :], ((0, 7), (0, DE - 2 * spans)))
    x_half = lax.dynamic_index_in_dim(
        enc_input.reshape(owned, 2, HR, DE), section, 1, keepdims=False
    ).reshape(owned * HR, DE)
    x_all = lax.all_gather(
        jnp.concatenate([x_half, id_rows], axis=0),
        "dp",
        axis=0,
        tiled=False,
        axis_index_groups=[list(order)],
    )

    held = None
    gots = []
    first = 0
    swap = [(0, 1), (1, 0)]
    for steps in CHUNKS:
        held, mine, send = _span_call(
            first,
            steps,
            section[None],
            queries,
            grad_out,
            log_sums,
            neighbours,
            key_weight,
            value_weight,
            held,
        )
        other = lax.ppermute(send, "section", swap)
        ref_grad = (mine.astype(F32) + other.astype(F32)).astype(BF16)
        ref_grad = ref_grad.reshape(peers, DE // peers, steps * STEP * R)
        gots.append(lax.all_to_all(ref_grad, "dp", 0, 0, tiled=True))
        first += steps

    id_table = x_all[:, owned * HR, : 2 * spans].astype(jnp.int32)
    inverse = [order.index(d) for d in range(peers)]
    ids = jnp.concatenate([id_table[i] for i in inverse], axis=0)
    chunk_spans = tuple(n * STEP for n in CHUNKS)
    weight = _weight_call(order, spans, chunk_spans, ids, gots, x_all, blocks)
    rows = DE // (2 * peers)
    tiles = lax.all_to_all(
        weight.reshape(2 * peers, rows, DE // peers), ("dp", "section"), 0, 0, tiled=True
    )
    tiles = tiles.reshape(peers, 2, rows, DE // peers)
    weight_grad = jnp.transpose(tiles[:, 0] + tiles[:, 1], (1, 0, 2)).reshape(rows, DE)
    return (held, weight_grad)


def solution(mesh):
    return jax.shard_map(
        per_device,
        mesh=mesh,
        in_specs=(
            P(("group", "dp"), "section"),
            P(("group", "dp"), "section"),
            P("section", ("group", "dp")),
            P(("group", "dp"), None, None),
            P(None, "section"),
            P(None, "section"),
            P(("group", "dp"), None),
            P("group"),
            P(("group", "dp"), None),
        ),
        out_specs=(P(("group", "dp"), "section"), P(("group", "dp", "section"), None)),
        check_vma=False,
    )
```

time: 291 us -> 122 us (0.42)
  waiting for transfers between devices: 183 us -> 37.6 us
  matrix products: 34.8 us -> 0 us
  Pallas kernels: 0 us -> 28.4 us
  local copies, waits for them, and re-layouts: 30.7 us -> 7.19 us
  blocking collectives: 8.16 us -> 16.8 us
    all_to_all x2, waiting for transfers between devices: 119 us -> 37.5 us  [per_device(): gots.append(lax.all_to_all(ref_grad, 'dp', 0, 0, tiled=True))]
    unnamed x2 -> x1, waiting for transfers between devices: 63.6 us -> 0.02 us
    dot_general x12 -> x0, matrix products: 34.8 us -> none  [the longest x1 5.12 us: per_device(): jnp.dot(flat_rows, key_weight, preferred_element_type=jnp.float32)]
    pallas_call x0 -> x3, Pallas kernels: none -> 28.4 us  [the longest x2 23.4 us: _span_call(): pl.pallas_call(_span_kernel, grid_spec=pltpu.PrefetchScalarGridSpec(num_s...]
    all_to_all x1, blocking collectives: 8.16 us -> 16.8 us  [per_device(): lax.all_to_all(weight.reshape(2 * peers, rows, DE // peers), ('dp', 'sect...]
    reshape x4 -> x1, local copies, waits for them, and re-layouts: 8.71 us -> 0.8 us  [per_device(): jnp.transpose(tiles[:, 0] + tiles[:, 1], (1, 0, 2)).reshape(rows, DE)]
    unnamed x30 -> x19, local copies, waits for them, and re-layouts: 12.2 us -> 5.62 us
    convert_element_type x3 -> x0, local copies, waits for them, and re-layouts: 4.59 us -> none  [the longest x1 2.04 us: per_device(): key_grad = (jnp.einsum('chqk,cqhe->ckhe', score_bf, query_heads, preferre...]
  transfers between devices with their start and end apart: 3 -> 5, of which waited for: 2 -> 2; matrix products, arithmetic and copies ran while one was open for 18% -> 4% of each run, Pallas kernels for 0% -> 19%
where the time goes in v1:
time: 122 us; the launch traced here: 121 us
  waiting for transfers between devices  37.6 us (31%)
  Pallas kernels  28.4 us (23%)
  blocking collectives  16.8 us (14%)
  between operations  14.1 us (12%)
  starting transfers between devices  11.6 us (10%)
  local copies, waits for them, and re-layouts  7.19 us (6%)
  other arithmetic  5.72 us (5%)
    all_to_all x2, waiting for transfers between devices, per_device(): gots.append(lax.all_to_all(ref_grad, 'dp', 0, 0, tiled=True))  37.5 us
    pallas_call x2, Pallas kernels, _span_call(): pl.pallas_call(_span_kernel, grid_spec=pltpu.PrefetchScalarGridSpec(num_s...  23.4 us
    all_to_all x1, blocking collectives, per_device(): lax.all_to_all(weight.reshape(2 * peers, rows, DE // peers), ('dp', 'sect...  16.8 us
    all_to_all x2, starting transfers between devices, per_device(): gots.append(lax.all_to_all(ref_grad, 'dp', 0, 0, tiled=True))  10.9 us
    unnamed x19, local copies, waits for them, and re-layouts  5.62 us
    pallas_call x1, Pallas kernels, _weight_call(): pl.pallas_call(functools.partial(_weight_kernel, order, spans, chunk_span...  5.07 us
    convert_element_type x2, other arithmetic, per_device(): ref_grad = (mine.astype(F32) + other.astype(F32)).astype(BF16)  3.25 us
  transfers between devices with their start and end apart: 5, of which 2 were waited for; matrix products, arithmetic and copies ran while one was open for 4% of the time, Pallas kernels for 19%

profile of v1, /device:TPU:0, one launch (start us, length us, event | category | flops | bytes accessed | tf_op | source)
XLA Modules:
  0.0 121.4 jit_solution(12842053682804391327)
XLA Ops:
  7.2 0.0 copy-start
  7.2 0.0 copy-start.1
  7.2 0.0 copy-start.6
  7.2 0.0 all-gather.3.cloned.1.call-start
  7.3 0.9 copy.18
  8.2 0.1 eq.15
  8.2 0.8 select_reduce_fusion
  9.1 0.0 copy-done
  9.2 0.8 fusion.1
  10.0 0.0 all-gather.3.cloned.1.call-update
  10.0 0.0 copy-done.1
  10.0 0.0 copy-done.6
  10.0 0.0 copy-start.3
  10.0 1.5 %copy-done.3 = bf16[896,1024]{1,0:T(8,128)(2,1)S(1)} copy-done((bf16[896,1024]{1,0:T(8,128)(2,1)S(1)}, bf16[896,1024]{1,0:T(8,128)(2,1)}, u32[]{:S(2)}) %copy-start.3) | copy-done | bytes 1835032
  11.5 0.0 copy-start.4
  11.5 1.1 copy-done.4
  12.7 0.0 copy-start.5
  12.7 1.1 copy-done.5
  13.8 0.0 copy-start.2
  13.8 8.0 %shard_map.104 = (bf16[384,1024]{1,0:T(8,128)(2,1)}, bf16[896,256]{1,0:T(8,128)(2,1)S(1)}, bf16[896,256]{1,0:T(8,128)(2,1)S(1)}) custom-call(s32[1]{0:T(128)} %bitcast.sec_ref, bf16[384,1024]{1,0:T(8,128)(2,1)S(1)} %copy-done.4, bf16[384,1024]{1,0:T(8,128)(2,1)S(1)} %copy-done.5, f32[8,384]{1,0:T(8,128)S(1)} %copy-done.6, bf16[6,256,896]{2,1,0:T(8,128)(2,1)} %n_ref.3, ...), custom_call_target="tpu_custom_call" | custom-call | flops 4093640704 | bytes 5670016 | tf_op jit(solution)/shard_map/pallas_call | solution.py:105
  21.8 0.5 collective-permute-start
  22.3 0.0 copy-done.2
  22.3 15.4 %shard_map.105 = (bf16[384,1024]{1,0:T(8,128)(2,1)}, bf16[896,512]{1,0:T(8,128)(2,1)S(1)}, bf16[896,512]{1,0:T(8,128)(2,1)S(1)}) custom-call(s32[1]{0:T(128)} %bitcast.sec_ref, bf16[384,1024]{1,0:T(8,128)(2,1)S(1)} %copy-done.4, bf16[384,1024]{1,0:T(8,128)(2,1)S(1)} %copy-done.5, f32[8,384]{1,0:T(8,128)S(1)} %copy-done.6, ...), custom_call_target="tpu_custom_call", output_to_operand_aliasing={{0}: (7, {})} | custom-call | flops 8187281408 | bytes 7670016 | tf_op jit(solution)/shard_map/pallas_call | solution.py:105
  37.7 0.1 collective-permute-start.1
  37.8 0.0 collective-permute-done
  37.8 0.9 add_convert_fusion.1
  38.7 7.3 %all-to-all-start = ((bf16[8,112,256]{2,1,0:T(8,128)(2,1)}), bf16[8,112,256]{2,1,0:T(8,128)(2,1)S(1)}, u32[]{:S(2)}, u32[]{:S(2)}) async-start(bf16[8,112,256]{2,1,0:T(8,128)(2,1)} %bitcast.36), calls=%async_computation | async-start | bytes 917504 | tf_op jit(solution)/shard_map/all_to_all | solution.py:235
  46.0 0.0 collective-permute-done.1
  46.0 2.4 %add_convert_fusion = bf16[896,512]{1,0:T(8,128)(2,1)} fusion(bf16[896,512]{1,0:T(8,128)(2,1)} %collective-permute-done.1, bf16[896,512]{1,0:T(8,128)(2,1)S(1)} %get-tuple-element.12), kind=kLoop, calls=%fused_computation | loop fusion | flops 1835008 | bytes 2752512 | tf_op jit(solution)/shard_map/convert_element_type | solution.py:233
  48.4 16.3 %all-to-all-done.refs_0_ = bf16[8,112,256]{2,1,0:T(8,128)(2,1)S(1)} async-done(((bf16[8,112,256]{2,1,0:T(8,128)(2,1)}), bf16[8,112,256]{2,1,0:T(8,128)(2,1)S(1)}, u32[]{:S(2)}, u32[]{:S(2)}) %all-to-all-start) | async-done | bytes 458784 | tf_op jit(solution)/shard_map/all_to_all | solution.py:235
  64.7 0.0 copy-start.8
  64.7 3.6 %all-to-all-start.1 = ((bf16[8,112,512]{2,1,0:T(8,128)(2,1)}), bf16[8,112,512]{2,1,0:T(8,128)(2,1)S(1)}, u32[]{:S(2)}, u32[]{:S(2)}) async-start(bf16[8,112,512]{2,1,0:T(8,128)(2,1)} %bitcast.14), calls=%async_computation.1 | async-start | bytes 1835008 | tf_op jit(solution)/shard_map/all_to_all | solution.py:235
  68.3 0.0 all-gather.3.cloned.1.call-done
  68.3 0.7 slice_convert_fusion
  69.1 0.6 concatenate.7.ids_ref
  69.7 21.2 %all-to-all-done.1.refs_1_ = bf16[8,112,512]{2,1,0:T(8,128)(2,1)S(1)} async-done(((bf16[8,112,512]{2,1,0:T(8,128)(2,1)}), bf16[8,112,512]{2,1,0:T(8,128)(2,1)S(1)}, u32[]{:S(2)}, u32[]{:S(2)}) %all-to-all-start.1) | async-done | bytes 917536 | tf_op jit(solution)/shard_map/all_to_all | solution.py:235
  90.9 0.0 copy-done.8
  90.9 0.0 copy-start.7
  90.9 0.9 copy-done.7
  91.8 5.1 %shard_map.106 = f32[896,112]{1,0:T(8,128)} custom-call(s32[96]{0:T(128)} %concatenate.7.ids_ref, bf16[8,112,256]{2,1,0:T(8,128)(2,1)} %copy-done.8, bf16[8,112,512]{2,1,0:T(8,128)(2,1)} %copy-done.7, bf16[8,264,896]{2,1,0:T(8,128)(2,1)} %bitcast.32), custom_call_target="tpu_custom_call" | custom-call | flops 411041792 | bytes 6000000 | tf_op jit(solution)/shard_map/pallas_call | solution.py:166
  96.8 16.8 %all_to_all.15 = f32[16,56,112]{2,1,0:T(8,128)S(1)} all-to-all(f32[16,56,112]{2,1,0:T(8,128)} %bitcast.33), channel_id=1, replica_groups=mesh['group'=2,'dp'=8,'section'=2] {'dp','section'}, dimensions={0} | all-to-all | bytes 802816 | tf_op jit(solution)/shard_map/all_to_all | solution.py:244
  113.6 0.1 fusion.2
  113.7 0.8 reshape.60
  (4 shorter events, 0.1 us)
Async XLA Ops:
  7.2 1.9 %copy-start = (bf16[512,896]{1,0:T(8,128)(2,1)S(1)}, bf16[512,896]{1,0:T(8,128)(2,1)}, u32[]{:S(2)}) copy-start(bf16[512,896]{1,0:T(8,128)(2,1)} %param.17) | copy-start | bytes 2752516
  7.2 2.8 %copy-start.1 = (bf16[896,1024]{1,0:T(8,128)(2,1)S(1)}, bf16[896,1024]{1,0:T(8,128)(2,1)}, u32[]{:S(2)}) copy-start(bf16[896,1024]{1,0:T(8,128)(2,1)} %wk_ref.3) | copy-start | bytes 5505028
  7.2 2.8 %copy-start.6 = (f32[8,384]{1,0:T(8,128)S(1)}, f32[8,384]{1,0:T(8,128)}, u32[]{:S(2)}) copy-start(f32[8,384]{1,0:T(8,128)} %l_ref.3) | copy-start | bytes 36868
  7.2 61.1 %all-gather.3.cloned.1.call-start = ((), (), s32[]{:S(2)}) async-start(), calls=%async_computation.3 | async-start | bytes 4257792 | tf_op jit(solution)/shard_map/all_gather | solution.py:207
  10.0 1.5 %copy-start.3 = (bf16[896,1024]{1,0:T(8,128)(2,1)S(1)}, bf16[896,1024]{1,0:T(8,128)(2,1)}, u32[]{:S(2)}) copy-start(bf16[896,1024]{1,0:T(8,128)(2,1)} %wv_ref.3) | copy-start | bytes 5505028
  11.5 1.1 copy-start.4
  12.7 1.1 copy-start.5
  13.8 8.5 %copy-start.2 = (bf16[896,1024]{1,0:T(8,128)(2,1)S(1)}, bf16[896,1024]{1,0:T(8,128)(2,1)}, u32[]{:S(2)}) copy-start(bf16[896,1024]{1,0:T(8,128)(2,1)} %wk_ref.3) | copy-start | bytes 5505028
  21.8 16.0 %collective-permute-start = (bf16[896,256]{1,0:T(8,128)(2,1)S(1)}, bf16[896,256]{1,0:T(8,128)(2,1)S(1)}, u32[]{:S(2)}, u32[]{:S(2)}) collective-permute-start(bf16[896,256]{1,0:T(8,128)(2,1)S(1)} %get-tuple-element.11), channel_id=1, source_target_pairs={{0,1},{1,0},{2,3},{3,2},{4,5},{5,4},{6,7},{7,6},{8,9},{9,8},{10,11... | collective-permute-start | bytes 1376264 | tf_op jit(solution)/shard_map/ppermute | solution.py:232
  37.7 8.3 %collective-permute-start.1 = (bf16[896,512]{1,0:T(8,128)(2,1)S(1)}, bf16[896,512]{1,0:T(8,128)(2,1)}, u32[]{:S(2)}, u32[]{:S(2)}) collective-permute-start(bf16[896,512]{1,0:T(8,128)(2,1)S(1)} %get-tuple-element.13), channel_id=1, source_target_pairs={{0,1},{1,0},{2,3},{3,2},{4,5},{5,4},{6,7},{7,6},{8,9},{9,8},{10,11... | collective-permute-start | bytes 2752520 | tf_op jit(solution)/shard_map/ppermute | solution.py:232
  38.7 26.0 %all-to-all-start = ((bf16[8,112,256]{2,1,0:T(8,128)(2,1)}), bf16[8,112,256]{2,1,0:T(8,128)(2,1)S(1)}, u32[]{:S(2)}, u32[]{:S(2)}) async-start(bf16[8,112,256]{2,1,0:T(8,128)(2,1)} %bitcast.36), calls=%async_computation | async-start | bytes 917504 | tf_op jit(solution)/shard_map/all_to_all | solution.py:235
  64.7 26.2 %copy-start.8 = (bf16[8,112,256]{2,1,0:T(8,128)(2,1)}, bf16[8,112,256]{2,1,0:T(8,128)(2,1)S(1)}, u32[]{:S(2)}) copy-start(bf16[8,112,256]{2,1,0:T(8,128)(2,1)S(1)} %all-to-all-done.refs_0_) | copy-start | bytes 1376260
  64.7 26.1 %all-to-all-start.1 = ((bf16[8,112,512]{2,1,0:T(8,128)(2,1)}), bf16[8,112,512]{2,1,0:T(8,128)(2,1)S(1)}, u32[]{:S(2)}, u32[]{:S(2)}) async-start(bf16[8,112,512]{2,1,0:T(8,128)(2,1)} %bitcast.14), calls=%async_computation.1 | async-start | bytes 1835008 | tf_op jit(solution)/shard_map/all_to_all | solution.py:235
  90.9 0.9 copy-start.7
Sparse Core Ops, SparseCore 0:
  10.1 53.9 all-gather.2

commit v2 on v1

v2 whole, which is shorter than its diff:
```python
import functools

import jax
import jax.numpy as jnp
from jax import lax
from jax.experimental import pallas as pl
from jax.experimental.pallas import tpu as pltpu
from jax.sharding import PartitionSpec as P

HD = 128
DE = 896
CL = 64
R = 128
HR = R // 2
F32 = jnp.float32
BF16 = jnp.bfloat16
NT = (((1,), (1,)), ((), ()))
TN = (((0,), (0,)), ((), ()))


def _dot(a, b, dims=(((1,), (0,)), ((), ()))):
    return lax.dot_general(a, b, dims, preferred_element_type=F32)


def _span_kernel(first, spans, sec_ref, q_ref, g_ref, l_ref, n_ref, wk_ref, wv_ref, *rest):
    dq_ref, mine_ref, send_ref = rest[-3:]
    sec = sec_ref[0]
    inv_root = HD ** (-0.5)
    pairs = q_ref.shape[1] // (2 * HD)
    rows = []
    for a in range(spans):
        for half in range(2):
            for k in range(2):
                lo = k * R + half * HR
                rows.append(n_ref[a, lo : lo + HR, :])
    rows = jnp.concatenate(rows, axis=0)
    left = lax.broadcasted_iota(jnp.int32, (CL, 2 * HD), 1) < HD
    key_cols = [[] for _ in range(spans)]
    value_cols = [[] for _ in range(spans)]
    for p in range(pairs):
        cols = slice(2 * HD * p, 2 * HD * (p + 1))
        keys = _dot(rows, wk_ref[:, cols]).astype(BF16)
        values = _dot(rows, wv_ref[:, cols]).astype(BF16)
        for a in range(spans):
            ks = keys[2 * R * a : 2 * R * (a + 1)]
            vs = values[2 * R * a : 2 * R * (a + 1)]
            q = q_ref[CL * a : CL * (a + 1), cols]
            g = g_ref[CL * a : CL * (a + 1), cols]
            zero = jnp.zeros_like(q)
            qd = jnp.concatenate([jnp.where(left, q, zero), jnp.where(left, zero, q)], axis=0)
            gd = jnp.concatenate([jnp.where(left, g, zero), jnp.where(left, zero, g)], axis=0)
            at = slice(CL * (first + a), CL * (first + a + 1))
            logs = jnp.concatenate(
                [l_ref[2 * p : 2 * p + 1, at], l_ref[2 * p + 1 : 2 * p + 2, at]], axis=1
            )
            prob = jnp.exp(_dot(ks, qd, NT) * inv_root - logs)
            prob_grad = _dot(vs, gd, NT)
            delta = jnp.sum(prob * prob_grad, axis=0, keepdims=True)
            score_bf = (prob * (prob_grad - delta)).astype(BF16)
            prob_bf = prob.astype(BF16)
            key_cols[a].append((_dot(score_bf, qd) * inv_root).astype(BF16))
            value_cols[a].append(_dot(prob_bf, gd).astype(BF16))
            dq = (_dot(score_bf, ks, TN) * inv_root).astype(BF16)
            dq_ref[CL * a : CL * (a + 1), 2 * HD * p : 2 * HD * p + HD] = dq[:CL, :HD]
            dq_ref[CL * a : CL * (a + 1), 2 * HD * p + HD : 2 * HD * (p + 1)] = dq[CL:, HD:]
    width = DE // 2
    for a in range(spans):
        key_grad = jnp.concatenate(key_cols[a], axis=1)
        value_grad = jnp.concatenate(value_cols[a], axis=1)
        for lane, out_ref in ((sec, mine_ref), (1 - sec, send_ref)):
            at = pl.ds(pl.multiple_of(lane * width, width), width)
            part = _dot(wk_ref[at, :], key_grad, NT) + _dot(wv_ref[at, :], value_grad, NT)
            part = part.astype(BF16)
            for half in range(2):
                out_ref[half, :, R * a : R * (a + 1)] = part[:, half * R : (half + 1) * R]


def _span_call(first, spans, section, queries, grad_out, log_sums, neighbours, kw, vw, held):
    tokens, columns = queries.shape
    heads = log_sums.shape[0]
    whole = lambda i, s: (0, 0)
    block = first // spans
    in_specs = [
        pl.BlockSpec((spans * CL, columns), lambda i, s: (block, 0)),
        pl.BlockSpec((spans * CL, columns), lambda i, s: (block, 0)),
        pl.BlockSpec((heads, tokens), whole),
        pl.BlockSpec((spans, 2 * R, DE), lambda i, s: (block, 0, 0)),
        pl.BlockSpec((DE, columns), whole),
        pl.BlockSpec((DE, columns), whole),
    ]
    args = [queries, grad_out, log_sums, neighbours, kw, vw]
    args = [pltpu.with_memory_space_constraint(x, pltpu.HBM) for x in args]
    aliases = {}
    if held is not None:
        in_specs.append(pl.BlockSpec(memory_space=pl.ANY))
        args.append(held)
        aliases = {len(args): 0}
    half_spec = pl.BlockSpec((2, DE // 2, spans * R), lambda i, s: (0, 0, 0))
    half_shape = jax.ShapeDtypeStruct((2, DE // 2, spans * R), BF16)
    return pl.pallas_call(
        functools.partial(_span_kernel, first, spans),
        grid_spec=pltpu.PrefetchScalarGridSpec(
            num_scalar_prefetch=1,
            grid=(1,),
            in_specs=in_specs,
            out_specs=[
                pl.BlockSpec((spans * CL, columns), lambda i, s: (block, 0)),
                half_spec,
                half_spec,
            ],
        ),
        out_shape=[jax.ShapeDtypeStruct((tokens, columns), BF16), half_shape, half_shape],
        input_output_aliases=aliases,
        compiler_params=pltpu.CompilerParams(vmem_limit_bytes=48 << 20),
        cost_estimate=pl.CostEstimate(
            flops=spans * 2 * R * columns * (8 * DE + 10 * CL),
            transcendentals=spans * 2 * R * CL * heads,
            bytes_accessed=4 * DE * columns + spans * 1000000,
        ),
    )(section, *args)


def _scatter(got, src, count, peers, spans, first, place_ref, ids_ref, slot_ref, acc_ref):
    inner = peers // 2
    low = lax.broadcasted_iota(jnp.int32, acc_ref.shape[1:], 1) < HR
    turn = jnp.bitwise_xor(src % inner, place_ref[1])
    side = jnp.bitwise_xor(src // inner, place_ref[0])
    at = ((2 * turn + side) * spans + first) * 2
    for c in range(count):
        tile = got[src, :, R * c : R * (c + 1)].astype(F32)
        left = slot_ref[ids_ref[at + 2 * c]]
        right = slot_ref[ids_ref[at + 2 * c + 1]]
        acc_ref[left] += jnp.where(low, tile, 0.0)
        acc_ref[right] += jnp.where(low, 0.0, tile)


def _weight_kernel(spans, chunks, place_ref, ids_ref, slot_ref, *refs):
    n_gots = len(chunks)
    n_xs = len(refs) - 5 - 2 * n_gots
    got_hbm, x_hbm = refs[:n_gots], refs[n_gots : n_gots + n_xs]
    out_ref, acc_ref, enc_ref = refs[n_gots + n_xs : n_gots + n_xs + 3]
    gots = refs[n_gots + n_xs + 3 : 2 * n_gots + n_xs + 3]
    x_refs, sems = refs[-2], refs[-1]
    peers = gots[0].shape[0]
    blocks, cols = acc_ref.shape[:2]
    owned = blocks // peers
    inner = peers // 2
    upper, lower, sec = place_ref[0], place_ref[1], place_ref[2]
    share = owned // 2
    rows = share * HR

    got_copies = [pltpu.make_async_copy(got_hbm[n], gots[n], sems.at[n]) for n in range(n_gots)]
    x_copies = []
    for n in range(n_xs):
        to = x_refs.at[n // 2, (n % 2) * rows : (n % 2 + 1) * rows, :]
        x_copies.append(pltpu.make_async_copy(x_hbm[n].at[:rows, :], to, sems.at[n_gots + n]))
    for copy in got_copies + x_copies:
        copy.start()
    acc_ref[...] = jnp.zeros_like(acc_ref)
    first = 0
    for n, count in enumerate(chunks):
        got_copies[n].wait()

        def add_peer(src, carry, n=n, count=count, first=first):
            _scatter(
                gots[n], src, count, peers, spans, first, place_ref, ids_ref, slot_ref, acc_ref
            )
            return carry

        lax.fori_loop(0, peers, add_peer, 0)
        first += count
    low = lax.broadcasted_iota(jnp.int32, (cols, R), 1) < HR
    total = None
    for turn in range(inner):
        for far in range(2):
            n = 2 * turn + far
            near_sec = 1 - sec if far else sec
            for side in range(2):
                owner = jnp.bitwise_xor(lower, turn) + inner * (1 - upper if side else upper)
                base = owner * owned + near_sec * share
                for b in range(0, share, 2):
                    even = acc_ref[base + b]
                    odd = acc_ref[base + b + 1]
                    even = even + pltpu.roll(even, HR, 1)
                    odd = odd + pltpu.roll(odd, HR, 1)
                    lo = side * rows + b * HR
                    enc_ref[n, :, lo : lo + 2 * HR] = jnp.where(low, even, odd).astype(BF16)
            x_copies[2 * n].wait()
            x_copies[2 * n + 1].wait()
            part = _dot(enc_ref[n], x_refs[n])
            total = part if total is None else total + part
    scale = (blocks * R) ** (-0.5)
    out_ref[...] = (total * scale).T


def _weight_call(spans, chunks, place, ids, slots, gots, xs):
    cols = gots[0].shape[1]
    blocks = slots.shape[0]
    owned = blocks // gots[0].shape[0]
    smem = pl.BlockSpec(memory_space=pltpu.SMEM)
    anywhere = pl.BlockSpec(memory_space=pl.ANY)
    large = [pltpu.with_memory_space_constraint(x, pltpu.HBM) for x in [*gots, *xs]]
    pairs = len(xs) // 2
    return pl.pallas_call(
        functools.partial(_weight_kernel, spans, chunks),
        in_specs=[smem] * 3 + [anywhere] * len(large),
        out_specs=pl.BlockSpec(memory_space=pltpu.VMEM),
        out_shape=jax.ShapeDtypeStruct((DE, cols), F32),
        scratch_shapes=[
            pltpu.VMEM((blocks, cols, R), F32),
            pltpu.VMEM((pairs, cols, owned * HR), BF16),
        ]
        + [pltpu.VMEM(x.shape, BF16) for x in gots]
        + [
            pltpu.VMEM((pairs, owned * HR, DE), BF16),
            pltpu.SemaphoreType.DMA((len(large),)),
        ],
        compiler_params=pltpu.CompilerParams(vmem_limit_bytes=40 << 20),
        cost_estimate=pl.CostEstimate(
            flops=2 * cols * blocks * HR * DE, transcendentals=0, bytes_accessed=6000000
        ),
    )(place, ids, slots, *large)


def per_device(
    queries,
    grad_out,
    log_sums,
    neighbours,
    key_weight,
    value_weight,
    neighbour_ids,
    block_slot,
    enc_input,
):
    spans = neighbour_ids.shape[0]
    owned = enc_input.shape[0] // R
    peers = lax.axis_size("dp")
    inner = peers // 2
    section = lax.axis_index("section").astype(jnp.int32)
    index = lax.axis_index("dp").astype(jnp.int32)
    upper, lower = index // inner, index % inner
    swap = [(0, 1), (1, 0)]

    id_rows = jnp.pad(neighbour_ids.astype(BF16), ((0, -spans % 8), (0, DE - 2)))
    split = enc_input.reshape(2, owned // 2, 2, HR, DE)
    split = lax.dynamic_index_in_dim(split, section, 0, keepdims=False)
    own = lax.dynamic_index_in_dim(split, upper, 1, keepdims=False)
    own = jnp.concatenate([own.reshape(owned // 2 * HR, DE), id_rows], axis=0)
    away = lax.dynamic_index_in_dim(split, 1 - upper, 1, keepdims=False)
    away = jnp.concatenate([away.reshape(owned // 2 * HR, DE), id_rows], axis=0)
    mirror = lax.ppermute(away, "dp", [(i, i ^ inner) for i in range(peers)])

    def spread(pack):
        return [pack] + [
            lax.ppermute(pack, "dp", [(i, i ^ m) for i in range(peers)]) for m in range(1, inner)
        ]

    own = spread(own)
    held = None
    gots = []
    first = 0
    chunks = (spans // 2, spans - spans // 2)
    for count in chunks:
        held, mine, send = _span_call(
            first,
            count,
            section[None],
            queries,
            grad_out,
            log_sums,
            neighbours,
            key_weight,
            value_weight,
            held,
        )
        if not gots:
            mirror, own, send = lax.optimization_barrier((mirror, own, send))
        other = lax.ppermute(send, "section", swap)
        if gots:
            gots[-1], other = lax.optimization_barrier((gots[-1], other))
        ref_grad = (mine.astype(F32) + other.astype(F32)).astype(BF16)
        ref_grad = ref_grad.reshape(peers, DE // peers, count * R)
        held, mirror, ref_grad = lax.optimization_barrier((held, mirror, ref_grad))
        gots.append(lax.all_to_all(ref_grad, "dp", 0, 0, tiled=True))
        first += count

    packs = spread(mirror)
    xs = []
    for pair in zip(own, packs):
        xs += list(pair) + [lax.ppermute(x, "section", swap) for x in pair]
    cut = owned // 2 * HR
    ids = [x[cut : cut + spans, :2] for pair in zip(own, packs) for x in pair]
    ids = jnp.concatenate(ids, axis=0).astype(jnp.int32)
    place = jnp.stack([upper, lower, section])
    weight = _weight_call(
        spans, chunks, place, ids.reshape(-1), block_slot, gots, xs
    )
    rows = DE // (2 * peers)
    cols = DE // peers
    tiles = lax.all_to_all(weight.reshape(2 * peers, rows, cols), ("dp", "section"), 0, 0, tiled=True)
    tiles = tiles.reshape(2, inner, 2, rows, cols)
    weight_grad = jnp.transpose(tiles[0] + tiles[1], (2, 1, 0, 3)).reshape(rows, DE)
    return (held, weight_grad)


def solution(mesh):
    return jax.shard_map(
        per_device,
        mesh=mesh,
        in_specs=(
            P(("group", "dp"), "section"),
            P(("group", "dp"), "section"),
            P("section", ("group", "dp")),
            P(("group", "dp"), None, None),
            P(None, "section"),
            P(None, "section"),
            P(("group", "dp"), None),
            P("group"),
            P(("group", "dp"), None),
        ),
        out_specs=(P(("group", "dp"), "section"), P(("group", "dp", "section"), None)),
        check_vma=False,
    )
```

time: 122 us -> 105 us (0.86)
  between operations: 14.1 us -> 0.97 us
  waiting for transfers between devices: 37.6 us -> 27.4 us
  starting transfers between devices: 11.6 us -> 21.4 us
  local copies, waits for them, and re-layouts: 7.19 us -> 4.28 us
  other arithmetic: 5.72 us -> 3 us
  Pallas kernels: 28.4 us -> 30.1 us
    all_to_all x2, waiting for transfers between devices: 37.5 us -> 3.42 us  [per_device(): gots.append(lax.all_to_all(ref_grad, 'dp', 0, 0, tiled=True))]
    ppermute x0 -> x15, waiting for transfers between devices: none -> 19.8 us  [the longest x6 19.7 us: spread(): lax.ppermute(pack, 'dp', [(i, i ^ m) for i in range(peers)])]
    ppermute x0 -> x15, starting transfers between devices: none -> 12.7 us  [the longest x6 8.18 us: spread(): lax.ppermute(pack, 'dp', [(i, i ^ m) for i in range(peers)])]
    unnamed x19 -> x28, local copies, waits for them, and re-layouts: 5.62 us -> 0.94 us
    ppermute x2, waiting for transfers between devices: 0.01 us -> 4.26 us  [per_device(): other = lax.ppermute(send, 'section', swap)]
    all_to_all x2, starting transfers between devices: 10.9 us -> 8.52 us  [per_device(): gots.append(lax.all_to_all(ref_grad, 'dp', 0, 0, tiled=True))]
    pallas_call x3, Pallas kernels: 28.4 us -> 30.1 us  [the longest x2 25.3 us: _span_call(): pl.pallas_call(functools.partial(_span_kernel, first, spans), grid_spec=p...]
  transfers between devices with their start and end apart: 5 -> 19, of which waited for: 2 -> 6; matrix products, arithmetic and copies ran while one was open for 4% -> 1% of each run, Pallas kernels for 19% -> 24%
where the time goes in v2:
time: 105 us
  Pallas kernels  30.1 us (29%)
  waiting for transfers between devices  27.4 us (26%)
  starting transfers between devices  21.4 us (20%)
  blocking collectives  17.8 us (17%)
  local copies, waits for them, and re-layouts  4.28 us (4%)
  other arithmetic  3 us (3%)
    pallas_call x2, Pallas kernels, _span_call(): pl.pallas_call(functools.partial(_span_kernel, first, spans), grid_spec=p...  25.3 us
    ppermute x6, waiting for transfers between devices, spread(): lax.ppermute(pack, 'dp', [(i, i ^ m) for i in range(peers)])  19.7 us
    all_to_all x1, blocking collectives, per_device(): lax.all_to_all(weight.reshape(2 * peers, rows, cols), ('dp', 'section'),...  17.8 us
    all_to_all x2, starting transfers between devices, per_device(): gots.append(lax.all_to_all(ref_grad, 'dp', 0, 0, tiled=True))  8.52 us
    ppermute x6, starting transfers between devices, spread(): lax.ppermute(pack, 'dp', [(i, i ^ m) for i in range(peers)])  8.18 us
    pallas_call x1, Pallas kernels, _weight_call(): pl.pallas_call(functools.partial(_weight_kernel, spans, chunks), in_specs...  4.74 us
    ppermute x2, waiting for transfers between devices, per_device(): other = lax.ppermute(send, 'section', swap)  4.26 us
    all_to_all x2, waiting for transfers between devices, per_device(): gots.append(lax.all_to_all(ref_grad, 'dp', 0, 0, tiled=True))  3.42 us
  transfers between devices with their start and end apart: 19, of which 6 were waited for; matrix products, arithmetic and copies ran while one was open for 1% of the time, Pallas kernels for 24%

profile of v2, /device:TPU:0, one launch (start us, length us, event | category | flops | bytes accessed | tf_op | source)
XLA Modules:
  0.0 104.9 jit_solution(12654028248485454212)
XLA Ops:
  0.7 0.7 convert_element_type.30
  1.3 0.1 copy.34
  1.5 1.1 %constant_dynamic-slice_fusion = (bf16[1,2,1,64,896]{4,3,2,1,0:T(8,128)(2,1)S(1)}, bf16[1,2,1,64,896]{4,3,2,1,0:T(8,128)(2,1)S(1)}) fusion(bf16[2,2,2,64,896]{4,3,2,1,0:T(8,128)(2,1)} %bitcast.22, s32[]{:T(128)S(6)} %select_n.29, s32[]{:T(128)S(6)} %select_n.34, s32[]{:T(128)S(6)} %select_n.32), kind=kLoop, calls=%fused_computation.9 | loop fusion | bytes 917516 | tf_op jit(solution)/shard_map/jit(dynamic_index_in_dim)/dynamic_slice | solution.py:248
  2.6 4.0 %collective-permute-start.3 = (bf16[136,896]{1,0:T(8,128)(2,1)S(1)}, bf16[136,896]{1,0:T(8,128)(2,1)S(1)}, u32[]{:S(2)}, u32[]{:S(2)}) collective-permute-start(bf16[136,896]{1,0:T(8,128)(2,1)S(1)} %get-tuple-element.35.refs_2_), channel_id=1, source_target_pairs={{0,6},{2,4},{4,2},{6,0},{8,14},{10,12},{12,10},{14,8},{1,7},{3,5},... | collective-permute-start | bytes 731144 | tf_op jit(solution)/shard_map/ppermute | solution.py:256
  6.7 0.4 collective-permute-start.2
  7.1 0.2 collective-permute-start.1
  7.3 2.9 %collective-permute-start = (bf16[136,896]{1,0:T(8,128)(2,1)S(1)}, bf16[136,896]{1,0:T(8,128)(2,1)S(1)}, u32[]{:S(2)}, u32[]{:S(2)}) collective-permute-start(bf16[136,896]{1,0:T(8,128)(2,1)S(1)} %get-tuple-element.45), channel_id=1, source_target_pairs={{0,8},{2,10},{4,12},{6,14},{8,0},{10,2},{12,4},{14,6},{1,9},{3,11}... | collective-permute-start | bytes 731144 | tf_op jit(solution)/shard_map/ppermute | solution.py:252
  10.2 12.7 %shard_map.104 = (bf16[384,1024]{1,0:T(8,128)(2,1)}, bf16[2,448,384]{2,1,0:T(8,128)(2,1)S(1)}, bf16[2,448,384]{2,1,0:T(8,128)(2,1)S(1)}) custom-call(s32[1]{0:T(128)} %bitcast.sec_ref, bf16[384,1024]{1,0:T(8,128)(2,1)} %q_ref.3, bf16[384,1024]{1,0:T(8,128)(2,1)} %g_ref.3, f32[8,384]{1,0:T(8,128)} %l_ref.3, bf16[6,256,896]{2,1,0:T(8,128)(2,1)} %n_ref.3, ...), custom_call_target="tpu_custom_call" | custom-call | flops 6140461056 | bytes 6670016 | tf_op jit(solution)/shard_map/pallas_call | solution.py:100
  22.9 0.0 collective-permute-done.refs_3_
  22.9 0.0 collective-permute-done.3.refs_14_
  22.9 0.3 collective-permute-done.2.refs_10_
  23.2 0.0 collective-permute-done.1.refs_6_
  23.2 0.1 collective-permute-start.4
  23.3 2.1 %collective-permute-done.4 = bf16[2,448,384]{2,1,0:T(8,128)(2,1)S(1)} collective-permute-done((bf16[2,448,384]{2,1,0:T(8,128)(2,1)S(1)}, bf16[2,448,384]{2,1,0:T(8,128)(2,1)S(1)}, u32[]{:S(2)}, u32[]{:S(2)}) %collective-permute-start.4) | collective-permute-done | bytes 688160 | tf_op jit(solution)/shard_map/ppermute | solution.py:279
  25.4 1.0 add_convert_fusion.1
  26.5 4.9 %all-to-all-start = ((bf16[8,112,384]{2,1,0:T(8,128)(2,1)}), bf16[8,112,384]{2,1,0:T(8,128)(2,1)S(1)}, u32[]{:S(2)}, u32[]{:S(2)}) async-start(bf16[8,112,384]{2,1,0:T(8,128)(2,1)} %bitcast.4), calls=%async_computation | async-start | bytes 1376256 | tf_op jit(solution)/shard_map/all_to_all | solution.py:285
  31.4 12.7 %shard_map.105 = (bf16[384,1024]{1,0:T(8,128)(2,1)}, bf16[2,448,384]{2,1,0:T(8,128)(2,1)S(1)}, bf16[2,448,384]{2,1,0:T(8,128)(2,1)S(1)}) custom-call(s32[1]{0:T(128)} %bitcast.sec_ref, bf16[384,1024]{1,0:T(8,128)(2,1)} %q_ref.3, bf16[384,1024]{1,0:T(8,128)(2,1)} %g_ref.3, f32[8,384]{1,0:T(8,128)} %l_ref.3, ...), custom_call_target="tpu_custom_call", output_to_operand_aliasing={{0}: (7, {})} | custom-call | flops 6140461056 | bytes 6670016 | tf_op jit(solution)/shard_map/pallas_call | solution.py:100
  44.0 0.1 collective-permute-start.5
  44.1 2.1 %collective-permute-done.5 = bf16[2,448,384]{2,1,0:T(8,128)(2,1)S(1)} collective-permute-done((bf16[2,448,384]{2,1,0:T(8,128)(2,1)S(1)}, bf16[2,448,384]{2,1,0:T(8,128)(2,1)S(1)}, u32[]{:S(2)}, u32[]{:S(2)}) %collective-permute-start.5) | collective-permute-done | bytes 688160 | tf_op jit(solution)/shard_map/ppermute | solution.py:279
  46.2 3.4 %all-to-all-done.refs_0_ = bf16[8,112,384]{2,1,0:T(8,128)(2,1)S(1)} async-done(((bf16[8,112,384]{2,1,0:T(8,128)(2,1)}), bf16[8,112,384]{2,1,0:T(8,128)(2,1)S(1)}, u32[]{:S(2)}, u32[]{:S(2)}) %all-to-all-start) | async-done | bytes 688160 | tf_op jit(solution)/shard_map/all_to_all | solution.py:285
  49.7 1.1 %add_convert_fusion = bf16[2,448,384]{2,1,0:T(8,128)(2,1)} fusion(bf16[2,448,384]{2,1,0:T(8,128)(2,1)S(1)} %collective-permute-done.5, bf16[2,448,384]{2,1,0:T(8,128)(2,1)S(1)} %get-tuple-element.30), kind=kLoop, calls=%fused_computation | loop fusion | flops 1376256 | bytes 2064384 | tf_op jit(solution)/shard_map/convert_element_type | solution.py:282
  50.8 0.0 copy-done.1
  50.8 3.6 %all-to-all-start.1 = ((bf16[8,112,384]{2,1,0:T(8,128)(2,1)}), bf16[8,112,384]{2,1,0:T(8,128)(2,1)S(1)}, u32[]{:S(2)}, u32[]{:S(2)}) async-start(bf16[8,112,384]{2,1,0:T(8,128)(2,1)} %bitcast.5), calls=%async_computation.1 | async-start | bytes 1376256 | tf_op jit(solution)/shard_map/all_to_all | solution.py:285
  54.4 0.0 collective-permute-start.9
  54.4 0.5 collective-permute-start.11
  54.9 0.1 collective-permute-start.13
  55.0 2.8 %collective-permute-start.8 = (bf16[136,896]{1,0:T(8,128)(2,1)S(1)}, bf16[136,896]{1,0:T(8,128)(2,1)S(1)}, u32[]{:S(2)}, u32[]{:S(2)}) collective-permute-start(bf16[136,896]{1,0:T(8,128)(2,1)S(1)} %collective-permute-done.refs_3_), channel_id=1, source_target_pairs={{0,6},{2,4},{4,2},{6,0},{8,14},{10,12},{12,10},{14,8},{1,7},{3,5},... | collective-permute-start | bytes 731144 | tf_op jit(solution)/shard_map/ppermute | solution.py:256
  57.9 0.6 collective-permute-start.7
  58.4 0.0 collective-permute-done.9.refs_4_
  58.4 0.1 collective-permute-start.6
  58.5 0.0 collective-permute-done.11.refs_8_
  58.5 0.0 collective-permute-start.15
  58.5 0.0 collective-permute-done.13.refs_12_
  58.6 0.5 collective-permute-start.10
  59.0 16.1 %collective-permute-done.8.refs_15_ = bf16[136,896]{1,0:T(8,128)(2,1)S(1)} collective-permute-done((bf16[136,896]{1,0:T(8,128)(2,1)S(1)}, bf16[136,896]{1,0:T(8,128)(2,1)S(1)}, u32[]{:S(2)}, u32[]{:S(2)}) %collective-permute-start.8) | collective-permute-done | bytes 243744 | tf_op jit(solution)/shard_map/ppermute | solution.py:256
  75.2 0.0 collective-permute-start.16
  75.2 3.3 %collective-permute-done.7.refs_11_ = bf16[136,896]{1,0:T(8,128)(2,1)S(1)} collective-permute-done((bf16[136,896]{1,0:T(8,128)(2,1)S(1)}, bf16[136,896]{1,0:T(8,128)(2,1)S(1)}, u32[]{:S(2)}, u32[]{:S(2)}) %collective-permute-start.7) | collective-permute-done | bytes 243744 | tf_op jit(solution)/shard_map/ppermute | solution.py:256
  78.5 0.0 collective-permute-start.14
  78.5 0.0 collective-permute-done.6.refs_7_
  78.5 0.6 collective-permute-start.12
  79.0 0.1 pad_add_fusion.place_ref
  79.1 0.0 copy-done.6
  79.2 0.1 copy.36
  79.3 0.1 copy.38
  79.4 0.1 copy.40
  79.5 0.1 copy.42
  79.6 0.1 copy.37
  79.7 0.1 copy.43
  79.8 0.1 copy.41
  79.9 0.1 copy.39
  80.1 0.1 concatenate.11
  80.2 0.1 copy.44
  80.3 0.1 reshape.48.ids_ref
  80.4 0.0 collective-permute-done.15.refs_16_
  80.4 0.0 collective-permute-done.10.refs_5_
  80.4 0.0 collective-permute-done.16.refs_17_
  80.4 0.0 collective-permute-done.14.refs_13_
  80.4 0.0 collective-permute-done.12.refs_9_
  80.4 0.0 all-to-all-done.1.refs_1_
  80.5 0.9 copy-done.2
  81.4 4.7 %shard_map.106 = f32[896,112]{1,0:T(8,128)S(1)} custom-call(s32[3]{0:T(128)S(1)} %pad_add_fusion.place_ref, s32[96]{0:T(128)S(1)} %reshape.48.ids_ref, s32[32]{0:T(128)S(1)} %copy-done, bf16[8,112,384]{2,1,0:T(8,128)(2,1)} %copy-done.1, bf16[8,112,384]{2,1,0:T(8,128)(2,1)} %copy-done.2, bf16[136,896]{1,0:T(8,128)(2,1)} %copy-done.3, ...), custom_call_target="tpu_custom_call" | custom-call | flops 411041792 | bytes 6000000 | tf_op jit(solution)/shard_map/pallas_call | solution.py:204
  86.1 17.8 %all_to_all.15 = f32[16,56,112]{2,1,0:T(8,128)S(1)} all-to-all(f32[16,56,112]{2,1,0:T(8,128)S(1)} %bitcast.17), channel_id=1, replica_groups=mesh['group'=2,'dp'=8,'section'=2] {'dp','section'}, dimensions={0} | all-to-all | bytes 802816 | tf_op jit(solution)/shard_map/all_to_all | solution.py:301
  104.0 0.1 copy.49
  104.1 0.9 reshape.47
  (36 shorter events, 0.1 us)
Async XLA Ops:
  2.6 76.5 %copy-start.3 = (bf16[136,896]{1,0:T(8,128)(2,1)}, bf16[136,896]{1,0:T(8,128)(2,1)S(1)}, u32[]{:S(2)}) copy-start(bf16[136,896]{1,0:T(8,128)(2,1)S(1)} %get-tuple-element.35.refs_2_) | copy-start | bytes 731140
  2.6 20.3 %collective-permute-start.3 = (bf16[136,896]{1,0:T(8,128)(2,1)S(1)}, bf16[136,896]{1,0:T(8,128)(2,1)S(1)}, u32[]{:S(2)}, u32[]{:S(2)}) collective-permute-start(bf16[136,896]{1,0:T(8,128)(2,1)S(1)} %get-tuple-element.35.refs_2_), channel_id=1, source_target_pairs={{0,6},{2,4},{4,2},{6,0},{8,14},{10,12},{12,10},{14,8},{1,7},{3,5},... | collective-permute-start | bytes 731144 | tf_op jit(solution)/shard_map/ppermute | solution.py:256
  6.7 16.6 %collective-permute-start.2 = (bf16[136,896]{1,0:T(8,128)(2,1)S(1)}, bf16[136,896]{1,0:T(8,128)(2,1)S(1)}, u32[]{:S(2)}, u32[]{:S(2)}) collective-permute-start(bf16[136,896]{1,0:T(8,128)(2,1)S(1)} %get-tuple-element.35.refs_2_), channel_id=1, source_target_pairs={{0,4},{2,6},{4,0},{6,2},{8,12},{10,14},{12,8},{14,10},{1,5},{3,7},... | collective-permute-start | bytes 731144 | tf_op jit(solution)/shard_map/ppermute | solution.py:256
  7.1 16.1 %collective-permute-start.1 = (bf16[136,896]{1,0:T(8,128)(2,1)S(1)}, bf16[136,896]{1,0:T(8,128)(2,1)S(1)}, u32[]{:S(2)}, u32[]{:S(2)}) collective-permute-start(bf16[136,896]{1,0:T(8,128)(2,1)S(1)} %get-tuple-element.35.refs_2_), channel_id=1, source_target_pairs={{0,2},{2,0},{4,6},{6,4},{8,10},{10,8},{12,14},{14,12},{1,3},{3,1},... | collective-permute-start | bytes 731144 | tf_op jit(solution)/shard_map/ppermute | solution.py:256
  7.3 15.6 %collective-permute-start = (bf16[136,896]{1,0:T(8,128)(2,1)S(1)}, bf16[136,896]{1,0:T(8,128)(2,1)S(1)}, u32[]{:S(2)}, u32[]{:S(2)}) collective-permute-start(bf16[136,896]{1,0:T(8,128)(2,1)S(1)} %get-tuple-element.45), channel_id=1, source_target_pairs={{0,8},{2,10},{4,12},{6,14},{8,0},{10,2},{12,4},{14,6},{1,9},{3,11}... | collective-permute-start | bytes 731144 | tf_op jit(solution)/shard_map/ppermute | solution.py:252
  22.9 56.7 %copy-start.7 = (bf16[136,896]{1,0:T(8,128)(2,1)}, bf16[136,896]{1,0:T(8,128)(2,1)S(1)}, u32[]{:S(2)}) copy-start(bf16[136,896]{1,0:T(8,128)(2,1)S(1)} %collective-permute-done.refs_3_) | copy-start | bytes 731140
  22.9 56.3 %copy-start.4 = (bf16[136,896]{1,0:T(8,128)(2,1)}, bf16[136,896]{1,0:T(8,128)(2,1)S(1)}, u32[]{:S(2)}) copy-start(bf16[136,896]{1,0:T(8,128)(2,1)S(1)} %collective-permute-done.3.refs_14_) | copy-start | bytes 731140
  23.2 55.9 %copy-start.5 = (bf16[136,896]{1,0:T(8,128)(2,1)}, bf16[136,896]{1,0:T(8,128)(2,1)S(1)}, u32[]{:S(2)}) copy-start(bf16[136,896]{1,0:T(8,128)(2,1)S(1)} %collective-permute-done.2.refs_10_) | copy-start | bytes 731140
  23.2 55.9 %copy-start.6 = (bf16[136,896]{1,0:T(8,128)(2,1)}, bf16[136,896]{1,0:T(8,128)(2,1)S(1)}, u32[]{:S(2)}) copy-start(bf16[136,896]{1,0:T(8,128)(2,1)S(1)} %collective-permute-done.1.refs_6_) | copy-start | bytes 731140
  23.2 2.2 %collective-permute-start.4 = (bf16[2,448,384]{2,1,0:T(8,128)(2,1)S(1)}, bf16[2,448,384]{2,1,0:T(8,128)(2,1)S(1)}, u32[]{:S(2)}, u32[]{:S(2)}) collective-permute-start(bf16[2,448,384]{2,1,0:T(8,128)(2,1)S(1)} %get-tuple-element.26), channel_id=1, source_target_pairs={{0,1},{1,0},{2,3},{3,2},{4,5},{5,4},{6,7},{7,6},{8,9},{9,8},{10,11... | collective-permute-start | bytes 2064392 | tf_op jit(solution)/shard_map/ppermute | solution.py:279
  26.5 23.2 %all-to-all-start = ((bf16[8,112,384]{2,1,0:T(8,128)(2,1)}), bf16[8,112,384]{2,1,0:T(8,128)(2,1)S(1)}, u32[]{:S(2)}, u32[]{:S(2)}) async-start(bf16[8,112,384]{2,1,0:T(8,128)(2,1)} %bitcast.4), calls=%async_computation | async-start | bytes 1376256 | tf_op jit(solution)/shard_map/all_to_all | solution.py:285
  44.0 2.2 %collective-permute-start.5 = (bf16[2,448,384]{2,1,0:T(8,128)(2,1)S(1)}, bf16[2,448,384]{2,1,0:T(8,128)(2,1)S(1)}, u32[]{:S(2)}, u32[]{:S(2)}) collective-permute-start(bf16[2,448,384]{2,1,0:T(8,128)(2,1)S(1)} %get-tuple-element.32), channel_id=1, source_target_pairs={{0,1},{1,0},{2,3},{3,2},{4,5},{5,4},{6,7},{7,6},{8,9},{9,8},{10,11... | collective-permute-start | bytes 2064392 | tf_op jit(solution)/shard_map/ppermute | solution.py:279
  49.6 1.1 %copy-start.1 = (bf16[8,112,384]{2,1,0:T(8,128)(2,1)}, bf16[8,112,384]{2,1,0:T(8,128)(2,1)S(1)}, u32[]{:S(2)}) copy-start(bf16[8,112,384]{2,1,0:T(8,128)(2,1)S(1)} %all-to-all-done.refs_0_) | copy-start | bytes 2064388
  49.7 31.7 %copy-start = (s32[32]{0:T(128)S(1)}, s32[32]{0:T(128)}, u32[]{:S(2)}) copy-start(s32[32]{0:T(128)} %slot_ref.1) | copy-start | bytes 388
  50.8 29.7 %all-to-all-start.1 = ((bf16[8,112,384]{2,1,0:T(8,128)(2,1)}), bf16[8,112,384]{2,1,0:T(8,128)(2,1)S(1)}, u32[]{:S(2)}, u32[]{:S(2)}) async-start(bf16[8,112,384]{2,1,0:T(8,128)(2,1)} %bitcast.5), calls=%async_computation.1 | async-start | bytes 1376256 | tf_op jit(solution)/shard_map/all_to_all | solution.py:285
  54.4 4.0 %collective-permute-start.9 = (bf16[136,896]{1,0:T(8,128)(2,1)S(1)}, bf16[136,896]{1,0:T(8,128)(2,1)S(1)}, u32[]{:S(2)}, u32[]{:S(2)}) collective-permute-start(bf16[136,896]{1,0:T(8,128)(2,1)S(1)} %get-tuple-element.35.refs_2_), channel_id=1, source_target_pairs={{0,1},{1,0},{2,3},{3,2},{4,5},{5,4},{6,7},{7,6},{8,9},{9,8},{10,11... | collective-permute-start | bytes 731144 | tf_op jit(solution)/shard_map/ppermute | solution.py:291
  54.4 4.1 %collective-permute-start.11 = (bf16[136,896]{1,0:T(8,128)(2,1)S(1)}, bf16[136,896]{1,0:T(8,128)(2,1)S(1)}, u32[]{:S(2)}, u32[]{:S(2)}) collective-permute-start(bf16[136,896]{1,0:T(8,128)(2,1)S(1)} %collective-permute-done.1.refs_6_), channel_id=1, source_target_pairs={{0,1},{1,0},{2,3},{3,2},{4,5},{5,4},{6,7},{7,6},{8,9},{9,8},{10,11... | collective-permute-start | bytes 731144 | tf_op jit(solution)/shard_map/ppermute | solution.py:291
  54.9 3.6 %collective-permute-start.13 = (bf16[136,896]{1,0:T(8,128)(2,1)S(1)}, bf16[136,896]{1,0:T(8,128)(2,1)S(1)}, u32[]{:S(2)}, u32[]{:S(2)}) collective-permute-start(bf16[136,896]{1,0:T(8,128)(2,1)S(1)} %collective-permute-done.2.refs_10_), channel_id=1, source_target_pairs={{0,1},{1,0},{2,3},{3,2},{4,5},{5,4},{6,7},{7,6},{8,9},{9,8},{10,11... | collective-permute-start | bytes 731144 | tf_op jit(solution)/shard_map/ppermute | solution.py:291
  55.0 20.2 %collective-permute-start.8 = (bf16[136,896]{1,0:T(8,128)(2,1)S(1)}, bf16[136,896]{1,0:T(8,128)(2,1)S(1)}, u32[]{:S(2)}, u32[]{:S(2)}) collective-permute-start(bf16[136,896]{1,0:T(8,128)(2,1)S(1)} %collective-permute-done.refs_3_), channel_id=1, source_target_pairs={{0,6},{2,4},{4,2},{6,0},{8,14},{10,12},{12,10},{14,8},{1,7},{3,5},... | collective-permute-start | bytes 731144 | tf_op jit(solution)/shard_map/ppermute | solution.py:256
  57.9 20.6 %collective-permute-start.7 = (bf16[136,896]{1,0:T(8,128)(2,1)S(1)}, bf16[136,896]{1,0:T(8,128)(2,1)S(1)}, u32[]{:S(2)}, u32[]{:S(2)}) collective-permute-start(bf16[136,896]{1,0:T(8,128)(2,1)S(1)} %collective-permute-done.refs_3_), channel_id=1, source_target_pairs={{0,4},{2,6},{4,0},{6,2},{8,12},{10,14},{12,8},{14,10},{1,5},{3,7},... | collective-permute-start | bytes 731144 | tf_op jit(solution)/shard_map/ppermute | solution.py:256
  58.4 22.0 %copy-start.11 = (bf16[136,896]{1,0:T(8,128)(2,1)}, bf16[136,896]{1,0:T(8,128)(2,1)S(1)}, u32[]{:S(2)}) copy-start(bf16[136,896]{1,0:T(8,128)(2,1)S(1)} %collective-permute-done.9.refs_4_) | copy-start | bytes 731140
  58.4 20.0 %collective-permute-start.6 = (bf16[136,896]{1,0:T(8,128)(2,1)S(1)}, bf16[136,896]{1,0:T(8,128)(2,1)S(1)}, u32[]{:S(2)}, u32[]{:S(2)}) collective-permute-start(bf16[136,896]{1,0:T(8,128)(2,1)S(1)} %collective-permute-done.refs_3_), channel_id=1, source_target_pairs={{0,2},{2,0},{4,6},{6,4},{8,10},{10,8},{12,14},{14,12},{1,3},{3,1},... | collective-permute-start | bytes 731144 | tf_op jit(solution)/shard_map/ppermute | solution.py:256
  58.5 21.9 %copy-start.12 = (bf16[136,896]{1,0:T(8,128)(2,1)}, bf16[136,896]{1,0:T(8,128)(2,1)S(1)}, u32[]{:S(2)}) copy-start(bf16[136,896]{1,0:T(8,128)(2,1)S(1)} %collective-permute-done.11.refs_8_) | copy-start | bytes 731140
  58.5 21.9 %collective-permute-start.15 = (bf16[136,896]{1,0:T(8,128)(2,1)S(1)}, bf16[136,896]{1,0:T(8,128)(2,1)}, u32[]{:S(2)}, u32[]{:S(2)}) collective-permute-start(bf16[136,896]{1,0:T(8,128)(2,1)S(1)} %collective-permute-done.3.refs_14_), channel_id=1, source_target_pairs={{0,1},{1,0},{2,3},{3,2},{4,5},{5,4},{6,7},{7,6},{8,9},{9,8},{10,11... | collective-permute-start | bytes 731144 | tf_op jit(solution)/shard_map/ppermute | solution.py:291
  58.5 19.9 %copy-start.13 = (bf16[136,896]{1,0:T(8,128)(2,1)}, bf16[136,896]{1,0:T(8,128)(2,1)S(1)}, u32[]{:S(2)}) copy-start(bf16[136,896]{1,0:T(8,128)(2,1)S(1)} %collective-permute-done.13.refs_12_) | copy-start | bytes 731140
  58.6 21.8 %collective-permute-start.10 = (bf16[136,896]{1,0:T(8,128)(2,1)S(1)}, bf16[136,896]{1,0:T(8,128)(2,1)}, u32[]{:S(2)}, u32[]{:S(2)}) collective-permute-start(bf16[136,896]{1,0:T(8,128)(2,1)S(1)} %collective-permute-done.refs_3_), channel_id=1, source_target_pairs={{0,1},{1,0},{2,3},{3,2},{4,5},{5,4},{6,7},{7,6},{8,9},{9,8},{10,11... | collective-permute-start | bytes 731144 | tf_op jit(solution)/shard_map/ppermute | solution.py:291
  75.2 5.3 %copy-start.8 = (bf16[136,896]{1,0:T(8,128)(2,1)}, bf16[136,896]{1,0:T(8,128)(2,1)S(1)}, u32[]{:S(2)}) copy-start(bf16[136,896]{1,0:T(8,128)(2,1)S(1)} %collective-permute-done.8.refs_15_) | copy-start | bytes 731140
  75.2 5.2 %collective-permute-start.16 = (bf16[136,896]{1,0:T(8,128)(2,1)S(1)}, bf16[136,896]{1,0:T(8,128)(2,1)}, u32[]{:S(2)}, u32[]{:S(2)}) collective-permute-start(bf16[136,896]{1,0:T(8,128)(2,1)S(1)} %collective-permute-done.8.refs_15_), channel_id=1, source_target_pairs={{0,1},{1,0},{2,3},{3,2},{4,5},{5,4},{6,7},{7,6},{8,9},{9,8},{10,11... | collective-permute-start | bytes 731144 | tf_op jit(solution)/shard_map/ppermute | solution.py:291
  78.5 2.0 %copy-start.9 = (bf16[136,896]{1,0:T(8,128)(2,1)}, bf16[136,896]{1,0:T(8,128)(2,1)S(1)}, u32[]{:S(2)}) copy-start(bf16[136,896]{1,0:T(8,128)(2,1)S(1)} %collective-permute-done.7.refs_11_) | copy-start | bytes 731140
  78.5 2.0 %collective-permute-start.14 = (bf16[136,896]{1,0:T(8,128)(2,1)S(1)}, bf16[136,896]{1,0:T(8,128)(2,1)}, u32[]{:S(2)}, u32[]{:S(2)}) collective-permute-start(bf16[136,896]{1,0:T(8,128)(2,1)S(1)} %collective-permute-done.7.refs_11_), channel_id=1, source_target_pairs={{0,1},{1,0},{2,3},{3,2},{4,5},{5,4},{6,7},{7,6},{8,9},{9,8},{10,11... | collective-permute-start | bytes 731144 | tf_op jit(solution)/shard_map/ppermute | solution.py:291
  78.5 2.0 %copy-start.10 = (bf16[136,896]{1,0:T(8,128)(2,1)}, bf16[136,896]{1,0:T(8,128)(2,1)S(1)}, u32[]{:S(2)}) copy-start(bf16[136,896]{1,0:T(8,128)(2,1)S(1)} %collective-permute-done.6.refs_7_) | copy-start | bytes 731140
  78.5 2.0 %collective-permute-start.12 = (bf16[136,896]{1,0:T(8,128)(2,1)S(1)}, bf16[136,896]{1,0:T(8,128)(2,1)}, u32[]{:S(2)}, u32[]{:S(2)}) collective-permute-start(bf16[136,896]{1,0:T(8,128)(2,1)S(1)} %collective-permute-done.6.refs_7_), channel_id=1, source_target_pairs={{0,1},{1,0},{2,3},{3,2},{4,5},{5,4},{6,7},{7,6},{8,9},{9,8},{10,11... | collective-permute-start | bytes 731144 | tf_op jit(solution)/shard_map/ppermute | solution.py:291
  80.5 0.9 copy-start.2

commit v3 on v2

--- a/solution.py
+++ b/solution.py
@@ -12,6 +12,7 @@
 CL = 64
 R = 128
 HR = R // 2
+COST = 1 << 36
 F32 = jnp.float32
 BF16 = jnp.bfloat16
 NT = (((1,), (1,)), ((), ()))
@@ -120,28 +121,69 @@
     )(section, *args)
 
 
+def _ids_kernel(*refs):
+    out_ref = refs[-1]
+    for n, x_ref in enumerate(refs[:-1]):
+        table = x_ref[...].astype(F32).astype(jnp.int32)
+        out_ref[2 * n : 2 * n + 2, :] = table[:2, :]
+
+
+def _ids_call(packs, start, rows):
+    spec = pl.BlockSpec((rows, R), lambda i: (start // rows, 0))
+    return pl.pallas_call(
+        _ids_kernel,
+        grid=(1,),
+        in_specs=[spec] * len(packs),
+        out_specs=pl.BlockSpec((2 * len(packs), R), lambda i: (0, 0)),
+        out_shape=jax.ShapeDtypeStruct((2 * len(packs), R), jnp.int32),
+        cost_estimate=pl.CostEstimate(flops=COST, transcendentals=0, bytes_accessed=1000),
+    )(*packs)
+
+
 def _scatter(got, src, count, peers, spans, first, place_ref, ids_ref, slot_ref, acc_ref):
     inner = peers // 2
     low = lax.broadcasted_iota(jnp.int32, acc_ref.shape[1:], 1) < HR
     turn = jnp.bitwise_xor(src % inner, place_ref[1])
     side = jnp.bitwise_xor(src // inner, place_ref[0])
-    at = ((2 * turn + side) * spans + first) * 2
+    at = (2 * turn + side) * 2
     for c in range(count):
         tile = got[src, :, R * c : R * (c + 1)].astype(F32)
-        left = slot_ref[ids_ref[at + 2 * c]]
-        right = slot_ref[ids_ref[at + 2 * c + 1]]
+        left = slot_ref[ids_ref[at, first + c]]
+        right = slot_ref[ids_ref[at + 1, first + c]]
         acc_ref[left] += jnp.where(low, tile, 0.0)
         acc_ref[right] += jnp.where(low, 0.0, tile)
 
 
-def _weight_kernel(spans, chunks, place_ref, ids_ref, slot_ref, *refs):
-    n_gots = len(chunks)
-    n_xs = len(refs) - 5 - 2 * n_gots
-    got_hbm, x_hbm = refs[:n_gots], refs[n_gots : n_gots + n_xs]
-    out_ref, acc_ref, enc_ref = refs[n_gots + n_xs : n_gots + n_xs + 3]
-    gots = refs[n_gots + n_xs + 3 : 2 * n_gots + n_xs + 3]
-    x_refs, sems = refs[-2], refs[-1]
-    peers = gots[0].shape[0]
+def _add_kernel(count, spans, first, place_ref, ids_ref, slot_ref, got_ref, acc_ref):
+    peers = got_ref.shape[0]
+    acc_ref[...] = jnp.zeros_like(acc_ref)
+
+    def add_peer(src, carry):
+        _scatter(
+            got_ref, src, count, peers, spans, first, place_ref, ids_ref, slot_ref, acc_ref
+        )
+        return carry
+
+    lax.fori_loop(0, peers, add_peer, 0)
+
+
+def _add_call(count, spans, first, place, ids, slots, got):
+    smem = pl.BlockSpec(memory_space=pltpu.SMEM)
+    vmem = pl.BlockSpec(memory_space=pltpu.VMEM)
+    return pl.pallas_call(
+        functools.partial(_add_kernel, count, spans, first),
+        in_specs=[smem] * 3 + [vmem],
+        out_specs=vmem,
+        out_shape=jax.ShapeDtypeStruct((slots.shape[0], got.shape[1], R), F32),
+        compiler_params=pltpu.CompilerParams(vmem_limit_bytes=16 << 20),
+        cost_estimate=pl.CostEstimate(flops=1000, transcendentals=0, bytes_accessed=1000),
+    )(place, ids, slots, got)
+
+
+def _weight_kernel(count, spans, first, place_ref, ids_ref, slot_ref, got_ref, sum_ref, *refs):
+    x_hbm = refs[:-5]
+    out_ref, acc_ref, enc_ref, x_refs, sems = refs[-5:]
+    peers = got_ref.shape[0]
     blocks, cols = acc_ref.shape[:2]
     owned = blocks // peers
     inner = peers // 2
@@ -149,26 +191,21 @@
     share = owned // 2
     rows = share * HR
 
-    got_copies = [pltpu.make_async_copy(got_hbm[n], gots[n], sems.at[n]) for n in range(n_gots)]
     x_copies = []
-    for n in range(n_xs):
+    for n in range(len(x_hbm)):
         to = x_refs.at[n // 2, (n % 2) * rows : (n % 2 + 1) * rows, :]
-        x_copies.append(pltpu.make_async_copy(x_hbm[n].at[:rows, :], to, sems.at[n_gots + n]))
-    for copy in got_copies + x_copies:
+        x_copies.append(pltpu.make_async_copy(x_hbm[n].at[:rows, :], to, sems.at[n]))
+    for copy in x_copies:
         copy.start()
-    acc_ref[...] = jnp.zeros_like(acc_ref)
-    first = 0
-    for n, count in enumerate(chunks):
-        got_copies[n].wait()
-
-        def add_peer(src, carry, n=n, count=count, first=first):
-            _scatter(
-                gots[n], src, count, peers, spans, first, place_ref, ids_ref, slot_ref, acc_ref
-            )
-            return carry
-
-        lax.fori_loop(0, peers, add_peer, 0)
-        first += count
+    acc_ref[...] = sum_ref[...]
+
+    def add_peer(src, carry):
+        _scatter(
+            got_ref, src, count, peers, spans, first, place_ref, ids_ref, slot_ref, acc_ref
+        )
+        return carry
+
+    lax.fori_loop(0, peers, add_peer, 0)
     low = lax.broadcasted_iota(jnp.int32, (cols, R), 1) < HR
     total = None
     for turn in range(inner):
@@ -193,33 +230,30 @@
     out_ref[...] = (total * scale).T
 
 
-def _weight_call(spans, chunks, place, ids, slots, gots, xs):
-    cols = gots[0].shape[1]
+def _weight_call(count, spans, first, place, ids, slots, got, partial_sum, xs):
+    cols = got.shape[1]
     blocks = slots.shape[0]
-    owned = blocks // gots[0].shape[0]
+    owned = blocks // got.shape[0]
     smem = pl.BlockSpec(memory_space=pltpu.SMEM)
-    anywhere = pl.BlockSpec(memory_space=pl.ANY)
-    large = [pltpu.with_memory_space_constraint(x, pltpu.HBM) for x in [*gots, *xs]]
+    vmem = pl.BlockSpec(memory_space=pltpu.VMEM)
+    xs = [pltpu.with_memory_space_constraint(x, pltpu.HBM) for x in xs]
     pairs = len(xs) // 2
     return pl.pallas_call(
-        functools.partial(_weight_kernel, spans, chunks),
-        in_specs=[smem] * 3 + [anywhere] * len(large),
-        out_specs=pl.BlockSpec(memory_space=pltpu.VMEM),
+        functools.partial(_weight_kernel, count, spans, first),
+        in_specs=[smem] * 3 + [vmem] * 2 + [pl.BlockSpec(memory_space=pl.ANY)] * len(xs),
+        out_specs=vmem,
         out_shape=jax.ShapeDtypeStruct((DE, cols), F32),
         scratch_shapes=[
             pltpu.VMEM((blocks, cols, R), F32),
             pltpu.VMEM((pairs, cols, owned * HR), BF16),
-        ]
-        + [pltpu.VMEM(x.shape, BF16) for x in gots]
-        + [
             pltpu.VMEM((pairs, owned * HR, DE), BF16),
-            pltpu.SemaphoreType.DMA((len(large),)),
+            pltpu.SemaphoreType.DMA((len(xs),)),
         ],
-        compiler_params=pltpu.CompilerParams(vmem_limit_bytes=40 << 20),
+        compiler_params=pltpu.CompilerParams(vmem_limit_bytes=32 << 20),
         cost_estimate=pl.CostEstimate(
             flops=2 * cols * blocks * HR * DE, transcendentals=0, bytes_accessed=6000000
         ),
-    )(place, ids, slots, *large)
+    )(place, ids, slots, got, partial_sum, *xs)
 
 
 def per_device(
@@ -242,7 +276,7 @@
     upper, lower = index // inner, index % inner
     swap = [(0, 1), (1, 0)]
 
-    id_rows = jnp.pad(neighbour_ids.astype(BF16), ((0, -spans % 8), (0, DE - 2)))
+    id_rows = jnp.pad(neighbour_ids.T.astype(BF16), ((0, 6), (0, DE - spans)))
     split = enc_input.reshape(2, owned // 2, 2, HR, DE)
     split = lax.dynamic_index_in_dim(split, section, 0, keepdims=False)
     own = lax.dynamic_index_in_dim(split, upper, 1, keepdims=False)
@@ -276,12 +310,15 @@
         )
         if not gots:
             mirror, own, send = lax.optimization_barrier((mirror, own, send))
+        else:
+            mirror, send = lax.optimization_barrier((mirror, send))
         other = lax.ppermute(send, "section", swap)
         if gots:
             gots[-1], other = lax.optimization_barrier((gots[-1], other))
         ref_grad = (mine.astype(F32) + other.astype(F32)).astype(BF16)
         ref_grad = ref_grad.reshape(peers, DE // peers, count * R)
-        held, mirror, ref_grad = lax.optimization_barrier((held, mirror, ref_grad))
+        if not gots:
+            held, ref_grad = lax.optimization_barrier((held, ref_grad))
         gots.append(lax.all_to_all(ref_grad, "dp", 0, 0, tiled=True))
         first += count
 
@@ -289,12 +326,13 @@
     xs = []
     for pair in zip(own, packs):
         xs += list(pair) + [lax.ppermute(x, "section", swap) for x in pair]
-    cut = owned // 2 * HR
-    ids = [x[cut : cut + spans, :2] for pair in zip(own, packs) for x in pair]
-    ids = jnp.concatenate(ids, axis=0).astype(jnp.int32)
+    pairs = [x for pair in zip(own, packs) for x in pair]
+    ids = _ids_call(pairs, owned // 2 * HR, id_rows.shape[0])
     place = jnp.stack([upper, lower, section])
+    ids = pltpu.with_memory_space_constraint(ids, pltpu.HBM)
+    partial_sum = _add_call(chunks[0], spans, 0, place, ids, block_slot, gots[0])
     weight = _weight_call(
-        spans, chunks, place, ids.reshape(-1), block_slot, gots, xs
+        chunks[1], spans, chunks[0], place, ids, block_slot, gots[1], partial_sum, xs
     )
     rows = DE // (2 * peers)
     cols = DE // peers

time: 105 us -> 96.9 us (0.923)
  waiting for transfers between devices: 27.4 us -> 17 us
  starting transfers between devices: 21.4 us -> 24.3 us
  local copies, waits for them, and re-layouts: 4.28 us -> 2.05 us
  Pallas kernels: 30.1 us -> 32 us
    ppermute x6, waiting for transfers between devices: 19.7 us -> 7.62 us  [spread(): lax.ppermute(pack, 'dp', [(i, i ^ m) for i in range(peers)])]
    all_to_all x2, waiting for transfers between devices: 3.42 us -> 7.23 us  [per_device(): gots.append(lax.all_to_all(ref_grad, 'dp', 0, 0, tiled=True))]
    all_to_all x2, starting transfers between devices: 8.52 us -> 10.8 us  [per_device(): gots.append(lax.all_to_all(ref_grad, 'dp', 0, 0, tiled=True))]
    ppermute x2, waiting for transfers between devices: 4.26 us -> 2.14 us  [per_device(): other = lax.ppermute(send, 'section', swap)]
    pallas_call x1 -> x3, Pallas kernels: 4.74 us -> 6.67 us  [the longest x1 3.99 us: _weight_call(): pl.pallas_call(functools.partial(_weight_kernel, count, spans, first), in...]
  transfers between devices with their start and end apart: 19 -> 19, of which waited for: 6 -> 5; matrix products, arithmetic and copies ran while one was open for 1% -> 1% of each run, Pallas kernels for 24% -> 29%
where the time goes in v3:
time: 96.9 us; the launch traced here: 96.4 us
  Pallas kernels  32 us (33%)
  starting transfers between devices  24.3 us (25%)
  blocking collectives  17.3 us (18%)
  waiting for transfers between devices  17 us (18%)
  other arithmetic  2.88 us (3%)
  local copies, waits for them, and re-layouts  2.05 us (2%)
    pallas_call x2, Pallas kernels, _span_call(): pl.pallas_call(functools.partial(_span_kernel, first, spans), grid_spec=p...  25.3 us
    all_to_all x1, blocking collectives, per_device(): lax.all_to_all(weight.reshape(2 * peers, rows, cols), ('dp', 'section'),...  17.3 us
    all_to_all x2, starting transfers between devices, per_device(): gots.append(lax.all_to_all(ref_grad, 'dp', 0, 0, tiled=True))  10.8 us
    ppermute x6, starting transfers between devices, spread(): lax.ppermute(pack, 'dp', [(i, i ^ m) for i in range(peers)])  8.33 us
    ppermute x6, waiting for transfers between devices, spread(): lax.ppermute(pack, 'dp', [(i, i ^ m) for i in range(peers)])  7.62 us
    all_to_all x2, waiting for transfers between devices, per_device(): gots.append(lax.all_to_all(ref_grad, 'dp', 0, 0, tiled=True))  7.23 us
    pallas_call x1, Pallas kernels, _weight_call(): pl.pallas_call(functools.partial(_weight_kernel, count, spans, first), in...  3.99 us
    ppermute x1, starting transfers between devices, per_device(): mirror = lax.ppermute(away, 'dp', [(i, i ^ inner) for i in range(peers)])  2.98 us
  transfers between devices with their start and end apart: 19, of which 5 were waited for; matrix products, arithmetic and copies ran while one was open for 1% of the time, Pallas kernels for 29%

profile of v3, /device:TPU:0, one launch (start us, length us, event | category | flops | bytes accessed | tf_op | source)
XLA Modules:
  0.0 96.4 jit_solution(4865266213697106451)
XLA Ops:
  0.6 0.7 convert_bitcast_fusion
  1.3 1.1 %constant_dynamic-slice_fusion = (bf16[1,2,1,64,896]{4,3,2,1,0:T(8,128)(2,1)S(1)}, bf16[1,2,1,64,896]{4,3,2,1,0:T(8,128)(2,1)S(1)}) fusion(bf16[2,2,2,64,896]{4,3,2,1,0:T(8,128)(2,1)} %bitcast.24, s32[]{:T(128)S(6)} %select_n.29, s32[]{:T(128)S(6)} %select_n.34, s32[]{:T(128)S(6)} %select_n.32), kind=kLoop, calls=%fused_computation.10 | loop fusion | bytes 917516 | tf_op jit(solution)/shard_map/jit(dynamic_index_in_dim)/dynamic_slice | solution.py:282
  2.5 0.0 copy-start.1
  2.5 3.0 %collective-permute-start.1 = (bf16[136,896]{1,0:T(8,128)(2,1)S(1)}, bf16[136,896]{1,0:T(8,128)(2,1)S(1)}, u32[]{:S(2)}, u32[]{:S(2)}) collective-permute-start(bf16[136,896]{1,0:T(8,128)(2,1)S(1)} %get-tuple-element.26.refs_0_), channel_id=1, source_target_pairs={{0,2},{2,0},{4,6},{6,4},{8,10},{10,8},{12,14},{14,12},{1,3},{3,1},... | collective-permute-start | bytes 731144 | tf_op jit(solution)/shard_map/ppermute | solution.py:290
  5.5 1.6 %collective-permute-start.2 = (bf16[136,896]{1,0:T(8,128)(2,1)S(1)}, bf16[136,896]{1,0:T(8,128)(2,1)S(1)}, u32[]{:S(2)}, u32[]{:S(2)}) collective-permute-start(bf16[136,896]{1,0:T(8,128)(2,1)S(1)} %get-tuple-element.26.refs_0_), channel_id=1, source_target_pairs={{0,4},{2,6},{4,0},{6,2},{8,12},{10,14},{12,8},{14,10},{1,5},{3,7},... | collective-permute-start | bytes 731144 | tf_op jit(solution)/shard_map/ppermute | solution.py:290
  7.1 0.0 collective-permute-start.3
  7.1 3.0 %collective-permute-start = (bf16[136,896]{1,0:T(8,128)(2,1)S(1)}, bf16[136,896]{1,0:T(8,128)(2,1)}, u32[]{:S(2)}, u32[]{:S(2)}) collective-permute-start(bf16[136,896]{1,0:T(8,128)(2,1)S(1)} %get-tuple-element.41), channel_id=1, source_target_pairs={{0,8},{2,10},{4,12},{6,14},{8,0},{10,2},{12,4},{14,6},{1,9},{3,11}... | collective-permute-start | bytes 731144 | tf_op jit(solution)/shard_map/ppermute | solution.py:286
  10.1 12.7 %shard_map.104 = (bf16[384,1024]{1,0:T(8,128)(2,1)}, bf16[2,448,384]{2,1,0:T(8,128)(2,1)S(1)}, bf16[2,448,384]{2,1,0:T(8,128)(2,1)S(1)}) custom-call(s32[1]{0:T(128)} %bitcast.sec_ref, bf16[384,1024]{1,0:T(8,128)(2,1)} %q_ref.3, bf16[384,1024]{1,0:T(8,128)(2,1)} %g_ref.3, f32[8,384]{1,0:T(8,128)} %l_ref.3, bf16[6,256,896]{2,1,0:T(8,128)(2,1)} %n_ref.3, ...), custom_call_target="tpu_custom_call" | custom-call | flops 6140461056 | bytes 6670016 | tf_op jit(solution)/shard_map/pallas_call | solution.py:101
  22.7 0.0 collective-permute-done.refs_1_
  22.8 0.0 collective-permute-done.1.refs_2_.refs_4_
  22.8 0.0 copy-start.2
  22.8 0.0 collective-permute-done.2.refs_4_.refs_8_
  22.8 0.0 copy-start.3
  22.8 0.3 collective-permute-done.3.refs_6_.refs_12_
  23.1 0.0 copy-start.4
  23.1 0.0 collective-permute-start.4
  23.1 2.1 %collective-permute-done.4 = bf16[2,448,384]{2,1,0:T(8,128)(2,1)S(1)} collective-permute-done((bf16[2,448,384]{2,1,0:T(8,128)(2,1)S(1)}, bf16[2,448,384]{2,1,0:T(8,128)(2,1)S(1)}, u32[]{:S(2)}, u32[]{:S(2)}) %collective-permute-start.4) | collective-permute-done | bytes 688160 | tf_op jit(solution)/shard_map/ppermute | solution.py:315
  25.3 1.0 %add_convert_fusion.1 = bf16[2,448,384]{2,1,0:T(8,128)(2,1)} fusion(bf16[2,448,384]{2,1,0:T(8,128)(2,1)S(1)} %collective-permute-done.4, bf16[2,448,384]{2,1,0:T(8,128)(2,1)S(1)} %get-tuple-element.21), kind=kLoop, calls=%fused_computation.1 | loop fusion | flops 1376256 | bytes 2064384 | tf_op jit(solution)/shard_map/convert_element_type | solution.py:318
  26.3 0.0 copy-done.3
  26.3 0.0 copy-done.4
  26.3 6.0 %all-to-all-start = ((bf16[8,112,384]{2,1,0:T(8,128)(2,1)}), bf16[8,112,384]{2,1,0:T(8,128)(2,1)S(1)}, u32[]{:S(2)}, u32[]{:S(2)}) async-start(bf16[8,112,384]{2,1,0:T(8,128)(2,1)} %bitcast.5), calls=%async_computation | async-start | bytes 1376256 | tf_op jit(solution)/shard_map/all_to_all | solution.py:322
  32.3 12.7 %shard_map.105 = (bf16[384,1024]{1,0:T(8,128)(2,1)}, bf16[2,448,384]{2,1,0:T(8,128)(2,1)S(1)}, bf16[2,448,384]{2,1,0:T(8,128)(2,1)S(1)}) custom-call(s32[1]{0:T(128)} %bitcast.sec_ref, bf16[384,1024]{1,0:T(8,128)(2,1)} %q_ref.3, bf16[384,1024]{1,0:T(8,128)(2,1)} %g_ref.3, f32[8,384]{1,0:T(8,128)} %l_ref.3, ...), custom_call_target="tpu_custom_call", output_to_operand_aliasing={{0}: (7, {})} | custom-call | flops 6140461056 | bytes 6670016 | tf_op jit(solution)/shard_map/pallas_call | solution.py:101
  45.0 0.1 collective-permute-start.8
  45.1 0.0 copy-done.1
  45.1 0.5 collective-permute-start.9
  45.6 0.1 pad_add_fusion.place_ref
  45.6 0.0 copy-done.2
  45.6 0.1 collective-permute-start.11
  45.7 0.4 collective-permute-start.13
  46.1 2.0 %collective-permute-start.5 = (bf16[136,896]{1,0:T(8,128)(2,1)}, bf16[136,896]{1,0:T(8,128)(2,1)}, u32[]{:S(2)}, u32[]{:S(2)}) collective-permute-start(bf16[136,896]{1,0:T(8,128)(2,1)} %collective-permute-done.refs_1_), channel_id=1, source_target_pairs={{0,2},{2,0},{4,6},{6,4},{8,10},{10,8},{12,14},{14,12},{1,3},{3,1},... | collective-permute-start | bytes 731144 | tf_op jit(solution)/shard_map/ppermute | solution.py:290
  48.2 0.0 collective-permute-done.8
  48.2 1.5 %collective-permute-start.6 = (bf16[136,896]{1,0:T(8,128)(2,1)}, bf16[136,896]{1,0:T(8,128)(2,1)}, u32[]{:S(2)}, u32[]{:S(2)}) collective-permute-start(bf16[136,896]{1,0:T(8,128)(2,1)} %collective-permute-done.refs_1_), channel_id=1, source_target_pairs={{0,4},{2,6},{4,0},{6,2},{8,12},{10,14},{12,8},{14,10},{1,5},{3,7},... | collective-permute-start | bytes 731144 | tf_op jit(solution)/shard_map/ppermute | solution.py:290
  49.6 1.0 all-to-all-done.got_ref
  50.6 0.0 collective-permute-done.9.refs_2_
  50.6 0.2 collective-permute-start.7
  50.8 0.0 copy-start.5
  50.8 1.0 %add_convert_fusion = bf16[2,448,384]{2,1,0:T(8,128)(2,1)} fusion(bf16[2,448,384]{2,1,0:T(8,128)(2,1)S(1)} %collective-permute-done.8, bf16[2,448,384]{2,1,0:T(8,128)(2,1)S(1)} %get-tuple-element.33), kind=kLoop, calls=%fused_computation | loop fusion | flops 1376256 | bytes 2064384 | tf_op jit(solution)/shard_map/convert_element_type | solution.py:318
  51.9 4.8 %all-to-all-start.1 = ((bf16[8,112,384]{2,1,0:T(8,128)(2,1)}), bf16[8,112,384]{2,1,0:T(8,128)(2,1)S(1)}, u32[]{:S(2)}, u32[]{:S(2)}) async-start(bf16[8,112,384]{2,1,0:T(8,128)(2,1)} %bitcast.8), calls=%async_computation.1 | async-start | bytes 1376256 | tf_op jit(solution)/shard_map/all_to_all | solution.py:322
  56.7 0.0 copy-start
  56.7 0.0 collective-permute-done.11.refs_6_
  56.7 0.0 copy-done.5
  56.7 0.1 collective-permute-start.15
  56.8 0.0 collective-permute-done.13.refs_10_
  56.8 0.5 collective-permute-start.10
  57.3 0.0 collective-permute-done.5.refs_3_.refs_5_
  57.3 0.1 collective-permute-start.12
  57.4 0.0 collective-permute-done.6.refs_5_.refs_9_
  57.4 0.4 collective-permute-start.14
  57.8 7.3 %collective-permute-done.7.refs_7_.refs_13_ = bf16[136,896]{1,0:T(8,128)(2,1)} collective-permute-done((bf16[136,896]{1,0:T(8,128)(2,1)}, bf16[136,896]{1,0:T(8,128)(2,1)}, u32[]{:S(2)}, u32[]{:S(2)}) %collective-permute-start.7) | collective-permute-done | bytes 243744 | tf_op jit(solution)/shard_map/ppermute | solution.py:290
  65.1 0.0 collective-permute-start.16
  65.1 1.3 %shard_map.106.ids_ref = s32[16,128]{1,0:T(8,128)} custom-call(bf16[136,896]{1,0:T(8,128)(2,1)} %copy-done.1, bf16[136,896]{1,0:T(8,128)(2,1)} %collective-permute-done.refs_1_, bf16[136,896]{1,0:T(8,128)(2,1)} %copy-done.2, bf16[136,896]{1,0:T(8,128)(2,1)} %collective-permute-done.5.refs_3_.refs_5_, bf16[136,896]{1,0:T(8,128)(2,1)} %copy-done.3, ...), custom_call_target="tpu_custom_call" | custom-call | flops 68719476736 | bytes 1000 | tf_op jit(solution)/shard_map/pallas_call | solution.py:133
  66.4 0.0 copy-done
  66.4 1.4 %shard_map.107.sum_ref = f32[32,112,128]{2,1,0:T(8,128)S(1)} custom-call(s32[3]{0:T(128)S(1)} %pad_add_fusion.place_ref, s32[16,128]{1,0:T(8,128)} %shard_map.106.ids_ref, s32[32]{0:T(128)S(1)} %copy-done, bf16[8,112,384]{2,1,0:T(8,128)(2,1)S(1)} %all-to-all-done.got_ref), custom_call_target="tpu_custom_call" | custom-call | flops 1000 | bytes 1000 | tf_op jit(solution)/shard_map/pallas_call | solution.py:173
  67.8 0.0 collective-permute-done.15.refs_14_
  67.8 0.0 collective-permute-done.10.refs_3_
  67.8 0.0 collective-permute-done.12.refs_7_
  67.8 0.0 collective-permute-done.14.refs_11_
  67.8 0.0 collective-permute-done.16.refs_15_
  67.8 6.3 %all-to-all-done.1.got_ref = bf16[8,112,384]{2,1,0:T(8,128)(2,1)S(1)} async-done(((bf16[8,112,384]{2,1,0:T(8,128)(2,1)}), bf16[8,112,384]{2,1,0:T(8,128)(2,1)S(1)}, u32[]{:S(2)}, u32[]{:S(2)}) %all-to-all-start.1) | async-done | bytes 688160 | tf_op jit(solution)/shard_map/all_to_all | solution.py:322
  74.1 4.0 %shard_map.108 = f32[896,112]{1,0:T(8,128)S(1)} custom-call(s32[3]{0:T(128)S(1)} %pad_add_fusion.place_ref, s32[16,128]{1,0:T(8,128)} %shard_map.106.ids_ref, s32[32]{0:T(128)S(1)} %copy-done, bf16[8,112,384]{2,1,0:T(8,128)(2,1)S(1)} %all-to-all-done.1.got_ref, f32[32,112,128]{2,1,0:T(8,128)S(1)} %shard_map.107.sum_ref, bf16[136,896]{1,0:T(8,128)(2,1)} %copy-done.1, ...), custom_call_target="tpu_custom_call" | custom-call | flops 411041792 | bytes 6000000 | tf_op jit(solution)/shard_map/pallas_call | solution.py:241
  78.1 17.3 %all_to_all.15 = f32[16,56,112]{2,1,0:T(8,128)S(1)} all-to-all(f32[16,56,112]{2,1,0:T(8,128)S(1)} %bitcast.19), channel_id=1, replica_groups=mesh['group'=2,'dp'=8,'section'=2] {'dp','section'}, dimensions={0} | all-to-all | bytes 802816 | tf_op jit(solution)/shard_map/all_to_all | solution.py:339
  95.4 0.1 copy.18
  95.5 0.9 reshape.43
  (2 shorter events, 0.1 us)
Async XLA Ops:
  2.5 42.6 %copy-start.1 = (bf16[136,896]{1,0:T(8,128)(2,1)}, bf16[136,896]{1,0:T(8,128)(2,1)S(1)}, u32[]{:S(2)}) copy-start(bf16[136,896]{1,0:T(8,128)(2,1)S(1)} %get-tuple-element.26.refs_0_) | copy-start | bytes 731140
  2.5 20.3 %collective-permute-start.1 = (bf16[136,896]{1,0:T(8,128)(2,1)S(1)}, bf16[136,896]{1,0:T(8,128)(2,1)S(1)}, u32[]{:S(2)}, u32[]{:S(2)}) collective-permute-start(bf16[136,896]{1,0:T(8,128)(2,1)S(1)} %get-tuple-element.26.refs_0_), channel_id=1, source_target_pairs={{0,2},{2,0},{4,6},{6,4},{8,10},{10,8},{12,14},{14,12},{1,3},{3,1},... | collective-permute-start | bytes 731144 | tf_op jit(solution)/shard_map/ppermute | solution.py:290
  5.5 17.3 %collective-permute-start.2 = (bf16[136,896]{1,0:T(8,128)(2,1)S(1)}, bf16[136,896]{1,0:T(8,128)(2,1)S(1)}, u32[]{:S(2)}, u32[]{:S(2)}) collective-permute-start(bf16[136,896]{1,0:T(8,128)(2,1)S(1)} %get-tuple-element.26.refs_0_), channel_id=1, source_target_pairs={{0,4},{2,6},{4,0},{6,2},{8,12},{10,14},{12,8},{14,10},{1,5},{3,7},... | collective-permute-start | bytes 731144 | tf_op jit(solution)/shard_map/ppermute | solution.py:290
  7.1 16.0 %collective-permute-start.3 = (bf16[136,896]{1,0:T(8,128)(2,1)S(1)}, bf16[136,896]{1,0:T(8,128)(2,1)S(1)}, u32[]{:S(2)}, u32[]{:S(2)}) collective-permute-start(bf16[136,896]{1,0:T(8,128)(2,1)S(1)} %get-tuple-element.26.refs_0_), channel_id=1, source_target_pairs={{0,6},{2,4},{4,2},{6,0},{8,14},{10,12},{12,10},{14,8},{1,7},{3,5},... | collective-permute-start | bytes 731144 | tf_op jit(solution)/shard_map/ppermute | solution.py:290
  7.1 15.7 %collective-permute-start = (bf16[136,896]{1,0:T(8,128)(2,1)S(1)}, bf16[136,896]{1,0:T(8,128)(2,1)}, u32[]{:S(2)}, u32[]{:S(2)}) collective-permute-start(bf16[136,896]{1,0:T(8,128)(2,1)S(1)} %get-tuple-element.41), channel_id=1, source_target_pairs={{0,8},{2,10},{4,12},{6,14},{8,0},{10,2},{12,4},{14,6},{1,9},{3,11}... | collective-permute-start | bytes 731144 | tf_op jit(solution)/shard_map/ppermute | solution.py:286
  22.8 22.9 %copy-start.2 = (bf16[136,896]{1,0:T(8,128)(2,1)}, bf16[136,896]{1,0:T(8,128)(2,1)S(1)}, u32[]{:S(2)}) copy-start(bf16[136,896]{1,0:T(8,128)(2,1)S(1)} %collective-permute-done.1.refs_2_.refs_4_) | copy-start | bytes 731140
  22.8 3.5 %copy-start.3 = (bf16[136,896]{1,0:T(8,128)(2,1)}, bf16[136,896]{1,0:T(8,128)(2,1)S(1)}, u32[]{:S(2)}) copy-start(bf16[136,896]{1,0:T(8,128)(2,1)S(1)} %collective-permute-done.2.refs_4_.refs_8_) | copy-start | bytes 731140
  23.1 3.2 %copy-start.4 = (bf16[136,896]{1,0:T(8,128)(2,1)}, bf16[136,896]{1,0:T(8,128)(2,1)S(1)}, u32[]{:S(2)}) copy-start(bf16[136,896]{1,0:T(8,128)(2,1)S(1)} %collective-permute-done.3.refs_6_.refs_12_) | copy-start | bytes 731140
  23.1 2.1 %collective-permute-start.4 = (bf16[2,448,384]{2,1,0:T(8,128)(2,1)S(1)}, bf16[2,448,384]{2,1,0:T(8,128)(2,1)S(1)}, u32[]{:S(2)}, u32[]{:S(2)}) collective-permute-start(bf16[2,448,384]{2,1,0:T(8,128)(2,1)S(1)} %get-tuple-element.23), channel_id=1, source_target_pairs={{0,1},{1,0},{2,3},{3,2},{4,5},{5,4},{6,7},{7,6},{8,9},{9,8},{10,11... | collective-permute-start | bytes 2064392 | tf_op jit(solution)/shard_map/ppermute | solution.py:315
  26.3 24.3 %all-to-all-start = ((bf16[8,112,384]{2,1,0:T(8,128)(2,1)}), bf16[8,112,384]{2,1,0:T(8,128)(2,1)S(1)}, u32[]{:S(2)}, u32[]{:S(2)}) async-start(bf16[8,112,384]{2,1,0:T(8,128)(2,1)} %bitcast.5), calls=%async_computation | async-start | bytes 1376256 | tf_op jit(solution)/shard_map/all_to_all | solution.py:322
  45.0 3.2 %collective-permute-start.8 = (bf16[2,448,384]{2,1,0:T(8,128)(2,1)S(1)}, bf16[2,448,384]{2,1,0:T(8,128)(2,1)S(1)}, u32[]{:S(2)}, u32[]{:S(2)}) collective-permute-start(bf16[2,448,384]{2,1,0:T(8,128)(2,1)S(1)} %get-tuple-element.35), channel_id=1, source_target_pairs={{0,1},{1,0},{2,3},{3,2},{4,5},{5,4},{6,7},{7,6},{8,9},{9,8},{10,11... | collective-permute-start | bytes 2064392 | tf_op jit(solution)/shard_map/ppermute | solution.py:315
  45.1 5.5 %collective-permute-start.9 = (bf16[136,896]{1,0:T(8,128)(2,1)S(1)}, bf16[136,896]{1,0:T(8,128)(2,1)}, u32[]{:S(2)}, u32[]{:S(2)}) collective-permute-start(bf16[136,896]{1,0:T(8,128)(2,1)S(1)} %get-tuple-element.26.refs_0_), channel_id=1, source_target_pairs={{0,1},{1,0},{2,3},{3,2},{4,5},{5,4},{6,7},{7,6},{8,9},{9,8},{10,11... | collective-permute-start | bytes 731144 | tf_op jit(solution)/shard_map/ppermute | solution.py:328
  45.6 11.0 %collective-permute-start.11 = (bf16[136,896]{1,0:T(8,128)(2,1)S(1)}, bf16[136,896]{1,0:T(8,128)(2,1)}, u32[]{:S(2)}, u32[]{:S(2)}) collective-permute-start(bf16[136,896]{1,0:T(8,128)(2,1)S(1)} %collective-permute-done.1.refs_2_.refs_4_), channel_id=1, source_target_pairs={{0,1},{1,0},{2,3},{3,2},{4,5},{5,4},{6,7},{7,6},{8,9},{9,8},{10,11... | collective-permute-start | bytes 731144 | tf_op jit(solution)/shard_map/ppermute | solution.py:328
  45.7 11.1 %collective-permute-start.13 = (bf16[136,896]{1,0:T(8,128)(2,1)}, bf16[136,896]{1,0:T(8,128)(2,1)}, u32[]{:S(2)}, u32[]{:S(2)}) collective-permute-start(bf16[136,896]{1,0:T(8,128)(2,1)} %copy-done.3), channel_id=1, source_target_pairs={{0,1},{1,0},{2,3},{3,2},{4,5},{5,4},{6,7},{7,6},{8,9},{9,8},{10,11... | collective-permute-start | bytes 731144 | tf_op jit(solution)/shard_map/ppermute | solution.py:328
  46.1 11.1 %collective-permute-start.5 = (bf16[136,896]{1,0:T(8,128)(2,1)}, bf16[136,896]{1,0:T(8,128)(2,1)}, u32[]{:S(2)}, u32[]{:S(2)}) collective-permute-start(bf16[136,896]{1,0:T(8,128)(2,1)} %collective-permute-done.refs_1_), channel_id=1, source_target_pairs={{0,2},{2,0},{4,6},{6,4},{8,10},{10,8},{12,14},{14,12},{1,3},{3,1},... | collective-permute-start | bytes 731144 | tf_op jit(solution)/shard_map/ppermute | solution.py:290
  48.2 9.2 %collective-permute-start.6 = (bf16[136,896]{1,0:T(8,128)(2,1)}, bf16[136,896]{1,0:T(8,128)(2,1)}, u32[]{:S(2)}, u32[]{:S(2)}) collective-permute-start(bf16[136,896]{1,0:T(8,128)(2,1)} %collective-permute-done.refs_1_), channel_id=1, source_target_pairs={{0,4},{2,6},{4,0},{6,2},{8,12},{10,14},{12,8},{14,10},{1,5},{3,7},... | collective-permute-start | bytes 731144 | tf_op jit(solution)/shard_map/ppermute | solution.py:290
  50.6 14.5 %collective-permute-start.7 = (bf16[136,896]{1,0:T(8,128)(2,1)}, bf16[136,896]{1,0:T(8,128)(2,1)}, u32[]{:S(2)}, u32[]{:S(2)}) collective-permute-start(bf16[136,896]{1,0:T(8,128)(2,1)} %collective-permute-done.refs_1_), channel_id=1, source_target_pairs={{0,6},{2,4},{4,2},{6,0},{8,14},{10,12},{12,10},{14,8},{1,7},{3,5},... | collective-permute-start | bytes 731144 | tf_op jit(solution)/shard_map/ppermute | solution.py:290
  50.8 5.8 %copy-start.5 = (bf16[136,896]{1,0:T(8,128)(2,1)S(1)}, bf16[136,896]{1,0:T(8,128)(2,1)}, u32[]{:S(2)}) copy-start(bf16[136,896]{1,0:T(8,128)(2,1)} %copy-done.4) | copy-start | bytes 731140
  51.9 22.2 %all-to-all-start.1 = ((bf16[8,112,384]{2,1,0:T(8,128)(2,1)}), bf16[8,112,384]{2,1,0:T(8,128)(2,1)S(1)}, u32[]{:S(2)}, u32[]{:S(2)}) async-start(bf16[8,112,384]{2,1,0:T(8,128)(2,1)} %bitcast.8), calls=%async_computation.1 | async-start | bytes 1376256 | tf_op jit(solution)/shard_map/all_to_all | solution.py:322
  56.7 9.7 %copy-start = (s32[32]{0:T(128)S(1)}, s32[32]{0:T(128)}, u32[]{:S(2)}) copy-start(s32[32]{0:T(128)} %slot_ref.3) | copy-start | bytes 388
  56.7 11.1 %collective-permute-start.15 = (bf16[136,896]{1,0:T(8,128)(2,1)S(1)}, bf16[136,896]{1,0:T(8,128)(2,1)}, u32[]{:S(2)}, u32[]{:S(2)}) collective-permute-start(bf16[136,896]{1,0:T(8,128)(2,1)S(1)} %copy-done.5), channel_id=1, source_target_pairs={{0,1},{1,0},{2,3},{3,2},{4,5},{5,4},{6,7},{7,6},{8,9},{9,8},{10,11... | collective-permute-start | bytes 731144 | tf_op jit(solution)/shard_map/ppermute | solution.py:328
  56.8 11.0 %collective-permute-start.10 = (bf16[136,896]{1,0:T(8,128)(2,1)}, bf16[136,896]{1,0:T(8,128)(2,1)}, u32[]{:S(2)}, u32[]{:S(2)}) collective-permute-start(bf16[136,896]{1,0:T(8,128)(2,1)} %collective-permute-done.refs_1_), channel_id=1, source_target_pairs={{0,1},{1,0},{2,3},{3,2},{4,5},{5,4},{6,7},{7,6},{8,9},{9,8},{10,11... | collective-permute-start | bytes 731144 | tf_op jit(solution)/shard_map/ppermute | solution.py:328
  57.3 10.5 %collective-permute-start.12 = (bf16[136,896]{1,0:T(8,128)(2,1)}, bf16[136,896]{1,0:T(8,128)(2,1)}, u32[]{:S(2)}, u32[]{:S(2)}) collective-permute-start(bf16[136,896]{1,0:T(8,128)(2,1)} %collective-permute-done.5.refs_3_.refs_5_), channel_id=1, source_target_pairs={{0,1},{1,0},{2,3},{3,2},{4,5},{5,4},{6,7},{7,6},{8,9},{9,8},{10,11... | collective-permute-start | bytes 731144 | tf_op jit(solution)/shard_map/ppermute | solution.py:328
  57.4 10.4 %collective-permute-start.14 = (bf16[136,896]{1,0:T(8,128)(2,1)}, bf16[136,896]{1,0:T(8,128)(2,1)}, u32[]{:S(2)}, u32[]{:S(2)}) collective-permute-start(bf16[136,896]{1,0:T(8,128)(2,1)} %collective-permute-done.6.refs_5_.refs_9_), channel_id=1, source_target_pairs={{0,1},{1,0},{2,3},{3,2},{4,5},{5,4},{6,7},{7,6},{8,9},{9,8},{10,11... | collective-permute-start | bytes 731144 | tf_op jit(solution)/shard_map/ppermute | solution.py:328
  65.1 2.7 %collective-permute-start.16 = (bf16[136,896]{1,0:T(8,128)(2,1)}, bf16[136,896]{1,0:T(8,128)(2,1)}, u32[]{:S(2)}, u32[]{:S(2)}) collective-permute-start(bf16[136,896]{1,0:T(8,128)(2,1)} %collective-permute-done.7.refs_7_.refs_13_), channel_id=1, source_target_pairs={{0,1},{1,0},{2,3},{3,2},{4,5},{5,4},{6,7},{7,6},{8,9},{9,8},{10,11... | collective-permute-start | bytes 731144 | tf_op jit(solution)/shard_map/ppermute | solution.py:328

commit v4 on v3

--- a/solution.py
+++ b/solution.py
@@ -276,21 +276,6 @@
     upper, lower = index // inner, index % inner
     swap = [(0, 1), (1, 0)]
 
-    id_rows = jnp.pad(neighbour_ids.T.astype(BF16), ((0, 6), (0, DE - spans)))
-    split = enc_input.reshape(2, owned // 2, 2, HR, DE)
-    split = lax.dynamic_index_in_dim(split, section, 0, keepdims=False)
-    own = lax.dynamic_index_in_dim(split, upper, 1, keepdims=False)
-    own = jnp.concatenate([own.reshape(owned // 2 * HR, DE), id_rows], axis=0)
-    away = lax.dynamic_index_in_dim(split, 1 - upper, 1, keepdims=False)
-    away = jnp.concatenate([away.reshape(owned // 2 * HR, DE), id_rows], axis=0)
-    mirror = lax.ppermute(away, "dp", [(i, i ^ inner) for i in range(peers)])
-
-    def spread(pack):
-        return [pack] + [
-            lax.ppermute(pack, "dp", [(i, i ^ m) for i in range(peers)]) for m in range(1, inner)
-        ]
-
-    own = spread(own)
     held = None
     gots = []
     first = 0
@@ -308,10 +293,25 @@
             value_weight,
             held,
         )
+        if gots:
+            mirror, own, send = lax.optimization_barrier((mirror, own, send))
         if not gots:
-            mirror, own, send = lax.optimization_barrier((mirror, own, send))
-        else:
-            mirror, send = lax.optimization_barrier((mirror, send))
+            enc_input, send = lax.optimization_barrier((enc_input, send))
+            id_rows = jnp.pad(neighbour_ids.T.astype(BF16), ((0, 6), (0, DE - spans)))
+            split = enc_input.reshape(2, owned // 2, 2, HR, DE)
+            split = lax.dynamic_index_in_dim(split, section, 0, keepdims=False)
+            own = lax.dynamic_index_in_dim(split, upper, 1, keepdims=False)
+            own = jnp.concatenate([own.reshape(owned // 2 * HR, DE), id_rows], axis=0)
+            away = lax.dynamic_index_in_dim(split, 1 - upper, 1, keepdims=False)
+            away = jnp.concatenate([away.reshape(owned // 2 * HR, DE), id_rows], axis=0)
+            mirror = lax.ppermute(away, "dp", [(i, i ^ inner) for i in range(peers)])
+
+            def spread(pack):
+                return [pack] + [
+                    lax.ppermute(pack, "dp", [(i, i ^ m) for i in range(peers)]) for m in range(1, inner)
+                ]
+
+            own = spread(own)
         other = lax.ppermute(send, "section", swap)
         if gots:
             gots[-1], other = lax.optimization_barrier((gots[-1], other))
@@ -323,11 +323,12 @@
         first += count
 
     packs = spread(mirror)
+    packs = [x for pair in zip(own, packs) for x in pair]
+    ids = _ids_call(packs, owned // 2 * HR, id_rows.shape[0])
+    ids, packs = lax.optimization_barrier((ids, packs))
     xs = []
-    for pair in zip(own, packs):
-        xs += list(pair) + [lax.ppermute(x, "section", swap) for x in pair]
-    pairs = [x for pair in zip(own, packs) for x in pair]
-    ids = _ids_call(pairs, owned // 2 * HR, id_rows.shape[0])
+    for n in range(0, len(packs), 2):
+        xs += packs[n : n + 2] + [lax.ppermute(x, "section", swap) for x in packs[n : n + 2]]
     place = jnp.stack([upper, lower, section])
     ids = pltpu.with_memory_space_constraint(ids, pltpu.HBM)
     partial_sum = _add_call(chunks[0], spans, 0, place, ids, block_slot, gots[0])

time: 96.9 us -> 92.7 us (0.957)
  waiting for transfers between devices: 17 us -> 15.1 us
  starting transfers between devices: 24.3 us -> 22.5 us
    ppermute x6, waiting for transfers between devices: 7.62 us -> 4.43 us  [spread(): lax.ppermute(pack, 'dp', [(i, i ^ m) for i in range(peers)])]
    all_to_all x2, waiting for transfers between devices: 7.23 us -> 9.47 us  [per_device(): gots.append(lax.all_to_all(ref_grad, 'dp', 0, 0, tiled=True))]
    ppermute x2, waiting for transfers between devices: 2.14 us -> 0.01 us  [per_device(): other = lax.ppermute(send, 'section', swap)]
    all_to_all x2, starting transfers between devices: 10.8 us -> 9.56 us  [per_device(): gots.append(lax.all_to_all(ref_grad, 'dp', 0, 0, tiled=True))]
    ppermute x8, waiting for transfers between devices: 0.02 us -> 1.17 us  [per_device(): lax.ppermute(x, 'section', swap)]
    dynamic_slice x1, local copies, waits for them, and re-layouts: 1.09 us -> 0.04 us  [per_device(): own = lax.dynamic_index_in_dim(split, upper, 1, keepdims=False)]
  transfers between devices with their start and end apart: 19 -> 19, of which waited for: 5 -> 6; matrix products, arithmetic and copies ran while one was open for 1% -> 2% of each run, Pallas kernels for 29% -> 17%
where the time goes in v4:
time: 92.7 us; the launch traced here: 92.3 us
  Pallas kernels  32.1 us (35%)
  starting transfers between devices  22.5 us (24%)
  blocking collectives  18 us (19%)
  waiting for transfers between devices  15.1 us (16%)
  other arithmetic  2.2 us (2%)
  local copies, waits for them, and re-layouts  1.57 us (2%)
    pallas_call x2, Pallas kernels, _span_call(): pl.pallas_call(functools.partial(_span_kernel, first, spans), grid_spec=p...  25.4 us
    all_to_all x1, blocking collectives, per_device(): lax.all_to_all(weight.reshape(2 * peers, rows, cols), ('dp', 'section'),...  18 us
    all_to_all x2, starting transfers between devices, per_device(): gots.append(lax.all_to_all(ref_grad, 'dp', 0, 0, tiled=True))  9.56 us
    all_to_all x2, waiting for transfers between devices, per_device(): gots.append(lax.all_to_all(ref_grad, 'dp', 0, 0, tiled=True))  9.47 us
    ppermute x6, starting transfers between devices, spread(): lax.ppermute(pack, 'dp', [(i, i ^ m) for i in range(peers)])  7.87 us
    ppermute x6, waiting for transfers between devices, spread(): lax.ppermute(pack, 'dp', [(i, i ^ m) for i in range(peers)])  4.43 us
    pallas_call x1, Pallas kernels, _weight_call(): pl.pallas_call(functools.partial(_weight_kernel, count, spans, first), in...  3.99 us
    ppermute x1, starting transfers between devices, per_device(): mirror = lax.ppermute(away, 'dp', [(i, i ^ inner) for i in range(peers)])  2.97 us
  transfers between devices with their start and end apart: 19, of which 6 were waited for; matrix products, arithmetic and copies ran while one was open for 2% of the time, Pallas kernels for 17%

profile of v4, /device:TPU:0, one launch (start us, length us, event | category | flops | bytes accessed | tf_op | source)
XLA Modules:
  0.0 92.3 jit_solution(12120343356136437943)
XLA Ops:
  0.6 0.0 copy-start.9
  0.6 0.0 copy-start.10
  0.7 12.7 %shard_map.104 = (bf16[384,1024]{1,0:T(8,128)(2,1)}, bf16[2,448,384]{2,1,0:T(8,128)(2,1)S(1)}, bf16[2,448,384]{2,1,0:T(8,128)(2,1)S(1)}) custom-call(s32[1]{0:T(128)} %bitcast.sec_ref, bf16[384,1024]{1,0:T(8,128)(2,1)} %q_ref.3, bf16[384,1024]{1,0:T(8,128)(2,1)} %g_ref.3, f32[8,384]{1,0:T(8,128)} %l_ref.3, bf16[6,256,896]{2,1,0:T(8,128)(2,1)} %n_ref.3, ...), custom_call_target="tpu_custom_call" | custom-call | flops 6140461056 | bytes 6670016 | tf_op jit(solution)/shard_map/pallas_call | solution.py:101
  13.4 0.5 collective-permute-start
  13.9 0.0 copy-done.9
  14.0 0.0 copy-done.10
  14.0 0.0 copy-start.1
  14.0 2.7 %collective-permute-start.2 = (bf16[136,896]{1,0:T(8,128)(2,1)S(1)}, bf16[136,896]{1,0:T(8,128)(2,1)S(1)}, u32[]{:S(2)}, u32[]{:S(2)}) collective-permute-start(bf16[136,896]{1,0:T(8,128)(2,1)S(1)} %get-tuple-element.48.refs_0_), channel_id=1, source_target_pairs={{0,2},{2,0},{4,6},{6,4},{8,10},{10,8},{12,14},{14,12},{1,3},{3,1},... | collective-permute-start | bytes 731144 | tf_op jit(solution)/shard_map/ppermute | solution.py:311
  16.7 1.6 %collective-permute-start.3 = (bf16[136,896]{1,0:T(8,128)(2,1)S(1)}, bf16[136,896]{1,0:T(8,128)(2,1)}, u32[]{:S(2)}, u32[]{:S(2)}) collective-permute-start(bf16[136,896]{1,0:T(8,128)(2,1)S(1)} %get-tuple-element.48.refs_0_), channel_id=1, source_target_pairs={{0,4},{2,6},{4,0},{6,2},{8,12},{10,14},{12,8},{14,10},{1,5},{3,7},... | collective-permute-start | bytes 731144 | tf_op jit(solution)/shard_map/ppermute | solution.py:311
  18.3 0.0 collective-permute-start.4
  18.3 3.0 %collective-permute-start.1 = (bf16[136,896]{1,0:T(8,128)(2,1)S(1)}, bf16[136,896]{1,0:T(8,128)(2,1)S(1)}, u32[]{:S(2)}, u32[]{:S(2)}) collective-permute-start(bf16[136,896]{1,0:T(8,128)(2,1)S(1)} %get-tuple-element.59), channel_id=1, source_target_pairs={{0,8},{2,10},{4,12},{6,14},{8,0},{10,2},{12,4},{14,6},{1,9},{3,11}... | collective-permute-start | bytes 731144 | tf_op jit(solution)/shard_map/ppermute | solution.py:307
  21.2 0.0 collective-permute-done
  21.2 1.0 %add_convert_fusion.1 = bf16[2,448,384]{2,1,0:T(8,128)(2,1)} fusion(bf16[2,448,384]{2,1,0:T(8,128)(2,1)S(1)} %collective-permute-done, bf16[2,448,384]{2,1,0:T(8,128)(2,1)S(1)} %get-tuple-element.30), kind=kLoop, calls=%fused_computation.1 | loop fusion | flops 1376256 | bytes 2064384 | tf_op jit(solution)/shard_map/convert_element_type | solution.py:318
  22.3 0.0 copy-done.1
  22.3 3.8 %all-to-all-start = ((bf16[8,112,384]{2,1,0:T(8,128)(2,1)}), bf16[8,112,384]{2,1,0:T(8,128)(2,1)S(1)}, u32[]{:S(2)}, u32[]{:S(2)}) async-start(bf16[8,112,384]{2,1,0:T(8,128)(2,1)} %bitcast.1), calls=%async_computation | async-start | bytes 1376256 | tf_op jit(solution)/shard_map/all_to_all | solution.py:322
  26.1 12.7 %shard_map.105 = (bf16[384,1024]{1,0:T(8,128)(2,1)}, bf16[2,448,384]{2,1,0:T(8,128)(2,1)S(1)}, bf16[2,448,384]{2,1,0:T(8,128)(2,1)S(1)}) custom-call(s32[1]{0:T(128)} %bitcast.sec_ref, bf16[384,1024]{1,0:T(8,128)(2,1)} %q_ref.3, bf16[384,1024]{1,0:T(8,128)(2,1)} %g_ref.3, f32[8,384]{1,0:T(8,128)} %l_ref.3, ...), custom_call_target="tpu_custom_call", output_to_operand_aliasing={{0}: (7, {})} | custom-call | flops 6140461056 | bytes 6670016 | tf_op jit(solution)/shard_map/pallas_call | solution.py:101
  38.8 0.0 collective-permute-done.1.refs_1_
  38.8 0.0 copy-start.5
  38.8 0.0 collective-permute-done.2.refs_2_.refs_4_
  38.8 0.0 copy-start.3
  38.8 0.0 collective-permute-done.3.refs_4_.refs_8_
  38.8 0.0 collective-permute-done.4.refs_6_.refs_12_
  38.8 0.1 collective-permute-start.8
  38.9 2.1 %collective-permute-start.5 = (bf16[136,896]{1,0:T(8,128)(2,1)S(1)}, bf16[136,896]{1,0:T(8,128)(2,1)}, u32[]{:S(2)}, u32[]{:S(2)}) collective-permute-start(bf16[136,896]{1,0:T(8,128)(2,1)S(1)} %collective-permute-done.1.refs_1_), channel_id=1, source_target_pairs={{0,2},{2,0},{4,6},{6,4},{8,10},{10,8},{12,14},{14,12},{1,3},{3,1},... | collective-permute-start | bytes 731144 | tf_op jit(solution)/shard_map/ppermute | solution.py:311
  41.0 1.5 %collective-permute-start.6 = (bf16[136,896]{1,0:T(8,128)(2,1)S(1)}, bf16[136,896]{1,0:T(8,128)(2,1)}, u32[]{:S(2)}, u32[]{:S(2)}) collective-permute-start(bf16[136,896]{1,0:T(8,128)(2,1)S(1)} %collective-permute-done.1.refs_1_), channel_id=1, source_target_pairs={{0,4},{2,6},{4,0},{6,2},{8,12},{10,14},{12,8},{14,10},{1,5},{3,7},... | collective-permute-start | bytes 731144 | tf_op jit(solution)/shard_map/ppermute | solution.py:311
  42.5 0.1 collective-permute-start.7
  42.5 0.0 collective-permute-done.8
  42.5 4.6 %all-to-all-done.got_ref = bf16[8,112,384]{2,1,0:T(8,128)(2,1)S(1)} async-done(((bf16[8,112,384]{2,1,0:T(8,128)(2,1)}), bf16[8,112,384]{2,1,0:T(8,128)(2,1)S(1)}, u32[]{:S(2)}, u32[]{:S(2)}) %all-to-all-start) | async-done | bytes 688160 | tf_op jit(solution)/shard_map/all_to_all | solution.py:322
  47.1 1.0 %add_convert_fusion = bf16[2,448,384]{2,1,0:T(8,128)(2,1)} fusion(bf16[2,448,384]{2,1,0:T(8,128)(2,1)S(1)} %collective-permute-done.8, bf16[2,448,384]{2,1,0:T(8,128)(2,1)S(1)} %get-tuple-element.43), kind=kLoop, calls=%fused_computation | loop fusion | flops 1376256 | bytes 2064384 | tf_op jit(solution)/shard_map/convert_element_type | solution.py:318
  48.1 0.0 copy-done.3
  48.2 5.8 %all-to-all-start.1 = ((bf16[8,112,384]{2,1,0:T(8,128)(2,1)}), bf16[8,112,384]{2,1,0:T(8,128)(2,1)S(1)}, u32[]{:S(2)}, u32[]{:S(2)}) async-start(bf16[8,112,384]{2,1,0:T(8,128)(2,1)} %bitcast.8), calls=%async_computation.1 | async-start | bytes 1376256 | tf_op jit(solution)/shard_map/all_to_all | solution.py:322
  53.9 0.0 copy-start.4
  53.9 0.0 copy-start
  53.9 0.0 collective-permute-done.5.refs_3_.refs_5_
  53.9 0.0 collective-permute-done.6.refs_5_.refs_9_
  54.0 4.4 %collective-permute-done.7.refs_7_.refs_13_ = bf16[136,896]{1,0:T(8,128)(2,1)} collective-permute-done((bf16[136,896]{1,0:T(8,128)(2,1)S(1)}, bf16[136,896]{1,0:T(8,128)(2,1)}, u32[]{:S(2)}, u32[]{:S(2)}) %collective-permute-start.7) | collective-permute-done | bytes 243744 | tf_op jit(solution)/shard_map/ppermute | solution.py:311
  58.4 0.0 copy-done.5
  58.4 1.3 %shard_map.106.ids_ref = s32[16,128]{1,0:T(8,128)} custom-call(bf16[136,896]{1,0:T(8,128)(2,1)} %copy-done.1, bf16[136,896]{1,0:T(8,128)(2,1)} %copy-done.5, bf16[136,896]{1,0:T(8,128)(2,1)} %copy-done.3, bf16[136,896]{1,0:T(8,128)(2,1)} %collective-permute-done.5.refs_3_.refs_5_, bf16[136,896]{1,0:T(8,128)(2,1)} %collective-permute-done.3.refs_4_.refs_8_, ...), custom_call_target="tpu_custom_call" | custom-call | flops 68719476736 | bytes 1000 | tf_op jit(solution)/shard_map/pallas_call | solution.py:133
  59.7 0.0 copy-done.2
  59.7 0.0 collective-permute-start.9
  59.7 0.5 collective-permute-start.10
  60.2 0.1 collective-permute-start.11
  60.3 0.4 collective-permute-start.12
  60.7 0.1 collective-permute-start.13
  60.8 0.4 collective-permute-done.9.refs_2_
  61.2 0.1 collective-permute-start.14
  61.3 0.4 collective-permute-done.10.refs_3_
  61.8 0.2 collective-permute-start.15
  61.9 0.3 collective-permute-done.11.refs_6_
  62.3 0.1 collective-permute-start.16
  62.4 0.1 copy-done.7
  62.5 0.5 copy-done.8
  62.9 0.1 pad_add_fusion.place_ref
  63.0 1.4 %shard_map.107.sum_ref = f32[32,112,128]{2,1,0:T(8,128)S(1)} custom-call(s32[3]{0:T(128)S(1)} %pad_add_fusion.place_ref, s32[16,128]{1,0:T(8,128)} %shard_map.106.ids_ref, s32[32]{0:T(128)S(1)} %copy-done, bf16[8,112,384]{2,1,0:T(8,128)(2,1)S(1)} %all-to-all-done.got_ref), custom_call_target="tpu_custom_call" | custom-call | flops 1000 | bytes 1000 | tf_op jit(solution)/shard_map/pallas_call | solution.py:173
  64.4 0.0 collective-permute-done.12.refs_7_
  64.4 0.0 collective-permute-done.13.refs_10_
  64.4 0.0 collective-permute-done.14.refs_11_
  64.4 0.0 collective-permute-done.15.refs_14_
  64.4 0.0 collective-permute-done.16.refs_15_
  64.5 4.9 %all-to-all-done.1.got_ref = bf16[8,112,384]{2,1,0:T(8,128)(2,1)S(1)} async-done(((bf16[8,112,384]{2,1,0:T(8,128)(2,1)}), bf16[8,112,384]{2,1,0:T(8,128)(2,1)S(1)}, u32[]{:S(2)}, u32[]{:S(2)}) %all-to-all-start.1) | async-done | bytes 688160 | tf_op jit(solution)/shard_map/all_to_all | solution.py:322
  69.3 4.0 %shard_map.108 = f32[896,112]{1,0:T(8,128)S(1)} custom-call(s32[3]{0:T(128)S(1)} %pad_add_fusion.place_ref, s32[16,128]{1,0:T(8,128)} %shard_map.106.ids_ref, s32[32]{0:T(128)S(1)} %copy-done, bf16[8,112,384]{2,1,0:T(8,128)(2,1)S(1)} %all-to-all-done.1.got_ref, f32[32,112,128]{2,1,0:T(8,128)S(1)} %shard_map.107.sum_ref, bf16[136,896]{1,0:T(8,128)(2,1)} %copy-done.1, ...), custom_call_target="tpu_custom_call" | custom-call | flops 411041792 | bytes 6000000 | tf_op jit(solution)/shard_map/pallas_call | solution.py:241
  73.3 18.0 %all_to_all.15 = f32[16,56,112]{2,1,0:T(8,128)S(1)} all-to-all(f32[16,56,112]{2,1,0:T(8,128)S(1)} %bitcast.19), channel_id=1, replica_groups=mesh['group'=2,'dp'=8,'section'=2] {'dp','section'}, dimensions={0} | all-to-all | bytes 802816 | tf_op jit(solution)/shard_map/all_to_all | solution.py:340
  91.3 0.1 copy.18
  91.4 0.9 reshape.43
  (11 shorter events, 0.1 us)
Async XLA Ops:
  0.6 13.3 %copy-start.9 = (bf16[512,896]{1,0:T(8,128)(2,1)S(1)}, bf16[512,896]{1,0:T(8,128)(2,1)}, u32[]{:S(2)}) copy-start(bf16[512,896]{1,0:T(8,128)(2,1)} %param.17) | copy-start | bytes 2752516
  0.6 13.3 %copy-start.10 = (s32[6,2]{0,1:T(2,128)S(1)}, s32[6,2]{0,1:T(2,128)}, u32[]{:S(2)}) copy-start(s32[6,2]{0,1:T(2,128)} %param.15) | copy-start | bytes 148
  13.4 7.9 %collective-permute-start = (bf16[2,448,384]{2,1,0:T(8,128)(2,1)S(1)}, bf16[2,448,384]{2,1,0:T(8,128)(2,1)S(1)}, u32[]{:S(2)}, u32[]{:S(2)}) collective-permute-start(bf16[2,448,384]{2,1,0:T(8,128)(2,1)S(1)} %get-tuple-element.32), channel_id=1, source_target_pairs={{0,1},{1,0},{2,3},{3,2},{4,5},{5,4},{6,7},{7,6},{8,9},{9,8},{10,11... | collective-permute-start | bytes 2064392 | tf_op jit(solution)/shard_map/ppermute | solution.py:315
  14.0 8.3 %copy-start.1 = (bf16[136,896]{1,0:T(8,128)(2,1)}, bf16[136,896]{1,0:T(8,128)(2,1)S(1)}, u32[]{:S(2)}) copy-start(bf16[136,896]{1,0:T(8,128)(2,1)S(1)} %get-tuple-element.48.refs_0_) | copy-start | bytes 731140
  14.0 24.7 %collective-permute-start.2 = (bf16[136,896]{1,0:T(8,128)(2,1)S(1)}, bf16[136,896]{1,0:T(8,128)(2,1)S(1)}, u32[]{:S(2)}, u32[]{:S(2)}) collective-permute-start(bf16[136,896]{1,0:T(8,128)(2,1)S(1)} %get-tuple-element.48.refs_0_), channel_id=1, source_target_pairs={{0,2},{2,0},{4,6},{6,4},{8,10},{10,8},{12,14},{14,12},{1,3},{3,1},... | collective-permute-start | bytes 731144 | tf_op jit(solution)/shard_map/ppermute | solution.py:311
  16.7 22.1 %collective-permute-start.3 = (bf16[136,896]{1,0:T(8,128)(2,1)S(1)}, bf16[136,896]{1,0:T(8,128)(2,1)}, u32[]{:S(2)}, u32[]{:S(2)}) collective-permute-start(bf16[136,896]{1,0:T(8,128)(2,1)S(1)} %get-tuple-element.48.refs_0_), channel_id=1, source_target_pairs={{0,4},{2,6},{4,0},{6,2},{8,12},{10,14},{12,8},{14,10},{1,5},{3,7},... | collective-permute-start | bytes 731144 | tf_op jit(solution)/shard_map/ppermute | solution.py:311
  18.3 20.5 %collective-permute-start.4 = (bf16[136,896]{1,0:T(8,128)(2,1)S(1)}, bf16[136,896]{1,0:T(8,128)(2,1)}, u32[]{:S(2)}, u32[]{:S(2)}) collective-permute-start(bf16[136,896]{1,0:T(8,128)(2,1)S(1)} %get-tuple-element.48.refs_0_), channel_id=1, source_target_pairs={{0,6},{2,4},{4,2},{6,0},{8,14},{10,12},{12,10},{14,8},{1,7},{3,5},... | collective-permute-start | bytes 731144 | tf_op jit(solution)/shard_map/ppermute | solution.py:311
  18.3 20.5 %collective-permute-start.1 = (bf16[136,896]{1,0:T(8,128)(2,1)S(1)}, bf16[136,896]{1,0:T(8,128)(2,1)S(1)}, u32[]{:S(2)}, u32[]{:S(2)}) collective-permute-start(bf16[136,896]{1,0:T(8,128)(2,1)S(1)} %get-tuple-element.59), channel_id=1, source_target_pairs={{0,8},{2,10},{4,12},{6,14},{8,0},{10,2},{12,4},{14,6},{1,9},{3,11}... | collective-permute-start | bytes 731144 | tf_op jit(solution)/shard_map/ppermute | solution.py:307
  22.3 24.8 %all-to-all-start = ((bf16[8,112,384]{2,1,0:T(8,128)(2,1)}), bf16[8,112,384]{2,1,0:T(8,128)(2,1)S(1)}, u32[]{:S(2)}, u32[]{:S(2)}) async-start(bf16[8,112,384]{2,1,0:T(8,128)(2,1)} %bitcast.1), calls=%async_computation | async-start | bytes 1376256 | tf_op jit(solution)/shard_map/all_to_all | solution.py:322
  38.8 19.6 %copy-start.5 = (bf16[136,896]{1,0:T(8,128)(2,1)}, bf16[136,896]{1,0:T(8,128)(2,1)S(1)}, u32[]{:S(2)}) copy-start(bf16[136,896]{1,0:T(8,128)(2,1)S(1)} %collective-permute-done.1.refs_1_) | copy-start | bytes 731140
  38.8 9.4 %copy-start.3 = (bf16[136,896]{1,0:T(8,128)(2,1)}, bf16[136,896]{1,0:T(8,128)(2,1)S(1)}, u32[]{:S(2)}) copy-start(bf16[136,896]{1,0:T(8,128)(2,1)S(1)} %collective-permute-done.2.refs_2_.refs_4_) | copy-start | bytes 731140
  38.8 3.7 %collective-permute-start.8 = (bf16[2,448,384]{2,1,0:T(8,128)(2,1)S(1)}, bf16[2,448,384]{2,1,0:T(8,128)(2,1)S(1)}, u32[]{:S(2)}, u32[]{:S(2)}) collective-permute-start(bf16[2,448,384]{2,1,0:T(8,128)(2,1)S(1)} %get-tuple-element.45), channel_id=1, source_target_pairs={{0,1},{1,0},{2,3},{3,2},{4,5},{5,4},{6,7},{7,6},{8,9},{9,8},{10,11... | collective-permute-start | bytes 2064392 | tf_op jit(solution)/shard_map/ppermute | solution.py:315
  38.9 15.0 %collective-permute-start.5 = (bf16[136,896]{1,0:T(8,128)(2,1)S(1)}, bf16[136,896]{1,0:T(8,128)(2,1)}, u32[]{:S(2)}, u32[]{:S(2)}) collective-permute-start(bf16[136,896]{1,0:T(8,128)(2,1)S(1)} %collective-permute-done.1.refs_1_), channel_id=1, source_target_pairs={{0,2},{2,0},{4,6},{6,4},{8,10},{10,8},{12,14},{14,12},{1,3},{3,1},... | collective-permute-start | bytes 731144 | tf_op jit(solution)/shard_map/ppermute | solution.py:311
  41.0 13.0 %collective-permute-start.6 = (bf16[136,896]{1,0:T(8,128)(2,1)S(1)}, bf16[136,896]{1,0:T(8,128)(2,1)}, u32[]{:S(2)}, u32[]{:S(2)}) collective-permute-start(bf16[136,896]{1,0:T(8,128)(2,1)S(1)} %collective-permute-done.1.refs_1_), channel_id=1, source_target_pairs={{0,4},{2,6},{4,0},{6,2},{8,12},{10,14},{12,8},{14,10},{1,5},{3,7},... | collective-permute-start | bytes 731144 | tf_op jit(solution)/shard_map/ppermute | solution.py:311
  42.5 15.9 %collective-permute-start.7 = (bf16[136,896]{1,0:T(8,128)(2,1)S(1)}, bf16[136,896]{1,0:T(8,128)(2,1)}, u32[]{:S(2)}, u32[]{:S(2)}) collective-permute-start(bf16[136,896]{1,0:T(8,128)(2,1)S(1)} %collective-permute-done.1.refs_1_), channel_id=1, source_target_pairs={{0,6},{2,4},{4,2},{6,0},{8,14},{10,12},{12,10},{14,8},{1,7},{3,5},... | collective-permute-start | bytes 731144 | tf_op jit(solution)/shard_map/ppermute | solution.py:311
  48.2 21.2 %all-to-all-start.1 = ((bf16[8,112,384]{2,1,0:T(8,128)(2,1)}), bf16[8,112,384]{2,1,0:T(8,128)(2,1)S(1)}, u32[]{:S(2)}, u32[]{:S(2)}) async-start(bf16[8,112,384]{2,1,0:T(8,128)(2,1)} %bitcast.8), calls=%async_computation.1 | async-start | bytes 1376256 | tf_op jit(solution)/shard_map/all_to_all | solution.py:322
  53.9 5.8 %copy-start.2 = (bf16[136,896]{1,0:T(8,128)(2,1)S(1)}, bf16[136,896]{1,0:T(8,128)(2,1)}, u32[]{:S(2)}) copy-start(bf16[136,896]{1,0:T(8,128)(2,1)} %copy-done.1) | copy-start | bytes 731140
  53.9 6.3 %copy-start.4 = (bf16[136,896]{1,0:T(8,128)(2,1)S(1)}, bf16[136,896]{1,0:T(8,128)(2,1)}, u32[]{:S(2)}) copy-start(bf16[136,896]{1,0:T(8,128)(2,1)} %copy-done.3) | copy-start | bytes 731140
  53.9 9.1 %copy-start = (s32[32]{0:T(128)S(1)}, s32[32]{0:T(128)}, u32[]{:S(2)}) copy-start(s32[32]{0:T(128)} %slot_ref.3) | copy-start | bytes 388
  59.7 1.5 %collective-permute-start.9 = (bf16[136,896]{1,0:T(8,128)(2,1)S(1)}, bf16[136,896]{1,0:T(8,128)(2,1)S(1)}, u32[]{:S(2)}, u32[]{:S(2)}) collective-permute-start(bf16[136,896]{1,0:T(8,128)(2,1)S(1)} %copy-done.2), channel_id=1, source_target_pairs={{0,1},{1,0},{2,3},{3,2},{4,5},{5,4},{6,7},{7,6},{8,9},{9,8},{10,11... | collective-permute-start | bytes 731144 | tf_op jit(solution)/shard_map/ppermute | solution.py:331
  59.7 2.1 %collective-permute-start.10 = (bf16[136,896]{1,0:T(8,128)(2,1)}, bf16[136,896]{1,0:T(8,128)(2,1)S(1)}, u32[]{:S(2)}, u32[]{:S(2)}) collective-permute-start(bf16[136,896]{1,0:T(8,128)(2,1)} %copy-done.5), channel_id=1, source_target_pairs={{0,1},{1,0},{2,3},{3,2},{4,5},{5,4},{6,7},{7,6},{8,9},{9,8},{10,11... | collective-permute-start | bytes 731144 | tf_op jit(solution)/shard_map/ppermute | solution.py:331
  60.2 2.0 %collective-permute-start.11 = (bf16[136,896]{1,0:T(8,128)(2,1)S(1)}, bf16[136,896]{1,0:T(8,128)(2,1)S(1)}, u32[]{:S(2)}, u32[]{:S(2)}) collective-permute-start(bf16[136,896]{1,0:T(8,128)(2,1)S(1)} %copy-done.4), channel_id=1, source_target_pairs={{0,1},{1,0},{2,3},{3,2},{4,5},{5,4},{6,7},{7,6},{8,9},{9,8},{10,11... | collective-permute-start | bytes 731144 | tf_op jit(solution)/shard_map/ppermute | solution.py:331
  60.3 4.1 %collective-permute-start.12 = (bf16[136,896]{1,0:T(8,128)(2,1)}, bf16[136,896]{1,0:T(8,128)(2,1)}, u32[]{:S(2)}, u32[]{:S(2)}) collective-permute-start(bf16[136,896]{1,0:T(8,128)(2,1)} %collective-permute-done.5.refs_3_.refs_5_), channel_id=1, source_target_pairs={{0,1},{1,0},{2,3},{3,2},{4,5},{5,4},{6,7},{7,6},{8,9},{9,8},{10,11... | collective-permute-start | bytes 731144 | tf_op jit(solution)/shard_map/ppermute | solution.py:331
  60.7 3.7 %collective-permute-start.13 = (bf16[136,896]{1,0:T(8,128)(2,1)}, bf16[136,896]{1,0:T(8,128)(2,1)}, u32[]{:S(2)}, u32[]{:S(2)}) collective-permute-start(bf16[136,896]{1,0:T(8,128)(2,1)} %collective-permute-done.3.refs_4_.refs_8_), channel_id=1, source_target_pairs={{0,1},{1,0},{2,3},{3,2},{4,5},{5,4},{6,7},{7,6},{8,9},{9,8},{10,11... | collective-permute-start | bytes 731144 | tf_op jit(solution)/shard_map/ppermute | solution.py:331
  61.2 8.1 %copy-start.6 = (bf16[136,896]{1,0:T(8,128)(2,1)}, bf16[136,896]{1,0:T(8,128)(2,1)S(1)}, u32[]{:S(2)}) copy-start(bf16[136,896]{1,0:T(8,128)(2,1)S(1)} %collective-permute-done.9.refs_2_) | copy-start | bytes 731140
  61.2 3.2 %collective-permute-start.14 = (bf16[136,896]{1,0:T(8,128)(2,1)}, bf16[136,896]{1,0:T(8,128)(2,1)}, u32[]{:S(2)}, u32[]{:S(2)}) collective-permute-start(bf16[136,896]{1,0:T(8,128)(2,1)} %collective-permute-done.6.refs_5_.refs_9_), channel_id=1, source_target_pairs={{0,1},{1,0},{2,3},{3,2},{4,5},{5,4},{6,7},{7,6},{8,9},{9,8},{10,11... | collective-permute-start | bytes 731144 | tf_op jit(solution)/shard_map/ppermute | solution.py:331
  61.8 0.7 copy-start.7
  61.8 2.7 %collective-permute-start.15 = (bf16[136,896]{1,0:T(8,128)(2,1)}, bf16[136,896]{1,0:T(8,128)(2,1)}, u32[]{:S(2)}, u32[]{:S(2)}) collective-permute-start(bf16[136,896]{1,0:T(8,128)(2,1)} %collective-permute-done.4.refs_6_.refs_12_), channel_id=1, source_target_pairs={{0,1},{1,0},{2,3},{3,2},{4,5},{5,4},{6,7},{7,6},{8,9},{9,8},{10,11... | collective-permute-start | bytes 731144 | tf_op jit(solution)/shard_map/ppermute | solution.py:331
  62.2 0.7 copy-start.8
  62.3 2.2 %collective-permute-start.16 = (bf16[136,896]{1,0:T(8,128)(2,1)}, bf16[136,896]{1,0:T(8,128)(2,1)}, u32[]{:S(2)}, u32[]{:S(2)}) collective-permute-start(bf16[136,896]{1,0:T(8,128)(2,1)} %collective-permute-done.7.refs_7_.refs_13_), channel_id=1, source_target_pairs={{0,1},{1,0},{2,3},{3,2},{4,5},{5,4},{6,7},{7,6},{8,9},{9,8},{10,11... | collective-permute-start | bytes 731144 | tf_op jit(solution)/shard_map/ppermute | solution.py:331

commit v5 on v4

--- a/solution.py
+++ b/solution.py
@@ -325,10 +325,10 @@
     packs = spread(mirror)
     packs = [x for pair in zip(own, packs) for x in pair]
     ids = _ids_call(packs, owned // 2 * HR, id_rows.shape[0])
-    ids, packs = lax.optimization_barrier((ids, packs))
+    ids, far = lax.optimization_barrier((ids, packs[1::2]))
     xs = []
-    for n in range(0, len(packs), 2):
-        xs += packs[n : n + 2] + [lax.ppermute(x, "section", swap) for x in packs[n : n + 2]]
+    for near, x in zip(packs[::2], far):
+        xs += [near, x] + [lax.ppermute(y, "section", swap) for y in (near, x)]
     place = jnp.stack([upper, lower, section])
     ids = pltpu.with_memory_space_constraint(ids, pltpu.HBM)
     partial_sum = _add_call(chunks[0], spans, 0, place, ids, block_slot, gots[0])

time: 92.7 us -> 92.7 us (level)
    ppermute x8, waiting for transfers between devices: 1.17 us -> 0.08 us  [per_device(): xs += [near, x] + [lax.ppermute(y, 'section', swap) for y in (near, x)]]
  transfers between devices with their start and end apart: 19 -> 19, of which waited for: 6 -> 4; matrix products, arithmetic and copies ran while one was open for 2% -> 2% of each run, Pallas kernels for 17% -> 17%
where the time goes in v5:
time: 92.7 us; the launch traced here: 92.3 us
  Pallas kernels  32.1 us (35%)
  starting transfers between devices  22.9 us (25%)
  blocking collectives  18 us (19%)
  waiting for transfers between devices  14.2 us (15%)
  other arithmetic  2.22 us (2%)
  local copies, waits for them, and re-layouts  2.01 us (2%)
    pallas_call x2, Pallas kernels, _span_call(): pl.pallas_call(functools.partial(_span_kernel, first, spans), grid_spec=p...  25.4 us
    all_to_all x1, blocking collectives, per_device(): lax.all_to_all(weight.reshape(2 * peers, rows, cols), ('dp', 'section'),...  18 us
    all_to_all x2, waiting for transfers between devices, per_device(): gots.append(lax.all_to_all(ref_grad, 'dp', 0, 0, tiled=True))  10.1 us
    all_to_all x2, starting transfers between devices, per_device(): gots.append(lax.all_to_all(ref_grad, 'dp', 0, 0, tiled=True))  9.56 us
    ppermute x6, starting transfers between devices, spread(): lax.ppermute(pack, 'dp', [(i, i ^ m) for i in range(peers)])  7.73 us
    ppermute x6, waiting for transfers between devices, spread(): lax.ppermute(pack, 'dp', [(i, i ^ m) for i in range(peers)])  4.06 us
    pallas_call x1, Pallas kernels, _weight_call(): pl.pallas_call(functools.partial(_weight_kernel, count, spans, first), in...  3.99 us
    ppermute x1, starting transfers between devices, per_device(): mirror = lax.ppermute(away, 'dp', [(i, i ^ inner) for i in range(peers)])  2.97 us
  transfers between devices with their start and end apart: 19, of which 4 were waited for; matrix products, arithmetic and copies ran while one was open for 2% of the time, Pallas kernels for 17%

profile of v5, /device:TPU:0, one launch (start us, length us, event | category | flops | bytes accessed | tf_op | source)
XLA Modules:
  0.0 92.3 jit_solution(11156550851508157384)
XLA Ops:
  0.6 0.0 copy-start.8
  0.6 0.0 copy-start.9
  0.7 12.7 %shard_map.104 = (bf16[384,1024]{1,0:T(8,128)(2,1)}, bf16[2,448,384]{2,1,0:T(8,128)(2,1)S(1)}, bf16[2,448,384]{2,1,0:T(8,128)(2,1)S(1)}) custom-call(s32[1]{0:T(128)} %bitcast.sec_ref, bf16[384,1024]{1,0:T(8,128)(2,1)} %q_ref.3, bf16[384,1024]{1,0:T(8,128)(2,1)} %g_ref.3, f32[8,384]{1,0:T(8,128)} %l_ref.3, bf16[6,256,896]{2,1,0:T(8,128)(2,1)} %n_ref.3, ...), custom_call_target="tpu_custom_call" | custom-call | flops 6140461056 | bytes 6670016 | tf_op jit(solution)/shard_map/pallas_call | solution.py:101
  13.4 0.5 collective-permute-start
  13.9 0.0 copy-done.8
  14.0 0.0 copy-done.9
  14.0 0.0 copy-start.1
  14.0 2.7 %collective-permute-start.2 = (bf16[136,896]{1,0:T(8,128)(2,1)S(1)}, bf16[136,896]{1,0:T(8,128)(2,1)S(1)}, u32[]{:S(2)}, u32[]{:S(2)}) collective-permute-start(bf16[136,896]{1,0:T(8,128)(2,1)S(1)} %get-tuple-element.33.refs_0_), channel_id=1, source_target_pairs={{0,2},{2,0},{4,6},{6,4},{8,10},{10,8},{12,14},{14,12},{1,3},{3,1},... | collective-permute-start | bytes 731144 | tf_op jit(solution)/shard_map/ppermute | solution.py:311
  16.7 1.6 %collective-permute-start.3 = (bf16[136,896]{1,0:T(8,128)(2,1)S(1)}, bf16[136,896]{1,0:T(8,128)(2,1)S(1)}, u32[]{:S(2)}, u32[]{:S(2)}) collective-permute-start(bf16[136,896]{1,0:T(8,128)(2,1)S(1)} %get-tuple-element.33.refs_0_), channel_id=1, source_target_pairs={{0,4},{2,6},{4,0},{6,2},{8,12},{10,14},{12,8},{14,10},{1,5},{3,7},... | collective-permute-start | bytes 731144 | tf_op jit(solution)/shard_map/ppermute | solution.py:311
  18.3 0.0 collective-permute-start.4
  18.3 3.0 %collective-permute-start.1 = (bf16[136,896]{1,0:T(8,128)(2,1)S(1)}, bf16[136,896]{1,0:T(8,128)(2,1)}, u32[]{:S(2)}, u32[]{:S(2)}) collective-permute-start(bf16[136,896]{1,0:T(8,128)(2,1)S(1)} %get-tuple-element.51), channel_id=1, source_target_pairs={{0,8},{2,10},{4,12},{6,14},{8,0},{10,2},{12,4},{14,6},{1,9},{3,11}... | collective-permute-start | bytes 731144 | tf_op jit(solution)/shard_map/ppermute | solution.py:307
  21.2 0.0 collective-permute-done
  21.2 1.0 %add_convert_fusion.1 = bf16[2,448,384]{2,1,0:T(8,128)(2,1)} fusion(bf16[2,448,384]{2,1,0:T(8,128)(2,1)S(1)} %collective-permute-done, bf16[2,448,384]{2,1,0:T(8,128)(2,1)S(1)} %get-tuple-element.26), kind=kLoop, calls=%fused_computation.1 | loop fusion | flops 1376256 | bytes 2064384 | tf_op jit(solution)/shard_map/convert_element_type | solution.py:318
  22.3 3.8 %all-to-all-start = ((bf16[8,112,384]{2,1,0:T(8,128)(2,1)}), bf16[8,112,384]{2,1,0:T(8,128)(2,1)S(1)}, u32[]{:S(2)}, u32[]{:S(2)}) async-start(bf16[8,112,384]{2,1,0:T(8,128)(2,1)} %bitcast.1), calls=%async_computation | async-start | bytes 1376256 | tf_op jit(solution)/shard_map/all_to_all | solution.py:322
  26.1 12.7 %shard_map.105 = (bf16[384,1024]{1,0:T(8,128)(2,1)}, bf16[2,448,384]{2,1,0:T(8,128)(2,1)S(1)}, bf16[2,448,384]{2,1,0:T(8,128)(2,1)S(1)}) custom-call(s32[1]{0:T(128)} %bitcast.sec_ref, bf16[384,1024]{1,0:T(8,128)(2,1)} %q_ref.3, bf16[384,1024]{1,0:T(8,128)(2,1)} %g_ref.3, f32[8,384]{1,0:T(8,128)} %l_ref.3, ...), custom_call_target="tpu_custom_call", output_to_operand_aliasing={{0}: (7, {})} | custom-call | flops 6140461056 | bytes 6670016 | tf_op jit(solution)/shard_map/pallas_call | solution.py:101
  38.8 0.0 collective-permute-done.1.refs_1_
  38.8 0.0 collective-permute-done.2.refs_2_.refs_4_
  38.8 0.0 copy-start.2
  38.8 0.0 collective-permute-done.3.refs_4_.refs_8_
  38.8 0.0 copy-start.3
  38.8 0.0 collective-permute-done.4.refs_6_.refs_12_
  38.8 0.7 copy-done.3
  39.5 0.0 collective-permute-start.8
  39.5 2.0 %collective-permute-start.5 = (bf16[136,896]{1,0:T(8,128)(2,1)}, bf16[136,896]{1,0:T(8,128)(2,1)}, u32[]{:S(2)}, u32[]{:S(2)}) collective-permute-start(bf16[136,896]{1,0:T(8,128)(2,1)} %collective-permute-done.1.refs_1_), channel_id=1, source_target_pairs={{0,2},{2,0},{4,6},{6,4},{8,10},{10,8},{12,14},{14,12},{1,3},{3,1},... | collective-permute-start | bytes 731144 | tf_op jit(solution)/shard_map/ppermute | solution.py:311
  41.6 1.5 %collective-permute-start.6 = (bf16[136,896]{1,0:T(8,128)(2,1)}, bf16[136,896]{1,0:T(8,128)(2,1)}, u32[]{:S(2)}, u32[]{:S(2)}) collective-permute-start(bf16[136,896]{1,0:T(8,128)(2,1)} %collective-permute-done.1.refs_1_), channel_id=1, source_target_pairs={{0,4},{2,6},{4,0},{6,2},{8,12},{10,14},{12,8},{14,10},{1,5},{3,7},... | collective-permute-start | bytes 731144 | tf_op jit(solution)/shard_map/ppermute | solution.py:311
  43.0 0.0 collective-permute-start.7
  43.0 0.0 copy-done.1
  43.0 0.0 collective-permute-start.9
  43.1 0.0 collective-permute-done.8
  43.1 0.5 collective-permute-start.11
  43.6 3.6 %all-to-all-done.got_ref = bf16[8,112,384]{2,1,0:T(8,128)(2,1)S(1)} async-done(((bf16[8,112,384]{2,1,0:T(8,128)(2,1)}), bf16[8,112,384]{2,1,0:T(8,128)(2,1)S(1)}, u32[]{:S(2)}, u32[]{:S(2)}) %all-to-all-start) | async-done | bytes 688160 | tf_op jit(solution)/shard_map/all_to_all | solution.py:322
  47.1 1.0 %add_convert_fusion = bf16[2,448,384]{2,1,0:T(8,128)(2,1)} fusion(bf16[2,448,384]{2,1,0:T(8,128)(2,1)S(1)} %collective-permute-done.8, bf16[2,448,384]{2,1,0:T(8,128)(2,1)S(1)} %get-tuple-element.39), kind=kLoop, calls=%fused_computation | loop fusion | flops 1376256 | bytes 2064384 | tf_op jit(solution)/shard_map/convert_element_type | solution.py:318
  48.2 0.0 copy-done.2
  48.2 5.8 %all-to-all-start.1 = ((bf16[8,112,384]{2,1,0:T(8,128)(2,1)}), bf16[8,112,384]{2,1,0:T(8,128)(2,1)S(1)}, u32[]{:S(2)}, u32[]{:S(2)}) async-start(bf16[8,112,384]{2,1,0:T(8,128)(2,1)} %bitcast.8), calls=%async_computation.1 | async-start | bytes 1376256 | tf_op jit(solution)/shard_map/all_to_all | solution.py:322
  53.9 0.0 collective-permute-done.5.refs_3_.refs_5_
  53.9 0.0 copy-done.4
  53.9 0.1 collective-permute-start.13
  54.0 0.0 collective-permute-done.6.refs_5_.refs_9_
  54.0 0.5 collective-permute-start.15
  54.5 4.0 %collective-permute-done.7.refs_7_.refs_13_ = bf16[136,896]{1,0:T(8,128)(2,1)} collective-permute-done((bf16[136,896]{1,0:T(8,128)(2,1)}, bf16[136,896]{1,0:T(8,128)(2,1)}, u32[]{:S(2)}, u32[]{:S(2)}) %collective-permute-start.7) | collective-permute-done | bytes 243744 | tf_op jit(solution)/shard_map/ppermute | solution.py:311
  58.6 1.3 %shard_map.106.ids_ref = s32[16,128]{1,0:T(8,128)} custom-call(bf16[136,896]{1,0:T(8,128)(2,1)} %copy-done.1, bf16[136,896]{1,0:T(8,128)(2,1)} %collective-permute-done.1.refs_1_, bf16[136,896]{1,0:T(8,128)(2,1)} %copy-done.2, bf16[136,896]{1,0:T(8,128)(2,1)} %collective-permute-done.5.refs_3_.refs_5_, bf16[136,896]{1,0:T(8,128)(2,1)} %copy-done.3, ...), custom_call_target="tpu_custom_call" | custom-call | flops 68719476736 | bytes 1000 | tf_op jit(solution)/shard_map/pallas_call | solution.py:133
  59.9 0.0 collective-permute-start.10
  59.9 0.0 collective-permute-done.9.refs_2_
  59.9 0.5 collective-permute-start.12
  60.4 0.0 collective-permute-done.11.refs_6_
  60.4 0.1 collective-permute-start.14
  60.5 0.0 collective-permute-done.13.refs_10_
  60.5 0.4 collective-permute-start.16
  60.9 0.2 copy-done.5
  61.1 0.1 copy-done.6
  61.2 0.1 pad_add_fusion.place_ref
  61.3 0.0 copy-done
  61.3 1.4 %shard_map.107.sum_ref = f32[32,112,128]{2,1,0:T(8,128)S(1)} custom-call(s32[3]{0:T(128)S(1)} %pad_add_fusion.place_ref, s32[16,128]{1,0:T(8,128)} %shard_map.106.ids_ref, s32[32]{0:T(128)S(1)} %copy-done, bf16[8,112,384]{2,1,0:T(8,128)(2,1)S(1)} %all-to-all-done.got_ref), custom_call_target="tpu_custom_call" | custom-call | flops 1000 | bytes 1000 | tf_op jit(solution)/shard_map/pallas_call | solution.py:173
  62.7 0.0 collective-permute-done.15.refs_14_
  62.7 0.0 collective-permute-done.10.refs_3_
  62.7 0.0 collective-permute-done.12.refs_7_
  62.7 0.0 copy-start.7
  62.7 0.0 collective-permute-done.14.refs_11_
  62.7 0.1 collective-permute-done.16.refs_15_
  62.8 6.5 %all-to-all-done.1.got_ref = bf16[8,112,384]{2,1,0:T(8,128)(2,1)S(1)} async-done(((bf16[8,112,384]{2,1,0:T(8,128)(2,1)}), bf16[8,112,384]{2,1,0:T(8,128)(2,1)S(1)}, u32[]{:S(2)}, u32[]{:S(2)}) %all-to-all-start.1) | async-done | bytes 688160 | tf_op jit(solution)/shard_map/all_to_all | solution.py:322
  69.3 4.0 %shard_map.108 = f32[896,112]{1,0:T(8,128)S(1)} custom-call(s32[3]{0:T(128)S(1)} %pad_add_fusion.place_ref, s32[16,128]{1,0:T(8,128)} %shard_map.106.ids_ref, s32[32]{0:T(128)S(1)} %copy-done, bf16[8,112,384]{2,1,0:T(8,128)(2,1)S(1)} %all-to-all-done.1.got_ref, f32[32,112,128]{2,1,0:T(8,128)S(1)} %shard_map.107.sum_ref, bf16[136,896]{1,0:T(8,128)(2,1)} %copy-done.1, ...), custom_call_target="tpu_custom_call" | custom-call | flops 411041792 | bytes 6000000 | tf_op jit(solution)/shard_map/pallas_call | solution.py:241
  73.3 18.0 %all_to_all.15 = f32[16,56,112]{2,1,0:T(8,128)S(1)} all-to-all(f32[16,56,112]{2,1,0:T(8,128)S(1)} %bitcast.19), channel_id=1, replica_groups=mesh['group'=2,'dp'=8,'section'=2] {'dp','section'}, dimensions={0} | all-to-all | bytes 802816 | tf_op jit(solution)/shard_map/all_to_all | solution.py:340
  91.4 0.1 copy.18
  91.5 0.9 reshape.43
  (9 shorter events, 0.1 us)
Async XLA Ops:
  0.6 13.3 %copy-start.8 = (bf16[512,896]{1,0:T(8,128)(2,1)S(1)}, bf16[512,896]{1,0:T(8,128)(2,1)}, u32[]{:S(2)}) copy-start(bf16[512,896]{1,0:T(8,128)(2,1)} %param.17) | copy-start | bytes 2752516
  0.6 13.3 %copy-start.9 = (s32[6,2]{0,1:T(2,128)S(1)}, s32[6,2]{0,1:T(2,128)}, u32[]{:S(2)}) copy-start(s32[6,2]{0,1:T(2,128)} %param.15) | copy-start | bytes 148
  13.4 7.9 %collective-permute-start = (bf16[2,448,384]{2,1,0:T(8,128)(2,1)S(1)}, bf16[2,448,384]{2,1,0:T(8,128)(2,1)S(1)}, u32[]{:S(2)}, u32[]{:S(2)}) collective-permute-start(bf16[2,448,384]{2,1,0:T(8,128)(2,1)S(1)} %get-tuple-element.28), channel_id=1, source_target_pairs={{0,1},{1,0},{2,3},{3,2},{4,5},{5,4},{6,7},{7,6},{8,9},{9,8},{10,11... | collective-permute-start | bytes 2064392 | tf_op jit(solution)/shard_map/ppermute | solution.py:315
  14.0 29.0 %copy-start.1 = (bf16[136,896]{1,0:T(8,128)(2,1)}, bf16[136,896]{1,0:T(8,128)(2,1)S(1)}, u32[]{:S(2)}) copy-start(bf16[136,896]{1,0:T(8,128)(2,1)S(1)} %get-tuple-element.33.refs_0_) | copy-start | bytes 731140
  14.0 24.7 %collective-permute-start.2 = (bf16[136,896]{1,0:T(8,128)(2,1)S(1)}, bf16[136,896]{1,0:T(8,128)(2,1)S(1)}, u32[]{:S(2)}, u32[]{:S(2)}) collective-permute-start(bf16[136,896]{1,0:T(8,128)(2,1)S(1)} %get-tuple-element.33.refs_0_), channel_id=1, source_target_pairs={{0,2},{2,0},{4,6},{6,4},{8,10},{10,8},{12,14},{14,12},{1,3},{3,1},... | collective-permute-start | bytes 731144 | tf_op jit(solution)/shard_map/ppermute | solution.py:311
  16.7 22.1 %collective-permute-start.3 = (bf16[136,896]{1,0:T(8,128)(2,1)S(1)}, bf16[136,896]{1,0:T(8,128)(2,1)S(1)}, u32[]{:S(2)}, u32[]{:S(2)}) collective-permute-start(bf16[136,896]{1,0:T(8,128)(2,1)S(1)} %get-tuple-element.33.refs_0_), channel_id=1, source_target_pairs={{0,4},{2,6},{4,0},{6,2},{8,12},{10,14},{12,8},{14,10},{1,5},{3,7},... | collective-permute-start | bytes 731144 | tf_op jit(solution)/shard_map/ppermute | solution.py:311
  18.3 20.5 %collective-permute-start.4 = (bf16[136,896]{1,0:T(8,128)(2,1)S(1)}, bf16[136,896]{1,0:T(8,128)(2,1)}, u32[]{:S(2)}, u32[]{:S(2)}) collective-permute-start(bf16[136,896]{1,0:T(8,128)(2,1)S(1)} %get-tuple-element.33.refs_0_), channel_id=1, source_target_pairs={{0,6},{2,4},{4,2},{6,0},{8,14},{10,12},{12,10},{14,8},{1,7},{3,5},... | collective-permute-start | bytes 731144 | tf_op jit(solution)/shard_map/ppermute | solution.py:311
  18.3 20.5 %collective-permute-start.1 = (bf16[136,896]{1,0:T(8,128)(2,1)S(1)}, bf16[136,896]{1,0:T(8,128)(2,1)}, u32[]{:S(2)}, u32[]{:S(2)}) collective-permute-start(bf16[136,896]{1,0:T(8,128)(2,1)S(1)} %get-tuple-element.51), channel_id=1, source_target_pairs={{0,8},{2,10},{4,12},{6,14},{8,0},{10,2},{12,4},{14,6},{1,9},{3,11}... | collective-permute-start | bytes 731144 | tf_op jit(solution)/shard_map/ppermute | solution.py:307
  22.3 24.8 %all-to-all-start = ((bf16[8,112,384]{2,1,0:T(8,128)(2,1)}), bf16[8,112,384]{2,1,0:T(8,128)(2,1)S(1)}, u32[]{:S(2)}, u32[]{:S(2)}) async-start(bf16[8,112,384]{2,1,0:T(8,128)(2,1)} %bitcast.1), calls=%async_computation | async-start | bytes 1376256 | tf_op jit(solution)/shard_map/all_to_all | solution.py:322
  38.8 9.4 %copy-start.2 = (bf16[136,896]{1,0:T(8,128)(2,1)}, bf16[136,896]{1,0:T(8,128)(2,1)S(1)}, u32[]{:S(2)}) copy-start(bf16[136,896]{1,0:T(8,128)(2,1)S(1)} %collective-permute-done.2.refs_2_.refs_4_) | copy-start | bytes 731140
  38.8 0.7 copy-start.3
  39.5 3.5 %collective-permute-start.8 = (bf16[2,448,384]{2,1,0:T(8,128)(2,1)S(1)}, bf16[2,448,384]{2,1,0:T(8,128)(2,1)S(1)}, u32[]{:S(2)}, u32[]{:S(2)}) collective-permute-start(bf16[2,448,384]{2,1,0:T(8,128)(2,1)S(1)} %get-tuple-element.41), channel_id=1, source_target_pairs={{0,1},{1,0},{2,3},{3,2},{4,5},{5,4},{6,7},{7,6},{8,9},{9,8},{10,11... | collective-permute-start | bytes 2064392 | tf_op jit(solution)/shard_map/ppermute | solution.py:315
  39.5 14.4 %collective-permute-start.5 = (bf16[136,896]{1,0:T(8,128)(2,1)}, bf16[136,896]{1,0:T(8,128)(2,1)}, u32[]{:S(2)}, u32[]{:S(2)}) collective-permute-start(bf16[136,896]{1,0:T(8,128)(2,1)} %collective-permute-done.1.refs_1_), channel_id=1, source_target_pairs={{0,2},{2,0},{4,6},{6,4},{8,10},{10,8},{12,14},{14,12},{1,3},{3,1},... | collective-permute-start | bytes 731144 | tf_op jit(solution)/shard_map/ppermute | solution.py:311
  41.6 12.4 %collective-permute-start.6 = (bf16[136,896]{1,0:T(8,128)(2,1)}, bf16[136,896]{1,0:T(8,128)(2,1)}, u32[]{:S(2)}, u32[]{:S(2)}) collective-permute-start(bf16[136,896]{1,0:T(8,128)(2,1)} %collective-permute-done.1.refs_1_), channel_id=1, source_target_pairs={{0,4},{2,6},{4,0},{6,2},{8,12},{10,14},{12,8},{14,10},{1,5},{3,7},... | collective-permute-start | bytes 731144 | tf_op jit(solution)/shard_map/ppermute | solution.py:311
  43.0 15.5 %collective-permute-start.7 = (bf16[136,896]{1,0:T(8,128)(2,1)}, bf16[136,896]{1,0:T(8,128)(2,1)}, u32[]{:S(2)}, u32[]{:S(2)}) collective-permute-start(bf16[136,896]{1,0:T(8,128)(2,1)} %collective-permute-done.1.refs_1_), channel_id=1, source_target_pairs={{0,6},{2,4},{4,2},{6,0},{8,14},{10,12},{12,10},{14,8},{1,7},{3,5},... | collective-permute-start | bytes 731144 | tf_op jit(solution)/shard_map/ppermute | solution.py:311
  43.0 16.8 %collective-permute-start.9 = (bf16[136,896]{1,0:T(8,128)(2,1)S(1)}, bf16[136,896]{1,0:T(8,128)(2,1)}, u32[]{:S(2)}, u32[]{:S(2)}) collective-permute-start(bf16[136,896]{1,0:T(8,128)(2,1)S(1)} %get-tuple-element.33.refs_0_), channel_id=1, source_target_pairs={{0,1},{1,0},{2,3},{3,2},{4,5},{5,4},{6,7},{7,6},{8,9},{9,8},{10,11... | collective-permute-start | bytes 731144 | tf_op jit(solution)/shard_map/ppermute | solution.py:331
  43.1 17.3 %collective-permute-start.11 = (bf16[136,896]{1,0:T(8,128)(2,1)S(1)}, bf16[136,896]{1,0:T(8,128)(2,1)S(1)}, u32[]{:S(2)}, u32[]{:S(2)}) collective-permute-start(bf16[136,896]{1,0:T(8,128)(2,1)S(1)} %collective-permute-done.2.refs_2_.refs_4_), channel_id=1, source_target_pairs={{0,1},{1,0},{2,3},{3,2},{4,5},{5,4},{6,7},{7,6},{8,9},{9,8},{10,11... | collective-permute-start | bytes 731144 | tf_op jit(solution)/shard_map/ppermute | solution.py:331
  47.1 6.8 %copy-start.4 = (bf16[136,896]{1,0:T(8,128)(2,1)S(1)}, bf16[136,896]{1,0:T(8,128)(2,1)}, u32[]{:S(2)}) copy-start(bf16[136,896]{1,0:T(8,128)(2,1)} %copy-done.3) | copy-start | bytes 731140
  48.2 21.2 %all-to-all-start.1 = ((bf16[8,112,384]{2,1,0:T(8,128)(2,1)}), bf16[8,112,384]{2,1,0:T(8,128)(2,1)S(1)}, u32[]{:S(2)}, u32[]{:S(2)}) async-start(bf16[8,112,384]{2,1,0:T(8,128)(2,1)} %bitcast.8), calls=%async_computation.1 | async-start | bytes 1376256 | tf_op jit(solution)/shard_map/all_to_all | solution.py:322
  53.9 7.4 %copy-start = (s32[32]{0:T(128)S(1)}, s32[32]{0:T(128)}, u32[]{:S(2)}) copy-start(s32[32]{0:T(128)} %slot_ref.3) | copy-start | bytes 388
  53.9 6.5 %collective-permute-start.13 = (bf16[136,896]{1,0:T(8,128)(2,1)S(1)}, bf16[136,896]{1,0:T(8,128)(2,1)S(1)}, u32[]{:S(2)}, u32[]{:S(2)}) collective-permute-start(bf16[136,896]{1,0:T(8,128)(2,1)S(1)} %copy-done.4), channel_id=1, source_target_pairs={{0,1},{1,0},{2,3},{3,2},{4,5},{5,4},{6,7},{7,6},{8,9},{9,8},{10,11... | collective-permute-start | bytes 731144 | tf_op jit(solution)/shard_map/ppermute | solution.py:331
  54.0 8.6 %collective-permute-start.15 = (bf16[136,896]{1,0:T(8,128)(2,1)}, bf16[136,896]{1,0:T(8,128)(2,1)}, u32[]{:S(2)}, u32[]{:S(2)}) collective-permute-start(bf16[136,896]{1,0:T(8,128)(2,1)} %collective-permute-done.4.refs_6_.refs_12_), channel_id=1, source_target_pairs={{0,1},{1,0},{2,3},{3,2},{4,5},{5,4},{6,7},{7,6},{8,9},{9,8},{10,11... | collective-permute-start | bytes 731144 | tf_op jit(solution)/shard_map/ppermute | solution.py:331
  59.9 2.8 %collective-permute-start.10 = (bf16[136,896]{1,0:T(8,128)(2,1)}, bf16[136,896]{1,0:T(8,128)(2,1)}, u32[]{:S(2)}, u32[]{:S(2)}) collective-permute-start(bf16[136,896]{1,0:T(8,128)(2,1)} %collective-permute-done.1.refs_1_), channel_id=1, source_target_pairs={{0,1},{1,0},{2,3},{3,2},{4,5},{5,4},{6,7},{7,6},{8,9},{9,8},{10,11... | collective-permute-start | bytes 731144 | tf_op jit(solution)/shard_map/ppermute | solution.py:331
  59.9 2.8 %collective-permute-start.12 = (bf16[136,896]{1,0:T(8,128)(2,1)}, bf16[136,896]{1,0:T(8,128)(2,1)S(1)}, u32[]{:S(2)}, u32[]{:S(2)}) collective-permute-start(bf16[136,896]{1,0:T(8,128)(2,1)} %collective-permute-done.5.refs_3_.refs_5_), channel_id=1, source_target_pairs={{0,1},{1,0},{2,3},{3,2},{4,5},{5,4},{6,7},{7,6},{8,9},{9,8},{10,11... | collective-permute-start | bytes 731144 | tf_op jit(solution)/shard_map/ppermute | solution.py:331
  60.4 0.7 copy-start.5
  60.4 2.3 %collective-permute-start.14 = (bf16[136,896]{1,0:T(8,128)(2,1)}, bf16[136,896]{1,0:T(8,128)(2,1)}, u32[]{:S(2)}, u32[]{:S(2)}) collective-permute-start(bf16[136,896]{1,0:T(8,128)(2,1)} %collective-permute-done.6.refs_5_.refs_9_), channel_id=1, source_target_pairs={{0,1},{1,0},{2,3},{3,2},{4,5},{5,4},{6,7},{7,6},{8,9},{9,8},{10,11... | collective-permute-start | bytes 731144 | tf_op jit(solution)/shard_map/ppermute | solution.py:331
  60.5 0.7 copy-start.6
  60.5 2.3 %collective-permute-start.16 = (bf16[136,896]{1,0:T(8,128)(2,1)}, bf16[136,896]{1,0:T(8,128)(2,1)}, u32[]{:S(2)}, u32[]{:S(2)}) collective-permute-start(bf16[136,896]{1,0:T(8,128)(2,1)} %collective-permute-done.7.refs_7_.refs_13_), channel_id=1, source_target_pairs={{0,1},{1,0},{2,3},{3,2},{4,5},{5,4},{6,7},{7,6},{8,9},{9,8},{10,11... | collective-permute-start | bytes 731144 | tf_op jit(solution)/shard_map/ppermute | solution.py:331
  62.7 6.6 %copy-start.7 = (bf16[136,896]{1,0:T(8,128)(2,1)}, bf16[136,896]{1,0:T(8,128)(2,1)S(1)}, u32[]{:S(2)}) copy-start(bf16[136,896]{1,0:T(8,128)(2,1)S(1)} %collective-permute-done.12.refs_7_) | copy-start | bytes 731140

commit v6 on v4

--- a/solution.py
+++ b/solution.py
@@ -193,7 +193,7 @@
 
     x_copies = []
     for n in range(len(x_hbm)):
-        to = x_refs.at[n // 2, (n % 2) * rows : (n % 2 + 1) * rows, :]
+        to = x_refs.at[n * rows : (n + 1) * rows, :]
         x_copies.append(pltpu.make_async_copy(x_hbm[n].at[:rows, :], to, sems.at[n]))
     for copy in x_copies:
         copy.start()
@@ -207,7 +207,6 @@
 
     lax.fori_loop(0, peers, add_peer, 0)
     low = lax.broadcasted_iota(jnp.int32, (cols, R), 1) < HR
-    total = None
     for turn in range(inner):
         for far in range(2):
             n = 2 * turn + far
@@ -220,12 +219,11 @@
                     odd = acc_ref[base + b + 1]
                     even = even + pltpu.roll(even, HR, 1)
                     odd = odd + pltpu.roll(odd, HR, 1)
-                    lo = side * rows + b * HR
-                    enc_ref[n, :, lo : lo + 2 * HR] = jnp.where(low, even, odd).astype(BF16)
-            x_copies[2 * n].wait()
-            x_copies[2 * n + 1].wait()
-            part = _dot(enc_ref[n], x_refs[n])
-            total = part if total is None else total + part
+                    lo = (2 * n + side) * rows + b * HR
+                    enc_ref[:, lo : lo + 2 * HR] = jnp.where(low, even, odd).astype(BF16)
+    for copy in x_copies:
+        copy.wait()
+    total = _dot(enc_ref[...], x_refs[...])
     scale = (blocks * R) ** (-0.5)
     out_ref[...] = (total * scale).T
 
@@ -237,7 +235,6 @@
     smem = pl.BlockSpec(memory_space=pltpu.SMEM)
     vmem = pl.BlockSpec(memory_space=pltpu.VMEM)
     xs = [pltpu.with_memory_space_constraint(x, pltpu.HBM) for x in xs]
-    pairs = len(xs) // 2
     return pl.pallas_call(
         functools.partial(_weight_kernel, count, spans, first),
         in_specs=[smem] * 3 + [vmem] * 2 + [pl.BlockSpec(memory_space=pl.ANY)] * len(xs),
@@ -245,8 +242,8 @@
         out_shape=jax.ShapeDtypeStruct((DE, cols), F32),
         scratch_shapes=[
             pltpu.VMEM((blocks, cols, R), F32),
-            pltpu.VMEM((pairs, cols, owned * HR), BF16),
-            pltpu.VMEM((pairs, owned * HR, DE), BF16),
+            pltpu.VMEM((cols, blocks * HR), BF16),
+            pltpu.VMEM((blocks * HR, DE), BF16),
             pltpu.SemaphoreType.DMA((len(xs),)),
         ],
         compiler_params=pltpu.CompilerParams(vmem_limit_bytes=32 << 20),

time: 92.7 us -> 92.6 us (level)
  no operation moved by 1% of the time
where the time goes in v6:
time: 92.6 us; the launch traced here: 92.2 us
  Pallas kernels  32 us (35%)
  starting transfers between devices  22.5 us (24%)
  blocking collectives  18 us (19%)
  waiting for transfers between devices  15.1 us (16%)
  other arithmetic  2.2 us (2%)
  local copies, waits for them, and re-layouts  1.57 us (2%)
    pallas_call x2, Pallas kernels, _span_call(): pl.pallas_call(functools.partial(_span_kernel, first, spans), grid_spec=p...  25.4 us
    all_to_all x1, blocking collectives, per_device(): lax.all_to_all(weight.reshape(2 * peers, rows, cols), ('dp', 'section'),...  18 us
    all_to_all x2, starting transfers between devices, per_device(): gots.append(lax.all_to_all(ref_grad, 'dp', 0, 0, tiled=True))  9.56 us
    all_to_all x2, waiting for transfers between devices, per_device(): gots.append(lax.all_to_all(ref_grad, 'dp', 0, 0, tiled=True))  9.47 us
    ppermute x6, starting transfers between devices, spread(): lax.ppermute(pack, 'dp', [(i, i ^ m) for i in range(peers)])  7.87 us
    ppermute x6, waiting for transfers between devices, spread(): lax.ppermute(pack, 'dp', [(i, i ^ m) for i in range(peers)])  4.43 us
    pallas_call x1, Pallas kernels, _weight_call(): pl.pallas_call(functools.partial(_weight_kernel, count, spans, first), in...  3.91 us
    ppermute x1, starting transfers between devices, per_device(): mirror = lax.ppermute(away, 'dp', [(i, i ^ inner) for i in range(peers)])  2.97 us
  transfers between devices with their start and end apart: 19, of which 6 were waited for; matrix products, arithmetic and copies ran while one was open for 2% of the time, Pallas kernels for 17%

profile of v6, /device:TPU:0, one launch (start us, length us, event | category | flops | bytes accessed | tf_op | source)
XLA Modules:
  0.0 92.2 jit_solution(4449222925330557988)
XLA Ops:
  0.6 0.0 copy-start.9
  0.6 0.0 copy-start.10
  0.7 12.7 %shard_map.104 = (bf16[384,1024]{1,0:T(8,128)(2,1)}, bf16[2,448,384]{2,1,0:T(8,128)(2,1)S(1)}, bf16[2,448,384]{2,1,0:T(8,128)(2,1)S(1)}) custom-call(s32[1]{0:T(128)} %bitcast.sec_ref, bf16[384,1024]{1,0:T(8,128)(2,1)} %q_ref.3, bf16[384,1024]{1,0:T(8,128)(2,1)} %g_ref.3, f32[8,384]{1,0:T(8,128)} %l_ref.3, bf16[6,256,896]{2,1,0:T(8,128)(2,1)} %n_ref.3, ...), custom_call_target="tpu_custom_call" | custom-call | flops 6140461056 | bytes 6670016 | tf_op jit(solution)/shard_map/pallas_call | solution.py:101
  13.4 0.5 collective-permute-start
  13.9 0.0 copy-done.9
  14.0 0.0 copy-done.10
  14.0 0.0 copy-start.1
  14.0 2.7 %collective-permute-start.2 = (bf16[136,896]{1,0:T(8,128)(2,1)S(1)}, bf16[136,896]{1,0:T(8,128)(2,1)S(1)}, u32[]{:S(2)}, u32[]{:S(2)}) collective-permute-start(bf16[136,896]{1,0:T(8,128)(2,1)S(1)} %get-tuple-element.48.refs_0_), channel_id=1, source_target_pairs={{0,2},{2,0},{4,6},{6,4},{8,10},{10,8},{12,14},{14,12},{1,3},{3,1},... | collective-permute-start | bytes 731144 | tf_op jit(solution)/shard_map/ppermute | solution.py:308
  16.7 1.6 %collective-permute-start.3 = (bf16[136,896]{1,0:T(8,128)(2,1)S(1)}, bf16[136,896]{1,0:T(8,128)(2,1)}, u32[]{:S(2)}, u32[]{:S(2)}) collective-permute-start(bf16[136,896]{1,0:T(8,128)(2,1)S(1)} %get-tuple-element.48.refs_0_), channel_id=1, source_target_pairs={{0,4},{2,6},{4,0},{6,2},{8,12},{10,14},{12,8},{14,10},{1,5},{3,7},... | collective-permute-start | bytes 731144 | tf_op jit(solution)/shard_map/ppermute | solution.py:308
  18.3 0.0 collective-permute-start.4
  18.3 3.0 %collective-permute-start.1 = (bf16[136,896]{1,0:T(8,128)(2,1)S(1)}, bf16[136,896]{1,0:T(8,128)(2,1)S(1)}, u32[]{:S(2)}, u32[]{:S(2)}) collective-permute-start(bf16[136,896]{1,0:T(8,128)(2,1)S(1)} %get-tuple-element.59), channel_id=1, source_target_pairs={{0,8},{2,10},{4,12},{6,14},{8,0},{10,2},{12,4},{14,6},{1,9},{3,11}... | collective-permute-start | bytes 731144 | tf_op jit(solution)/shard_map/ppermute | solution.py:304
  21.2 0.0 collective-permute-done
  21.2 1.0 %add_convert_fusion.1 = bf16[2,448,384]{2,1,0:T(8,128)(2,1)} fusion(bf16[2,448,384]{2,1,0:T(8,128)(2,1)S(1)} %collective-permute-done, bf16[2,448,384]{2,1,0:T(8,128)(2,1)S(1)} %get-tuple-element.30), kind=kLoop, calls=%fused_computation.1 | loop fusion | flops 1376256 | bytes 2064384 | tf_op jit(solution)/shard_map/convert_element_type | solution.py:315
  22.3 0.0 copy-done.1
  22.3 3.8 %all-to-all-start = ((bf16[8,112,384]{2,1,0:T(8,128)(2,1)}), bf16[8,112,384]{2,1,0:T(8,128)(2,1)S(1)}, u32[]{:S(2)}, u32[]{:S(2)}) async-start(bf16[8,112,384]{2,1,0:T(8,128)(2,1)} %bitcast.1), calls=%async_computation | async-start | bytes 1376256 | tf_op jit(solution)/shard_map/all_to_all | solution.py:319
  26.1 12.7 %shard_map.105 = (bf16[384,1024]{1,0:T(8,128)(2,1)}, bf16[2,448,384]{2,1,0:T(8,128)(2,1)S(1)}, bf16[2,448,384]{2,1,0:T(8,128)(2,1)S(1)}) custom-call(s32[1]{0:T(128)} %bitcast.sec_ref, bf16[384,1024]{1,0:T(8,128)(2,1)} %q_ref.3, bf16[384,1024]{1,0:T(8,128)(2,1)} %g_ref.3, f32[8,384]{1,0:T(8,128)} %l_ref.3, ...), custom_call_target="tpu_custom_call", output_to_operand_aliasing={{0}: (7, {})} | custom-call | flops 6140461056 | bytes 6670016 | tf_op jit(solution)/shard_map/pallas_call | solution.py:101
  38.8 0.0 collective-permute-done.1.refs_1_
  38.8 0.0 copy-start.5
  38.8 0.0 collective-permute-done.2.refs_2_.refs_4_
  38.8 0.0 copy-start.3
  38.8 0.0 collective-permute-done.3.refs_4_.refs_8_
  38.8 0.0 collective-permute-done.4.refs_6_.refs_12_
  38.8 0.1 collective-permute-start.8
  38.9 2.1 %collective-permute-start.5 = (bf16[136,896]{1,0:T(8,128)(2,1)S(1)}, bf16[136,896]{1,0:T(8,128)(2,1)}, u32[]{:S(2)}, u32[]{:S(2)}) collective-permute-start(bf16[136,896]{1,0:T(8,128)(2,1)S(1)} %collective-permute-done.1.refs_1_), channel_id=1, source_target_pairs={{0,2},{2,0},{4,6},{6,4},{8,10},{10,8},{12,14},{14,12},{1,3},{3,1},... | collective-permute-start | bytes 731144 | tf_op jit(solution)/shard_map/ppermute | solution.py:308
  41.0 1.5 %collective-permute-start.6 = (bf16[136,896]{1,0:T(8,128)(2,1)S(1)}, bf16[136,896]{1,0:T(8,128)(2,1)}, u32[]{:S(2)}, u32[]{:S(2)}) collective-permute-start(bf16[136,896]{1,0:T(8,128)(2,1)S(1)} %collective-permute-done.1.refs_1_), channel_id=1, source_target_pairs={{0,4},{2,6},{4,0},{6,2},{8,12},{10,14},{12,8},{14,10},{1,5},{3,7},... | collective-permute-start | bytes 731144 | tf_op jit(solution)/shard_map/ppermute | solution.py:308
  42.5 0.1 collective-permute-start.7
  42.5 0.0 collective-permute-done.8
  42.5 4.6 %all-to-all-done.got_ref = bf16[8,112,384]{2,1,0:T(8,128)(2,1)S(1)} async-done(((bf16[8,112,384]{2,1,0:T(8,128)(2,1)}), bf16[8,112,384]{2,1,0:T(8,128)(2,1)S(1)}, u32[]{:S(2)}, u32[]{:S(2)}) %all-to-all-start) | async-done | bytes 688160 | tf_op jit(solution)/shard_map/all_to_all | solution.py:319
  47.1 1.0 %add_convert_fusion = bf16[2,448,384]{2,1,0:T(8,128)(2,1)} fusion(bf16[2,448,384]{2,1,0:T(8,128)(2,1)S(1)} %collective-permute-done.8, bf16[2,448,384]{2,1,0:T(8,128)(2,1)S(1)} %get-tuple-element.43), kind=kLoop, calls=%fused_computation | loop fusion | flops 1376256 | bytes 2064384 | tf_op jit(solution)/shard_map/convert_element_type | solution.py:315
  48.1 0.0 copy-done.3
  48.2 5.8 %all-to-all-start.1 = ((bf16[8,112,384]{2,1,0:T(8,128)(2,1)}), bf16[8,112,384]{2,1,0:T(8,128)(2,1)S(1)}, u32[]{:S(2)}, u32[]{:S(2)}) async-start(bf16[8,112,384]{2,1,0:T(8,128)(2,1)} %bitcast.8), calls=%async_computation.1 | async-start | bytes 1376256 | tf_op jit(solution)/shard_map/all_to_all | solution.py:319
  53.9 0.0 copy-start.4
  53.9 0.0 copy-start
  53.9 0.0 collective-permute-done.5.refs_3_.refs_5_
  53.9 0.0 collective-permute-done.6.refs_5_.refs_9_
  54.0 4.4 %collective-permute-done.7.refs_7_.refs_13_ = bf16[136,896]{1,0:T(8,128)(2,1)} collective-permute-done((bf16[136,896]{1,0:T(8,128)(2,1)S(1)}, bf16[136,896]{1,0:T(8,128)(2,1)}, u32[]{:S(2)}, u32[]{:S(2)}) %collective-permute-start.7) | collective-permute-done | bytes 243744 | tf_op jit(solution)/shard_map/ppermute | solution.py:308
  58.4 0.0 copy-done.5
  58.4 1.3 %shard_map.106.ids_ref = s32[16,128]{1,0:T(8,128)} custom-call(bf16[136,896]{1,0:T(8,128)(2,1)} %copy-done.1, bf16[136,896]{1,0:T(8,128)(2,1)} %copy-done.5, bf16[136,896]{1,0:T(8,128)(2,1)} %copy-done.3, bf16[136,896]{1,0:T(8,128)(2,1)} %collective-permute-done.5.refs_3_.refs_5_, bf16[136,896]{1,0:T(8,128)(2,1)} %collective-permute-done.3.refs_4_.refs_8_, ...), custom_call_target="tpu_custom_call" | custom-call | flops 68719476736 | bytes 1000 | tf_op jit(solution)/shard_map/pallas_call | solution.py:133
  59.7 0.0 copy-done.2
  59.7 0.0 collective-permute-start.9
  59.7 0.5 collective-permute-start.10
  60.2 0.1 collective-permute-start.11
  60.3 0.4 collective-permute-start.12
  60.7 0.1 collective-permute-start.13
  60.8 0.4 collective-permute-done.9.refs_2_
  61.2 0.1 collective-permute-start.14
  61.3 0.4 collective-permute-done.10.refs_3_
  61.8 0.2 collective-permute-start.15
  61.9 0.3 collective-permute-done.11.refs_6_
  62.3 0.1 collective-permute-start.16
  62.4 0.1 copy-done.7
  62.5 0.5 copy-done.8
  62.9 0.1 pad_add_fusion.place_ref
  63.0 1.4 %shard_map.107.sum_ref = f32[32,112,128]{2,1,0:T(8,128)S(1)} custom-call(s32[3]{0:T(128)S(1)} %pad_add_fusion.place_ref, s32[16,128]{1,0:T(8,128)} %shard_map.106.ids_ref, s32[32]{0:T(128)S(1)} %copy-done, bf16[8,112,384]{2,1,0:T(8,128)(2,1)S(1)} %all-to-all-done.got_ref), custom_call_target="tpu_custom_call" | custom-call | flops 1000 | bytes 1000 | tf_op jit(solution)/shard_map/pallas_call | solution.py:173
  64.4 0.0 collective-permute-done.12.refs_7_
  64.4 0.0 collective-permute-done.13.refs_10_
  64.4 0.0 collective-permute-done.14.refs_11_
  64.4 0.0 collective-permute-done.15.refs_14_
  64.4 0.0 collective-permute-done.16.refs_15_
  64.5 4.9 %all-to-all-done.1.got_ref = bf16[8,112,384]{2,1,0:T(8,128)(2,1)S(1)} async-done(((bf16[8,112,384]{2,1,0:T(8,128)(2,1)}), bf16[8,112,384]{2,1,0:T(8,128)(2,1)S(1)}, u32[]{:S(2)}, u32[]{:S(2)}) %all-to-all-start.1) | async-done | bytes 688160 | tf_op jit(solution)/shard_map/all_to_all | solution.py:319
  69.3 3.9 %shard_map.108 = f32[896,112]{1,0:T(8,128)S(1)} custom-call(s32[3]{0:T(128)S(1)} %pad_add_fusion.place_ref, s32[16,128]{1,0:T(8,128)} %shard_map.106.ids_ref, s32[32]{0:T(128)S(1)} %copy-done, bf16[8,112,384]{2,1,0:T(8,128)(2,1)S(1)} %all-to-all-done.1.got_ref, f32[32,112,128]{2,1,0:T(8,128)S(1)} %shard_map.107.sum_ref, bf16[136,896]{1,0:T(8,128)(2,1)} %copy-done.1, ...), custom_call_target="tpu_custom_call" | custom-call | flops 411041792 | bytes 6000000 | tf_op jit(solution)/shard_map/pallas_call | solution.py:238
  73.3 18.0 %all_to_all.15 = f32[16,56,112]{2,1,0:T(8,128)S(1)} all-to-all(f32[16,56,112]{2,1,0:T(8,128)S(1)} %bitcast.19), channel_id=1, replica_groups=mesh['group'=2,'dp'=8,'section'=2] {'dp','section'}, dimensions={0} | all-to-all | bytes 802816 | tf_op jit(solution)/shard_map/all_to_all | solution.py:337
  91.3 0.1 copy.18
  91.4 0.9 reshape.43
  (11 shorter events, 0.1 us)
Async XLA Ops:
  0.6 13.3 %copy-start.9 = (bf16[512,896]{1,0:T(8,128)(2,1)S(1)}, bf16[512,896]{1,0:T(8,128)(2,1)}, u32[]{:S(2)}) copy-start(bf16[512,896]{1,0:T(8,128)(2,1)} %param.17) | copy-start | bytes 2752516
  0.6 13.3 %copy-start.10 = (s32[6,2]{0,1:T(2,128)S(1)}, s32[6,2]{0,1:T(2,128)}, u32[]{:S(2)}) copy-start(s32[6,2]{0,1:T(2,128)} %param.15) | copy-start | bytes 148
  13.4 7.9 %collective-permute-start = (bf16[2,448,384]{2,1,0:T(8,128)(2,1)S(1)}, bf16[2,448,384]{2,1,0:T(8,128)(2,1)S(1)}, u32[]{:S(2)}, u32[]{:S(2)}) collective-permute-start(bf16[2,448,384]{2,1,0:T(8,128)(2,1)S(1)} %get-tuple-element.32), channel_id=1, source_target_pairs={{0,1},{1,0},{2,3},{3,2},{4,5},{5,4},{6,7},{7,6},{8,9},{9,8},{10,11... | collective-permute-start | bytes 2064392 | tf_op jit(solution)/shard_map/ppermute | solution.py:312
  14.0 8.3 %copy-start.1 = (bf16[136,896]{1,0:T(8,128)(2,1)}, bf16[136,896]{1,0:T(8,128)(2,1)S(1)}, u32[]{:S(2)}) copy-start(bf16[136,896]{1,0:T(8,128)(2,1)S(1)} %get-tuple-element.48.refs_0_) | copy-start | bytes 731140
  14.0 24.7 %collective-permute-start.2 = (bf16[136,896]{1,0:T(8,128)(2,1)S(1)}, bf16[136,896]{1,0:T(8,128)(2,1)S(1)}, u32[]{:S(2)}, u32[]{:S(2)}) collective-permute-start(bf16[136,896]{1,0:T(8,128)(2,1)S(1)} %get-tuple-element.48.refs_0_), channel_id=1, source_target_pairs={{0,2},{2,0},{4,6},{6,4},{8,10},{10,8},{12,14},{14,12},{1,3},{3,1},... | collective-permute-start | bytes 731144 | tf_op jit(solution)/shard_map/ppermute | solution.py:308
  16.7 22.1 %collective-permute-start.3 = (bf16[136,896]{1,0:T(8,128)(2,1)S(1)}, bf16[136,896]{1,0:T(8,128)(2,1)}, u32[]{:S(2)}, u32[]{:S(2)}) collective-permute-start(bf16[136,896]{1,0:T(8,128)(2,1)S(1)} %get-tuple-element.48.refs_0_), channel_id=1, source_target_pairs={{0,4},{2,6},{4,0},{6,2},{8,12},{10,14},{12,8},{14,10},{1,5},{3,7},... | collective-permute-start | bytes 731144 | tf_op jit(solution)/shard_map/ppermute | solution.py:308
  18.3 20.5 %collective-permute-start.4 = (bf16[136,896]{1,0:T(8,128)(2,1)S(1)}, bf16[136,896]{1,0:T(8,128)(2,1)}, u32[]{:S(2)}, u32[]{:S(2)}) collective-permute-start(bf16[136,896]{1,0:T(8,128)(2,1)S(1)} %get-tuple-element.48.refs_0_), channel_id=1, source_target_pairs={{0,6},{2,4},{4,2},{6,0},{8,14},{10,12},{12,10},{14,8},{1,7},{3,5},... | collective-permute-start | bytes 731144 | tf_op jit(solution)/shard_map/ppermute | solution.py:308
  18.3 20.5 %collective-permute-start.1 = (bf16[136,896]{1,0:T(8,128)(2,1)S(1)}, bf16[136,896]{1,0:T(8,128)(2,1)S(1)}, u32[]{:S(2)}, u32[]{:S(2)}) collective-permute-start(bf16[136,896]{1,0:T(8,128)(2,1)S(1)} %get-tuple-element.59), channel_id=1, source_target_pairs={{0,8},{2,10},{4,12},{6,14},{8,0},{10,2},{12,4},{14,6},{1,9},{3,11}... | collective-permute-start | bytes 731144 | tf_op jit(solution)/shard_map/ppermute | solution.py:304
  22.3 24.8 %all-to-all-start = ((bf16[8,112,384]{2,1,0:T(8,128)(2,1)}), bf16[8,112,384]{2,1,0:T(8,128)(2,1)S(1)}, u32[]{:S(2)}, u32[]{:S(2)}) async-start(bf16[8,112,384]{2,1,0:T(8,128)(2,1)} %bitcast.1), calls=%async_computation | async-start | bytes 1376256 | tf_op jit(solution)/shard_map/all_to_all | solution.py:319
  38.8 19.6 %copy-start.5 = (bf16[136,896]{1,0:T(8,128)(2,1)}, bf16[136,896]{1,0:T(8,128)(2,1)S(1)}, u32[]{:S(2)}) copy-start(bf16[136,896]{1,0:T(8,128)(2,1)S(1)} %collective-permute-done.1.refs_1_) | copy-start | bytes 731140
  38.8 9.4 %copy-start.3 = (bf16[136,896]{1,0:T(8,128)(2,1)}, bf16[136,896]{1,0:T(8,128)(2,1)S(1)}, u32[]{:S(2)}) copy-start(bf16[136,896]{1,0:T(8,128)(2,1)S(1)} %collective-permute-done.2.refs_2_.refs_4_) | copy-start | bytes 731140
  38.8 3.7 %collective-permute-start.8 = (bf16[2,448,384]{2,1,0:T(8,128)(2,1)S(1)}, bf16[2,448,384]{2,1,0:T(8,128)(2,1)S(1)}, u32[]{:S(2)}, u32[]{:S(2)}) collective-permute-start(bf16[2,448,384]{2,1,0:T(8,128)(2,1)S(1)} %get-tuple-element.45), channel_id=1, source_target_pairs={{0,1},{1,0},{2,3},{3,2},{4,5},{5,4},{6,7},{7,6},{8,9},{9,8},{10,11... | collective-permute-start | bytes 2064392 | tf_op jit(solution)/shard_map/ppermute | solution.py:312
  38.9 15.0 %collective-permute-start.5 = (bf16[136,896]{1,0:T(8,128)(2,1)S(1)}, bf16[136,896]{1,0:T(8,128)(2,1)}, u32[]{:S(2)}, u32[]{:S(2)}) collective-permute-start(bf16[136,896]{1,0:T(8,128)(2,1)S(1)} %collective-permute-done.1.refs_1_), channel_id=1, source_target_pairs={{0,2},{2,0},{4,6},{6,4},{8,10},{10,8},{12,14},{14,12},{1,3},{3,1},... | collective-permute-start | bytes 731144 | tf_op jit(solution)/shard_map/ppermute | solution.py:308
  41.0 13.0 %collective-permute-start.6 = (bf16[136,896]{1,0:T(8,128)(2,1)S(1)}, bf16[136,896]{1,0:T(8,128)(2,1)}, u32[]{:S(2)}, u32[]{:S(2)}) collective-permute-start(bf16[136,896]{1,0:T(8,128)(2,1)S(1)} %collective-permute-done.1.refs_1_), channel_id=1, source_target_pairs={{0,4},{2,6},{4,0},{6,2},{8,12},{10,14},{12,8},{14,10},{1,5},{3,7},... | collective-permute-start | bytes 731144 | tf_op jit(solution)/shard_map/ppermute | solution.py:308
  42.5 15.9 %collective-permute-start.7 = (bf16[136,896]{1,0:T(8,128)(2,1)S(1)}, bf16[136,896]{1,0:T(8,128)(2,1)}, u32[]{:S(2)}, u32[]{:S(2)}) collective-permute-start(bf16[136,896]{1,0:T(8,128)(2,1)S(1)} %collective-permute-done.1.refs_1_), channel_id=1, source_target_pairs={{0,6},{2,4},{4,2},{6,0},{8,14},{10,12},{12,10},{14,8},{1,7},{3,5},... | collective-permute-start | bytes 731144 | tf_op jit(solution)/shard_map/ppermute | solution.py:308
  48.2 21.2 %all-to-all-start.1 = ((bf16[8,112,384]{2,1,0:T(8,128)(2,1)}), bf16[8,112,384]{2,1,0:T(8,128)(2,1)S(1)}, u32[]{:S(2)}, u32[]{:S(2)}) async-start(bf16[8,112,384]{2,1,0:T(8,128)(2,1)} %bitcast.8), calls=%async_computation.1 | async-start | bytes 1376256 | tf_op jit(solution)/shard_map/all_to_all | solution.py:319
  53.9 5.8 %copy-start.2 = (bf16[136,896]{1,0:T(8,128)(2,1)S(1)}, bf16[136,896]{1,0:T(8,128)(2,1)}, u32[]{:S(2)}) copy-start(bf16[136,896]{1,0:T(8,128)(2,1)} %copy-done.1) | copy-start | bytes 731140
  53.9 6.3 %copy-start.4 = (bf16[136,896]{1,0:T(8,128)(2,1)S(1)}, bf16[136,896]{1,0:T(8,128)(2,1)}, u32[]{:S(2)}) copy-start(bf16[136,896]{1,0:T(8,128)(2,1)} %copy-done.3) | copy-start | bytes 731140
  53.9 9.1 %copy-start = (s32[32]{0:T(128)S(1)}, s32[32]{0:T(128)}, u32[]{:S(2)}) copy-start(s32[32]{0:T(128)} %slot_ref.3) | copy-start | bytes 388
  59.7 1.5 %collective-permute-start.9 = (bf16[136,896]{1,0:T(8,128)(2,1)S(1)}, bf16[136,896]{1,0:T(8,128)(2,1)S(1)}, u32[]{:S(2)}, u32[]{:S(2)}) collective-permute-start(bf16[136,896]{1,0:T(8,128)(2,1)S(1)} %copy-done.2), channel_id=1, source_target_pairs={{0,1},{1,0},{2,3},{3,2},{4,5},{5,4},{6,7},{7,6},{8,9},{9,8},{10,11... | collective-permute-start | bytes 731144 | tf_op jit(solution)/shard_map/ppermute | solution.py:328
  59.7 2.1 %collective-permute-start.10 = (bf16[136,896]{1,0:T(8,128)(2,1)}, bf16[136,896]{1,0:T(8,128)(2,1)S(1)}, u32[]{:S(2)}, u32[]{:S(2)}) collective-permute-start(bf16[136,896]{1,0:T(8,128)(2,1)} %copy-done.5), channel_id=1, source_target_pairs={{0,1},{1,0},{2,3},{3,2},{4,5},{5,4},{6,7},{7,6},{8,9},{9,8},{10,11... | collective-permute-start | bytes 731144 | tf_op jit(solution)/shard_map/ppermute | solution.py:328
  60.2 2.0 %collective-permute-start.11 = (bf16[136,896]{1,0:T(8,128)(2,1)S(1)}, bf16[136,896]{1,0:T(8,128)(2,1)S(1)}, u32[]{:S(2)}, u32[]{:S(2)}) collective-permute-start(bf16[136,896]{1,0:T(8,128)(2,1)S(1)} %copy-done.4), channel_id=1, source_target_pairs={{0,1},{1,0},{2,3},{3,2},{4,5},{5,4},{6,7},{7,6},{8,9},{9,8},{10,11... | collective-permute-start | bytes 731144 | tf_op jit(solution)/shard_map/ppermute | solution.py:328
  60.3 4.1 %collective-permute-start.12 = (bf16[136,896]{1,0:T(8,128)(2,1)}, bf16[136,896]{1,0:T(8,128)(2,1)}, u32[]{:S(2)}, u32[]{:S(2)}) collective-permute-start(bf16[136,896]{1,0:T(8,128)(2,1)} %collective-permute-done.5.refs_3_.refs_5_), channel_id=1, source_target_pairs={{0,1},{1,0},{2,3},{3,2},{4,5},{5,4},{6,7},{7,6},{8,9},{9,8},{10,11... | collective-permute-start | bytes 731144 | tf_op jit(solution)/shard_map/ppermute | solution.py:328
  60.7 3.7 %collective-permute-start.13 = (bf16[136,896]{1,0:T(8,128)(2,1)}, bf16[136,896]{1,0:T(8,128)(2,1)}, u32[]{:S(2)}, u32[]{:S(2)}) collective-permute-start(bf16[136,896]{1,0:T(8,128)(2,1)} %collective-permute-done.3.refs_4_.refs_8_), channel_id=1, source_target_pairs={{0,1},{1,0},{2,3},{3,2},{4,5},{5,4},{6,7},{7,6},{8,9},{9,8},{10,11... | collective-permute-start | bytes 731144 | tf_op jit(solution)/shard_map/ppermute | solution.py:328
  61.2 8.1 %copy-start.6 = (bf16[136,896]{1,0:T(8,128)(2,1)}, bf16[136,896]{1,0:T(8,128)(2,1)S(1)}, u32[]{:S(2)}) copy-start(bf16[136,896]{1,0:T(8,128)(2,1)S(1)} %collective-permute-done.9.refs_2_) | copy-start | bytes 731140
  61.2 3.2 %collective-permute-start.14 = (bf16[136,896]{1,0:T(8,128)(2,1)}, bf16[136,896]{1,0:T(8,128)(2,1)}, u32[]{:S(2)}, u32[]{:S(2)}) collective-permute-start(bf16[136,896]{1,0:T(8,128)(2,1)} %collective-permute-done.6.refs_5_.refs_9_), channel_id=1, source_target_pairs={{0,1},{1,0},{2,3},{3,2},{4,5},{5,4},{6,7},{7,6},{8,9},{9,8},{10,11... | collective-permute-start | bytes 731144 | tf_op jit(solution)/shard_map/ppermute | solution.py:328
  61.8 0.7 copy-start.7
  61.8 2.7 %collective-permute-start.15 = (bf16[136,896]{1,0:T(8,128)(2,1)}, bf16[136,896]{1,0:T(8,128)(2,1)}, u32[]{:S(2)}, u32[]{:S(2)}) collective-permute-start(bf16[136,896]{1,0:T(8,128)(2,1)} %collective-permute-done.4.refs_6_.refs_12_), channel_id=1, source_target_pairs={{0,1},{1,0},{2,3},{3,2},{4,5},{5,4},{6,7},{7,6},{8,9},{9,8},{10,11... | collective-permute-start | bytes 731144 | tf_op jit(solution)/shard_map/ppermute | solution.py:328
  62.2 0.7 copy-start.8
  62.3 2.2 %collective-permute-start.16 = (bf16[136,896]{1,0:T(8,128)(2,1)}, bf16[136,896]{1,0:T(8,128)(2,1)}, u32[]{:S(2)}, u32[]{:S(2)}) collective-permute-start(bf16[136,896]{1,0:T(8,128)(2,1)} %collective-permute-done.7.refs_7_.refs_13_), channel_id=1, source_target_pairs={{0,1},{1,0},{2,3},{3,2},{4,5},{5,4},{6,7},{7,6},{8,9},{9,8},{10,11... | collective-permute-start | bytes 731144 | tf_op jit(solution)/shard_map/ppermute | solution.py:328
